TPU v7x, 1024 devices: a whole 8x8x8 slice. The times are simulated.
1024 devices in a mesh: sx: 8 (over z), sy: 16 (over y, core), ev: 8 (over x).
Axes of the slice: x: 8, y: 8, z: 8, core: 2. Of those that a mesh axis runs over, the one named last changes fastest.
Arguments:
- adjoint_state: float32 [8, 9, 64, 128, 128], P('ev', None, 'sx', 'sy'), may hold values from -6 to 6
- forward_state: bfloat16 [8, 3, 9, 64, 128, 128], P('ev', None, None, 'sx', 'sy'), may hold values from -6 to 6
- inv_density: float32 [64, 128, 128], P('sx', 'sy'), may hold values from 0.6 to 1.6
- lame_lambda: float32 [64, 128, 128], P('sx', 'sy'), may hold values from 0.15 to 0.5
- shear_modulus: float32 [64, 128, 128], P('sx', 'sy'), may hold values from 0.1 to 0.4
- station_block: int32 [8, 4096, 1], P('ev', ('sx', 'sy')), may hold values from 0 to 15; in each aligned block of 32 rows (0 to 31, 32 to 63, ..., all dimensions but the last counted through in order) at most 4 rows name the same one
- station_cell: int32 [8, 4096], P('ev', ('sx', 'sy')), may hold values from 0 to 63
- station_trace: float32 [8, 4096, 9], P('ev', ('sx', 'sy')), may hold values from -6 to 6
- source_count: int32 [8, 128], P('ev', ('sx', 'sy')), may hold values from 1 to 32, 3080 in all within a row
Outputs:
- adjoint_final: float32 [8, 9, 64, 128, 128], P('ev', None, 'sx', 'sy')
- kernels: float32 [3, 64, 128, 128], P(None, 'sx', 'sy')
Inputs may be any that keep to these rules, and one draw needn't show every extreme that they name: `station_block`: among the 32 rows of one device no block is named more than 4 times.
All inputs are finite; a program needn't handle non-finite values. No bound on the sum of `source_count` on one device may be relied on, other than what follows from the above.
Results may differ from a plain program's by a relative error of at most 0.0003.
Values sent between devices are 32-bit elements; how exact they have to be, the bound alone decides.
No kernel may reach another device: no remote copies, remote signals or barrier semaphores. Data moves between devices by JAX's collectives and lax.ppermute only.
A program may use at most 32 MiB of HBM per device.

v0:
```python
import jax
import jax.numpy as jnp
from jax import lax
from jax.sharding import PartitionSpec as P

DT = 0.35
stress_faces = ([0], [3, 4], [1], [3, 5])
velocity_faces = ([1, 2], [0], [0, 2], [1])


def extended(block, sides, width):
    for axis, dim in sides:
        count = lax.axis_size(axis)
        forward = [(i, i + 1) for i in range(count - 1)]
        backward = [(target, source) for source, target in forward]
        low = lax.ppermute(
            lax.slice_in_dim(block, block.shape[dim] - width, None, axis=dim), axis, forward
        )
        high = lax.ppermute(lax.slice_in_dim(block, 0, width, axis=dim), axis, backward)
        block = jnp.concatenate([low, block, high], axis=dim)
    return block


def shift_upper(field, axis, plane):
    size = field.shape[axis]
    inner = lax.slice_in_dim(field, 1, size, axis=axis)
    return jnp.concatenate([inner, plane], axis=axis)


def shift_lower(field, axis, plane):
    size = field.shape[axis]
    inner = lax.slice_in_dim(field, 0, size - 1, axis=axis)
    return jnp.concatenate([plane, inner], axis=axis)


def above_diff(field):
    zeros_plane = jnp.zeros(field.shape[:-1] + (1,), jnp.float32)
    return jnp.concatenate([field[..., 1:], zeros_plane], axis=-1) - field


def below_diff(field):
    zeros_plane = jnp.zeros(field.shape[:-1] + (1,), jnp.float32)
    return field - jnp.concatenate([zeros_plane, field[..., :-1]], axis=-1)


def accelerate(stress, planes, inv_density, force):
    high_x, low_x, high_y, low_y = planes
    next_x = shift_upper(stress[:, stress_faces[0]], 2, high_x)
    prev_x = shift_lower(stress[:, stress_faces[1]], 2, low_x)
    next_y = shift_upper(stress[:, stress_faces[2]], 3, high_y)
    prev_y = shift_lower(stress[:, stress_faces[3]], 3, low_y)
    sxx, syy, szz, sxy, sxz, syz = [stress[:, c] for c in range(6)]
    accel_x = next_x[:, 0] - sxx + (sxy - prev_y[:, 0]) + below_diff(sxz)
    accel_y = sxy - prev_x[:, 0] + (next_y[:, 0] - syy) + below_diff(syz)
    accel_z = sxz - prev_x[:, 1] + (syz - prev_y[:, 1]) + above_diff(szz)
    accel = jnp.stack([accel_x, accel_y, accel_z], axis=1)
    accel = accel.at[..., 0].add(force)
    return DT * inv_density * accel


def strain_rates(velocity, planes):
    high_x, low_x, high_y, low_y = planes
    next_x = shift_upper(velocity[:, velocity_faces[0]], 2, high_x)
    prev_x = shift_lower(velocity[:, velocity_faces[1]], 2, low_x)
    next_y = shift_upper(velocity[:, velocity_faces[2]], 3, high_y)
    prev_y = shift_lower(velocity[:, velocity_faces[3]], 3, low_y)
    vel_x, vel_y, vel_z = (velocity[:, 0], velocity[:, 1], velocity[:, 2])
    rate_xx = vel_x - prev_x[:, 0]
    rate_yy = vel_y - prev_y[:, 0]
    rate_zz = below_diff(vel_z)
    rate_xy = 0.5 * (next_y[:, 0] - vel_x + (next_x[:, 0] - vel_y))
    rate_xz = 0.5 * (above_diff(vel_x) + (next_x[:, 1] - vel_z))
    rate_yz = 0.5 * (above_diff(vel_y) + (next_y[:, 1] - vel_z))
    return jnp.stack([rate_xx, rate_yy, rate_zz, rate_xy, rate_xz, rate_yz], axis=1)


def stress_step(stress, rates, lame_lambda, shear_modulus):
    trace = rates[:, 0] + rates[:, 1] + rates[:, 2]
    diagonal = stress[:, :3] + DT * (
        lame_lambda * trace[:, None] + 2.0 * shear_modulus * rates[:, :3]
    )
    offdiag = stress[:, 3:] + DT * 2.0 * shear_modulus * rates[:, 3:]
    return jnp.concatenate([diagonal, offdiag], axis=1)


def kernel_terms(rates, strains):
    trace = rates[:, 0] + rates[:, 1] + rates[:, 2]
    forward_trace = strains[:, 0] + strains[:, 1] + strains[:, 2]
    lambda_term = DT * forward_trace * trace
    shear_term = (
        DT
        * 2.0
        * (
            jnp.sum(strains[:, :3] * rates[:, :3], axis=1)
            + 2.0 * jnp.sum(strains[:, 3:] * rates[:, 3:], axis=1)
        )
    )
    return (lambda_term, shear_term)


def border_planes(stack, faces):
    padded = extended(stack, (("sx", 2), ("sy", 3)), 1)
    return (
        padded[:, faces[0], -1:, 1:-1],
        padded[:, faces[1], :1, 1:-1],
        padded[:, faces[2], 1:-1, -1:],
        padded[:, faces[3], 1:-1, :1],
    )


def pack_rows(position, values, cells, slots):
    send_values = jnp.zeros((slots, values.shape[1]), jnp.float32).at[position].set(values)
    send_cells = jnp.zeros((slots,), jnp.float32).at[position].set(cells.astype(jnp.float32))
    return (send_values, send_cells)


def on_device(
    adjoint_state,
    forward_state,
    inv_density,
    lame_lambda,
    shear_modulus,
    station_block,
    station_cell,
    station_trace,
    source_count,
):
    events, owned = station_cell.shape
    blocks_y = lax.axis_size("sy")
    capacity = max(2, 2 * owned // blocks_y)
    slots = blocks_y * capacity
    width_x, width_y = (adjoint_state.shape[2], adjoint_state.shape[3])
    steps = forward_state.shape[1]
    live = (jnp.arange(owned, dtype=jnp.int32)[None, :] < source_count).astype(jnp.float32)
    traces = station_trace * live[:, :, None]
    targets = station_block[:, :, 0]
    member = (targets[:, :, None] == jnp.arange(blocks_y, dtype=jnp.int32)[None, None, :]).astype(
        jnp.int32
    )
    earlier = jnp.cumsum(member, axis=1) - member
    rank = jnp.sum(earlier * member, axis=2)
    position = targets * capacity + rank
    send_values, send_cells = jax.vmap(lambda pos, vals, cells: pack_rows(pos, vals, cells, slots))(
        position, traces, station_cell
    )
    surface_ids = jnp.arange(width_x * width_y, dtype=jnp.float32)
    zero_k = jnp.zeros((events,) + adjoint_state.shape[2:], jnp.float32)
    rho_kernel, lambda_kernel, shear_kernel = (zero_k, zero_k, zero_k)
    state = adjoint_state
    for step in range(steps):
        step_values = lax.all_to_all(
            send_values[:, :, 3 * step : 3 * step + 3],
            "sy",
            split_axis=1,
            concat_axis=1,
            tiled=True,
        )
        step_cells = lax.all_to_all(send_cells, "sy", split_axis=1, concat_axis=1, tiled=True)
        table = (surface_ids[None, :, None] == step_cells[:, None, :]).astype(jnp.float32)
        dense = jnp.einsum("ecr,erw->ecw", table, step_values, precision=lax.Precision.HIGHEST)
        here = dense.reshape(events, width_x, width_y, step_values.shape[2])
        force = jnp.moveaxis(here, 3, 1)
        stress = state[:, 3:]
        change = accelerate(stress, border_planes(stress, stress_faces), inv_density, force)
        velocity = state[:, :3] + change
        rho_kernel = rho_kernel + jnp.sum(
            forward_state[:, step, :3].astype(jnp.float32) * change, axis=1
        )
        rates = strain_rates(velocity, border_planes(velocity, velocity_faces))
        stress = stress_step(stress, rates, lame_lambda, shear_modulus)
        lambda_term, shear_term = kernel_terms(
            rates, forward_state[:, step, 3:].astype(jnp.float32)
        )
        lambda_kernel = lambda_kernel + lambda_term
        shear_kernel = shear_kernel + shear_term
        state = jnp.concatenate([velocity, stress], axis=1)
    totals = lax.psum(
        (
            jnp.sum(rho_kernel, axis=0),
            jnp.sum(lambda_kernel, axis=0),
            jnp.sum(shear_kernel, axis=0),
        ),
        "ev",
    )
    return (state, jnp.stack(totals, axis=0))


def solution(mesh):
    return jax.shard_map(
        on_device,
        mesh=mesh,
        in_specs=(
            P("ev", None, "sx", "sy", None),
            P("ev", None, None, "sx", "sy", None),
            P("sx", "sy", None),
            P("sx", "sy", None),
            P("sx", "sy", None),
            P("ev", ("sx", "sy"), None),
            P("ev", ("sx", "sy")),
            P("ev", ("sx", "sy"), None),
            P("ev", ("sx", "sy")),
        ),
        out_specs=(P("ev", None, "sx", "sy", None), P(None, "sx", "sy", None)),
        check_vma=False,
    )
```

profile of v0, /device:TPU:16, one launch (start us, length us, event | category | flops | bytes accessed | tf_op | source)
XLA Modules:
  0.0 275.7 jit_solution(12762057219389058203)
XLA Ops:
  7.2 0.8 fusion.171
  8.0 1.3 collective-permute-start.1
  9.3 5.8 %collective-permute-start = (f32[1,6,1,8,128]{4,3,2,1,0:T(8,128)S(1)}, f32[1,6,1,8,128]{4,3,2,1,0:T(8,128)S(1)}, u32[]{:S(2)}, u32[]{:S(2)}) collective-permute-start(f32[1,6,1,8,128]{4,3,2,1,0:T(8,128)S(1)} %get-tuple-element.340), channel_id=1, source_target_pairs={{0,128},{128,256},{256,384},{384,512},{512,640},{640,768},{768,896... | collective-permute-start | bytes 73736 | tf_op jit(solution)/shard_map/ppermute | solution.py:16
  15.1 0.7 fusion.152
  15.9 0.8 select_reduce_fusion
  19.4 14.9 %all-to-all-start = ((f32[1,16,4]{2,0,1:T(1,128)}), f32[1,16,4]{2,0,1:T(1,128)S(1)}, u32[]{:S(2)}, u32[]{:S(2)}) async-start(f32[1,16,4]{2,0,1:T(1,128)} %bitcast.22), calls=%async_computation | async-start | bytes 16384 | tf_op jit(solution)/shard_map/all_to_all | solution.py:158
  34.3 1.0 fusion.172
  37.5 0.7 scatter_custom_fusion.1
  38.2 0.7 fusion.176
  39.0 0.8 copy-done.6
  40.4 2.0 collective-permute-start.3
  42.5 2.3 collective-permute-start.2
  46.1 8.2 %all-to-all-start.1 = ((f32[1,64,3]{2,0,1:T(1,128)}), f32[1,64,3]{2,0,1:T(1,128)S(1)}, u32[]{:S(2)}, u32[]{:S(2)}) async-start(f32[1,64,3]{2,0,1:T(1,128)} %bitcast.27), calls=%async_computation.1 | async-start | bytes 65536 | tf_op jit(solution)/shard_map/all_to_all | solution.py:151
  59.4 1.3 all-to-all-done.1
  60.7 6.0 %all-to-all-start.2 = ((f32[1,64,3]{2,0,1:T(1,128)}), f32[1,64,3]{2,0,1:T(1,128)S(1)}, u32[]{:S(2)}, u32[]{:S(2)}) async-start(f32[1,64,3]{2,0,1:T(1,128)} %bitcast.68), calls=%async_computation.2 | async-start | bytes 65536 | tf_op jit(solution)/shard_map/all_to_all | solution.py:151
  67.4 1.9 collective-permute-start.4
  69.4 1.3 collective-permute-start.5
  70.8 4.2 %collective-permute-done.5 = f32[1,3,1,8,128]{4,3,2,1,0:T(8,128)S(1)} collective-permute-done((f32[1,3,1,8,128]{4,3,2,1,0:T(8,128)S(1)}, f32[1,3,1,8,128]{4,3,2,1,0:T(8,128)S(1)}, u32[]{:S(2)}, u32[]{:S(2)}) %collective-permute-start.5) | collective-permute-done | bytes 12320 | tf_op jit(solution)/shard_map/ppermute | solution.py:19
  75.0 1.9 collective-permute-start.6
  76.9 3.6 %collective-permute-start.7 = (f32[1,3,10,1,128]{4,3,2,1,0:T(1,128)S(1)}, f32[1,3,10,1,128]{4,3,2,1,0:T(1,128)S(1)}, u32[]{:S(2)}, u32[]{:S(2)}) collective-permute-start(f32[1,3,10,1,128]{4,3,2,1,0:T(1,128)S(1)} %get-tuple-element.372), channel_id=1, source_target_pairs={{8,0},{16,8},{24,16},{32,24},{40,32},{48,40},{56,48},{64,56},{72,6... | collective-permute-start | bytes 46088 | tf_op jit(solution)/shard_map/ppermute | solution.py:19
  84.2 0.7 copy-done.2
  85.1 1.3 collective-permute-start.9
  86.4 4.6 %collective-permute-start.8 = (f32[1,6,1,8,128]{4,3,2,1,0:T(8,128)S(1)}, f32[1,6,1,8,128]{4,3,2,1,0:T(8,128)S(1)}, u32[]{:S(2)}, u32[]{:S(2)}) collective-permute-start(f32[1,6,1,8,128]{4,3,2,1,0:T(8,128)S(1)} %get-tuple-element.358), channel_id=1, source_target_pairs={{0,128},{128,256},{256,384},{384,512},{512,640},{640,768},{768,896... | collective-permute-start | bytes 73736 | tf_op jit(solution)/shard_map/ppermute | solution.py:16
  91.0 1.5 collective-permute-done.8
  92.5 2.8 %collective-permute-start.11 = (f32[1,6,10,1,128]{4,3,2,1,0:T(1,128)S(1)}, f32[1,6,10,1,128]{4,3,2,1,0:T(1,128)S(1)}, u32[]{:S(2)}, u32[]{:S(2)}) collective-permute-start(f32[1,6,10,1,128]{4,3,2,1,0:T(1,128)S(1)} %get-tuple-element.351), channel_id=1, source_target_pairs={{8,0},{16,8},{24,16},{32,24},{40,32},{48,40},{56,48},{64,56},{72,6... | collective-permute-start | bytes 92168 | tf_op jit(solution)/shard_map/ppermute | solution.py:19
  95.3 1.9 collective-permute-start.10
  98.5 2.0 collective-permute-done.10
  104.0 4.3 %collective-permute-start.12 = (f32[1,3,1,8,128]{4,3,2,1,0:T(8,128)S(1)}, f32[1,3,1,8,128]{4,3,2,1,0:T(8,128)S(1)}, u32[]{:S(2)}, u32[]{:S(2)}) collective-permute-start(f32[1,3,1,8,128]{4,3,2,1,0:T(8,128)S(1)} %get-tuple-element.399), channel_id=1, source_target_pairs={{0,128},{128,256},{256,384},{384,512},{512,640},{640,768},{768,896... | collective-permute-start | bytes 36872 | tf_op jit(solution)/shard_map/ppermute | solution.py:16
  108.3 1.3 collective-permute-start.13
  109.7 5.4 %collective-permute-done.13 = f32[1,3,1,8,128]{4,3,2,1,0:T(8,128)S(1)} collective-permute-done((f32[1,3,1,8,128]{4,3,2,1,0:T(8,128)S(1)}, f32[1,3,1,8,128]{4,3,2,1,0:T(8,128)S(1)}, u32[]{:S(2)}, u32[]{:S(2)}) %collective-permute-start.13) | collective-permute-done | bytes 12320 | tf_op jit(solution)/shard_map/ppermute | solution.py:19
  115.1 1.9 collective-permute-start.14
  117.0 3.6 %collective-permute-start.15 = (f32[1,3,10,1,128]{4,3,2,1,0:T(1,128)S(1)}, f32[1,3,10,1,128]{4,3,2,1,0:T(1,128)S(1)}, u32[]{:S(2)}, u32[]{:S(2)}) collective-permute-start(f32[1,3,10,1,128]{4,3,2,1,0:T(1,128)S(1)} %get-tuple-element.370), channel_id=1, source_target_pairs={{8,0},{16,8},{24,16},{32,24},{40,32},{48,40},{56,48},{64,56},{72,6... | collective-permute-start | bytes 46088 | tf_op jit(solution)/shard_map/ppermute | solution.py:19
  120.7 12.1 %all-to-all-start.3 = ((f32[1,64,3]{2,0,1:T(1,128)}), f32[1,64,3]{2,0,1:T(1,128)S(1)}, u32[]{:S(2)}, u32[]{:S(2)}) async-start(f32[1,64,3]{2,0,1:T(1,128)} %bitcast.109), calls=%async_computation.3 | async-start | bytes 65536 | tf_op jit(solution)/shard_map/all_to_all | solution.py:151
  135.9 1.3 collective-permute-start.17
  137.2 5.5 %collective-permute-start.16 = (f32[1,6,1,8,128]{4,3,2,1,0:T(8,128)S(1)}, f32[1,6,1,8,128]{4,3,2,1,0:T(8,128)S(1)}, u32[]{:S(2)}, u32[]{:S(2)}) collective-permute-start(f32[1,6,1,8,128]{4,3,2,1,0:T(8,128)S(1)} %get-tuple-element.356), channel_id=1, source_target_pairs={{0,128},{128,256},{256,384},{384,512},{512,640},{640,768},{768,896... | collective-permute-start | bytes 73736 | tf_op jit(solution)/shard_map/ppermute | solution.py:16
  142.7 1.5 collective-permute-done.16
  144.2 1.9 collective-permute-start.19
  146.2 2.4 collective-permute-start.18
  149.8 1.5 collective-permute-done.18
  154.9 5.1 %collective-permute-start.20 = (f32[1,3,1,8,128]{4,3,2,1,0:T(8,128)S(1)}, f32[1,3,1,8,128]{4,3,2,1,0:T(8,128)S(1)}, u32[]{:S(2)}, u32[]{:S(2)}) collective-permute-start(f32[1,3,1,8,128]{4,3,2,1,0:T(8,128)S(1)} %get-tuple-element.386), channel_id=1, source_target_pairs={{0,128},{128,256},{256,384},{384,512},{512,640},{640,768},{768,896... | collective-permute-start | bytes 36872 | tf_op jit(solution)/shard_map/ppermute | solution.py:16
  160.0 1.3 collective-permute-start.21
  161.4 5.4 %collective-permute-done.21 = f32[1,3,1,8,128]{4,3,2,1,0:T(8,128)S(1)} collective-permute-done((f32[1,3,1,8,128]{4,3,2,1,0:T(8,128)S(1)}, f32[1,3,1,8,128]{4,3,2,1,0:T(8,128)S(1)}, u32[]{:S(2)}, u32[]{:S(2)}) %collective-permute-start.21) | collective-permute-done | bytes 12320 | tf_op jit(solution)/shard_map/ppermute | solution.py:19
  166.9 1.9 collective-permute-start.22
  168.8 3.6 %collective-permute-start.23 = (f32[1,3,10,1,128]{4,3,2,1,0:T(1,128)S(1)}, f32[1,3,10,1,128]{4,3,2,1,0:T(1,128)S(1)}, u32[]{:S(2)}, u32[]{:S(2)}) collective-permute-start(f32[1,3,10,1,128]{4,3,2,1,0:T(1,128)S(1)} %get-tuple-element.368), channel_id=1, source_target_pairs={{8,0},{16,8},{24,16},{32,24},{40,32},{48,40},{56,48},{64,56},{72,6... | collective-permute-start | bytes 46088 | tf_op jit(solution)/shard_map/ppermute | solution.py:19
  175.9 0.7 fusion.71
  177.4 0.7 pad_maximum_fusion.3
  178.1 89.4 %all-reduce.21.cloned.1.call-done = (f32[1,8,8,128]{3,2,1,0:T(8,128)}, f32[1,8,8,128]{3,2,1,0:T(8,128)}, f32[1,8,8,128]{3,2,1,0:T(8,128)}) async-done(((f32[1,8,8,128]{3,2,1,0:T(8,128)}, f32[1,8,8,128]{3,2,1,0:T(8,128)}, f32[1,8,8,128]{3,2,1,0:T(8,128)}), (f32[1,8,8,128]{3,2,1,0:T(8,128)}, f32[1,8,8,128]{3,2,1,0:T(8,128)}, f32[1,8,8,128]{3,2,1,0:T(8,128)})) %all-reduce.21.cloned.1.call-update) | async-done | bytes 98320 | tf_op jit(solution)/shard_map/psum | solution.py:177
  267.5 1.4 pad_maximum_fusion.18
  (228 shorter events, 32.4 us)
Async XLA Ops:
  7.2 28.2 %copy-start.1 = (bf16[1,3,9,8,8,128]{5,4,3,2,1,0:T(8,128)(2,1)S(1)}, bf16[1,3,9,8,8,128]{5,4,3,2,1,0:T(8,128)(2,1)}, u32[]{:S(2)}) copy-start(bf16[1,3,9,8,8,128]{5,4,3,2,1,0:T(8,128)(2,1)} %param.64) | copy-start | bytes 1327108
  8.0 32.4 %collective-permute-start.1 = (f32[1,6,1,8,128]{4,3,2,1,0:T(8,128)S(1)}, f32[1,6,1,8,128]{4,3,2,1,0:T(8,128)S(1)}, u32[]{:S(2)}, u32[]{:S(2)}) collective-permute-start(f32[1,6,1,8,128]{4,3,2,1,0:T(8,128)S(1)} %get-tuple-element.341), channel_id=1, source_target_pairs={{128,0},{256,128},{384,256},{512,384},{640,512},{768,640},{896,768... | collective-permute-start | bytes 73736 | tf_op jit(solution)/shard_map/ppermute | solution.py:19
  9.3 31.1 %collective-permute-start = (f32[1,6,1,8,128]{4,3,2,1,0:T(8,128)S(1)}, f32[1,6,1,8,128]{4,3,2,1,0:T(8,128)S(1)}, u32[]{:S(2)}, u32[]{:S(2)}) collective-permute-start(f32[1,6,1,8,128]{4,3,2,1,0:T(8,128)S(1)} %get-tuple-element.340), channel_id=1, source_target_pairs={{0,128},{128,256},{256,384},{384,512},{512,640},{640,768},{768,896... | collective-permute-start | bytes 73736 | tf_op jit(solution)/shard_map/ppermute | solution.py:16
  19.4 26.7 %all-to-all-start = ((f32[1,16,4]{2,0,1:T(1,128)}), f32[1,16,4]{2,0,1:T(1,128)S(1)}, u32[]{:S(2)}, u32[]{:S(2)}) async-start(f32[1,16,4]{2,0,1:T(1,128)} %bitcast.22), calls=%async_computation | async-start | bytes 16384 | tf_op jit(solution)/shard_map/all_to_all | solution.py:158
  34.3 1.1 copy-start
  35.4 0.7 copy-start.14
  36.1 0.7 copy-start.13
  36.7 0.7 copy-start.11
  38.2 0.8 copy-start.7
  39.0 0.8 copy-start.6
  39.7 0.7 copy-start.12
  40.4 15.2 %copy-start.3 = (f32[1,6,1,8,128]{4,3,2,1,0:T(8,128)}, f32[1,6,1,8,128]{4,3,2,1,0:T(8,128)S(1)}, u32[]{:S(2)}) copy-start(f32[1,6,1,8,128]{4,3,2,1,0:T(8,128)S(1)} %collective-permute-done.1) | copy-start | bytes 73732
  40.4 15.1 %collective-permute-start.3 = (f32[1,6,10,1,128]{4,3,2,1,0:T(1,128)S(1)}, f32[1,6,10,1,128]{4,3,2,1,0:T(1,128)S(1)}, u32[]{:S(2)}, u32[]{:S(2)}) collective-permute-start(f32[1,6,10,1,128]{4,3,2,1,0:T(1,128)S(1)} %get-tuple-element.353), channel_id=1, source_target_pairs={{8,0},{16,8},{24,16},{32,24},{40,32},{48,40},{56,48},{64,56},{72,6... | collective-permute-start | bytes 92168 | tf_op jit(solution)/shard_map/ppermute | solution.py:19
  42.5 13.1 %collective-permute-start.2 = (f32[1,6,10,1,128]{4,3,2,1,0:T(1,128)S(1)}, f32[1,6,10,1,128]{4,3,2,1,0:T(1,128)S(1)}, u32[]{:S(2)}, u32[]{:S(2)}) collective-permute-start(f32[1,6,10,1,128]{4,3,2,1,0:T(1,128)S(1)} %get-tuple-element.352), channel_id=1, source_target_pairs={{0,8},{8,16},{16,24},{24,32},{32,40},{40,48},{48,56},{56,64},{64,7... | collective-permute-start | bytes 92168 | tf_op jit(solution)/shard_map/ppermute | solution.py:16
  46.1 14.5 %all-to-all-start.1 = ((f32[1,64,3]{2,0,1:T(1,128)}), f32[1,64,3]{2,0,1:T(1,128)S(1)}, u32[]{:S(2)}, u32[]{:S(2)}) async-start(f32[1,64,3]{2,0,1:T(1,128)} %bitcast.27), calls=%async_computation.1 | async-start | bytes 65536 | tf_op jit(solution)/shard_map/all_to_all | solution.py:151
  55.7 0.7 copy-start.10
  57.0 0.7 copy-start.9
  58.4 0.7 slice-start
  60.7 42.5 %all-to-all-start.2 = ((f32[1,64,3]{2,0,1:T(1,128)}), f32[1,64,3]{2,0,1:T(1,128)S(1)}, u32[]{:S(2)}, u32[]{:S(2)}) async-start(f32[1,64,3]{2,0,1:T(1,128)} %bitcast.68), calls=%async_computation.2 | async-start | bytes 65536 | tf_op jit(solution)/shard_map/all_to_all | solution.py:151
  67.4 3.3 %collective-permute-start.4 = (f32[1,3,1,8,128]{4,3,2,1,0:T(8,128)S(1)}, f32[1,3,1,8,128]{4,3,2,1,0:T(8,128)S(1)}, u32[]{:S(2)}, u32[]{:S(2)}) collective-permute-start(f32[1,3,1,8,128]{4,3,2,1,0:T(8,128)S(1)} %get-tuple-element.412), channel_id=1, source_target_pairs={{0,128},{128,256},{256,384},{384,512},{512,640},{640,768},{768,896... | collective-permute-start | bytes 36872 | tf_op jit(solution)/shard_map/ppermute | solution.py:16
  69.4 5.6 %collective-permute-start.5 = (f32[1,3,1,8,128]{4,3,2,1,0:T(8,128)S(1)}, f32[1,3,1,8,128]{4,3,2,1,0:T(8,128)S(1)}, u32[]{:S(2)}, u32[]{:S(2)}) collective-permute-start(f32[1,3,1,8,128]{4,3,2,1,0:T(8,128)S(1)} %get-tuple-element.413), channel_id=1, source_target_pairs={{128,0},{256,128},{384,256},{512,384},{640,512},{768,640},{896,768... | collective-permute-start | bytes 36872 | tf_op jit(solution)/shard_map/ppermute | solution.py:19
  75.0 6.8 %collective-permute-start.6 = (f32[1,3,10,1,128]{4,3,2,1,0:T(1,128)S(1)}, f32[1,3,10,1,128]{4,3,2,1,0:T(1,128)S(1)}, u32[]{:S(2)}, u32[]{:S(2)}) collective-permute-start(f32[1,3,10,1,128]{4,3,2,1,0:T(1,128)S(1)} %get-tuple-element.371), channel_id=1, source_target_pairs={{0,8},{8,16},{16,24},{24,32},{32,40},{40,48},{48,56},{56,64},{64,7... | collective-permute-start | bytes 46088 | tf_op jit(solution)/shard_map/ppermute | solution.py:16
  76.9 5.1 %collective-permute-start.7 = (f32[1,3,10,1,128]{4,3,2,1,0:T(1,128)S(1)}, f32[1,3,10,1,128]{4,3,2,1,0:T(1,128)S(1)}, u32[]{:S(2)}, u32[]{:S(2)}) collective-permute-start(f32[1,3,10,1,128]{4,3,2,1,0:T(1,128)S(1)} %get-tuple-element.372), channel_id=1, source_target_pairs={{8,0},{16,8},{24,16},{32,24},{40,32},{48,40},{56,48},{64,56},{72,6... | collective-permute-start | bytes 46088 | tf_op jit(solution)/shard_map/ppermute | solution.py:19
  82.0 0.7 copy-start.8
  84.1 0.8 copy-start.2
  85.1 5.9 %collective-permute-start.9 = (f32[1,6,1,8,128]{4,3,2,1,0:T(8,128)S(1)}, f32[1,6,1,8,128]{4,3,2,1,0:T(8,128)S(1)}, u32[]{:S(2)}, u32[]{:S(2)}) collective-permute-start(f32[1,6,1,8,128]{4,3,2,1,0:T(8,128)S(1)} %get-tuple-element.359), channel_id=1, source_target_pairs={{128,0},{256,128},{384,256},{512,384},{640,512},{768,640},{896,768... | collective-permute-start | bytes 73736 | tf_op jit(solution)/shard_map/ppermute | solution.py:19
  86.4 6.1 %collective-permute-start.8 = (f32[1,6,1,8,128]{4,3,2,1,0:T(8,128)S(1)}, f32[1,6,1,8,128]{4,3,2,1,0:T(8,128)S(1)}, u32[]{:S(2)}, u32[]{:S(2)}) collective-permute-start(f32[1,6,1,8,128]{4,3,2,1,0:T(8,128)S(1)} %get-tuple-element.358), channel_id=1, source_target_pairs={{0,128},{128,256},{256,384},{384,512},{512,640},{640,768},{768,896... | collective-permute-start | bytes 73736 | tf_op jit(solution)/shard_map/ppermute | solution.py:16
  91.0 9.5 %copy-start.4 = (f32[1,6,1,8,128]{4,3,2,1,0:T(8,128)}, f32[1,6,1,8,128]{4,3,2,1,0:T(8,128)S(1)}, u32[]{:S(2)}) copy-start(f32[1,6,1,8,128]{4,3,2,1,0:T(8,128)S(1)} %collective-permute-done.9) | copy-start | bytes 73732
  92.5 6.0 %collective-permute-start.11 = (f32[1,6,10,1,128]{4,3,2,1,0:T(1,128)S(1)}, f32[1,6,10,1,128]{4,3,2,1,0:T(1,128)S(1)}, u32[]{:S(2)}, u32[]{:S(2)}) collective-permute-start(f32[1,6,10,1,128]{4,3,2,1,0:T(1,128)S(1)} %get-tuple-element.351), channel_id=1, source_target_pairs={{8,0},{16,8},{24,16},{32,24},{40,32},{48,40},{56,48},{64,56},{72,6... | collective-permute-start | bytes 92168 | tf_op jit(solution)/shard_map/ppermute | solution.py:19
  95.3 5.2 %collective-permute-start.10 = (f32[1,6,10,1,128]{4,3,2,1,0:T(1,128)S(1)}, f32[1,6,10,1,128]{4,3,2,1,0:T(1,128)S(1)}, u32[]{:S(2)}, u32[]{:S(2)}) collective-permute-start(f32[1,6,10,1,128]{4,3,2,1,0:T(1,128)S(1)} %get-tuple-element.350), channel_id=1, source_target_pairs={{0,8},{8,16},{16,24},{24,32},{32,40},{40,48},{48,56},{56,64},{64,7... | collective-permute-start | bytes 92168 | tf_op jit(solution)/shard_map/ppermute | solution.py:16
  102.1 0.7 slice-start.1
  104.0 5.7 %collective-permute-start.12 = (f32[1,3,1,8,128]{4,3,2,1,0:T(8,128)S(1)}, f32[1,3,1,8,128]{4,3,2,1,0:T(8,128)S(1)}, u32[]{:S(2)}, u32[]{:S(2)}) collective-permute-start(f32[1,3,1,8,128]{4,3,2,1,0:T(8,128)S(1)} %get-tuple-element.399), channel_id=1, source_target_pairs={{0,128},{128,256},{256,384},{384,512},{512,640},{640,768},{768,896... | collective-permute-start | bytes 36872 | tf_op jit(solution)/shard_map/ppermute | solution.py:16
  108.3 6.8 %collective-permute-start.13 = (f32[1,3,1,8,128]{4,3,2,1,0:T(8,128)S(1)}, f32[1,3,1,8,128]{4,3,2,1,0:T(8,128)S(1)}, u32[]{:S(2)}, u32[]{:S(2)}) collective-permute-start(f32[1,3,1,8,128]{4,3,2,1,0:T(8,128)S(1)} %get-tuple-element.400), channel_id=1, source_target_pairs={{128,0},{256,128},{384,256},{512,384},{640,512},{768,640},{896,768... | collective-permute-start | bytes 36872 | tf_op jit(solution)/shard_map/ppermute | solution.py:19
  115.1 18.9 %collective-permute-start.14 = (f32[1,3,10,1,128]{4,3,2,1,0:T(1,128)S(1)}, f32[1,3,10,1,128]{4,3,2,1,0:T(1,128)S(1)}, u32[]{:S(2)}, u32[]{:S(2)}) collective-permute-start(f32[1,3,10,1,128]{4,3,2,1,0:T(1,128)S(1)} %get-tuple-element.369), channel_id=1, source_target_pairs={{0,8},{8,16},{16,24},{24,32},{32,40},{40,48},{48,56},{56,64},{64,7... | collective-permute-start | bytes 46088 | tf_op jit(solution)/shard_map/ppermute | solution.py:16
  117.0 17.0 %collective-permute-start.15 = (f32[1,3,10,1,128]{4,3,2,1,0:T(1,128)S(1)}, f32[1,3,10,1,128]{4,3,2,1,0:T(1,128)S(1)}, u32[]{:S(2)}, u32[]{:S(2)}) collective-permute-start(f32[1,3,10,1,128]{4,3,2,1,0:T(1,128)S(1)} %get-tuple-element.370), channel_id=1, source_target_pairs={{8,0},{16,8},{24,16},{32,24},{40,32},{48,40},{56,48},{64,56},{72,6... | collective-permute-start | bytes 46088 | tf_op jit(solution)/shard_map/ppermute | solution.py:19
  120.7 33.3 %all-to-all-start.3 = ((f32[1,64,3]{2,0,1:T(1,128)}), f32[1,64,3]{2,0,1:T(1,128)S(1)}, u32[]{:S(2)}, u32[]{:S(2)}) async-start(f32[1,64,3]{2,0,1:T(1,128)} %bitcast.109), calls=%async_computation.3 | async-start | bytes 65536 | tf_op jit(solution)/shard_map/all_to_all | solution.py:151
  132.8 134.7 %all-reduce.21.cloned.1.call-start = ((), (), s32[]{:S(2)}) async-start(), calls=%async_computation.4 | async-start | bytes 196608 | tf_op jit(solution)/shard_map/psum | solution.py:177
  135.9 6.8 %collective-permute-start.17 = (f32[1,6,1,8,128]{4,3,2,1,0:T(8,128)S(1)}, f32[1,6,1,8,128]{4,3,2,1,0:T(8,128)S(1)}, u32[]{:S(2)}, u32[]{:S(2)}) collective-permute-start(f32[1,6,1,8,128]{4,3,2,1,0:T(8,128)S(1)} %get-tuple-element.357), channel_id=1, source_target_pairs={{128,0},{256,128},{384,256},{512,384},{640,512},{768,640},{896,768... | collective-permute-start | bytes 73736 | tf_op jit(solution)/shard_map/ppermute | solution.py:19
  137.2 7.0 %collective-permute-start.16 = (f32[1,6,1,8,128]{4,3,2,1,0:T(8,128)S(1)}, f32[1,6,1,8,128]{4,3,2,1,0:T(8,128)S(1)}, u32[]{:S(2)}, u32[]{:S(2)}) collective-permute-start(f32[1,6,1,8,128]{4,3,2,1,0:T(8,128)S(1)} %get-tuple-element.356), channel_id=1, source_target_pairs={{0,128},{128,256},{256,384},{384,512},{512,640},{640,768},{768,896... | collective-permute-start | bytes 73736 | tf_op jit(solution)/shard_map/ppermute | solution.py:16
  142.7 8.7 %copy-start.5 = (f32[1,6,1,8,128]{4,3,2,1,0:T(8,128)}, f32[1,6,1,8,128]{4,3,2,1,0:T(8,128)S(1)}, u32[]{:S(2)}) copy-start(f32[1,6,1,8,128]{4,3,2,1,0:T(8,128)S(1)} %collective-permute-done.17) | copy-start | bytes 73732
  144.2 5.6 %collective-permute-start.19 = (f32[1,6,10,1,128]{4,3,2,1,0:T(1,128)S(1)}, f32[1,6,10,1,128]{4,3,2,1,0:T(1,128)S(1)}, u32[]{:S(2)}, u32[]{:S(2)}) collective-permute-start(f32[1,6,10,1,128]{4,3,2,1,0:T(1,128)S(1)} %get-tuple-element.349), channel_id=1, source_target_pairs={{8,0},{16,8},{24,16},{32,24},{40,32},{48,40},{56,48},{64,56},{72,6... | collective-permute-start | bytes 92168 | tf_op jit(solution)/shard_map/ppermute | solution.py:19
  146.2 5.2 %collective-permute-start.18 = (f32[1,6,10,1,128]{4,3,2,1,0:T(1,128)S(1)}, f32[1,6,10,1,128]{4,3,2,1,0:T(1,128)S(1)}, u32[]{:S(2)}, u32[]{:S(2)}) collective-permute-start(f32[1,6,10,1,128]{4,3,2,1,0:T(1,128)S(1)} %get-tuple-element.348), channel_id=1, source_target_pairs={{0,8},{8,16},{16,24},{24,32},{32,40},{40,48},{48,56},{56,64},{64,7... | collective-permute-start | bytes 92168 | tf_op jit(solution)/shard_map/ppermute | solution.py:16
  153.0 0.7 slice-start.2
  154.9 6.5 %collective-permute-start.20 = (f32[1,3,1,8,128]{4,3,2,1,0:T(8,128)S(1)}, f32[1,3,1,8,128]{4,3,2,1,0:T(8,128)S(1)}, u32[]{:S(2)}, u32[]{:S(2)}) collective-permute-start(f32[1,3,1,8,128]{4,3,2,1,0:T(8,128)S(1)} %get-tuple-element.386), channel_id=1, source_target_pairs={{0,128},{128,256},{256,384},{384,512},{512,640},{640,768},{768,896... | collective-permute-start | bytes 36872 | tf_op jit(solution)/shard_map/ppermute | solution.py:16
  160.0 6.8 %collective-permute-start.21 = (f32[1,3,1,8,128]{4,3,2,1,0:T(8,128)S(1)}, f32[1,3,1,8,128]{4,3,2,1,0:T(8,128)S(1)}, u32[]{:S(2)}, u32[]{:S(2)}) collective-permute-start(f32[1,3,1,8,128]{4,3,2,1,0:T(8,128)S(1)} %get-tuple-element.387), channel_id=1, source_target_pairs={{128,0},{256,128},{384,256},{512,384},{640,512},{768,640},{896,768... | collective-permute-start | bytes 36872 | tf_op jit(solution)/shard_map/ppermute | solution.py:19
  166.9 7.4 %collective-permute-start.22 = (f32[1,3,10,1,128]{4,3,2,1,0:T(1,128)S(1)}, f32[1,3,10,1,128]{4,3,2,1,0:T(1,128)S(1)}, u32[]{:S(2)}, u32[]{:S(2)}) collective-permute-start(f32[1,3,10,1,128]{4,3,2,1,0:T(1,128)S(1)} %get-tuple-element.367), channel_id=1, source_target_pairs={{0,8},{8,16},{16,24},{24,32},{32,40},{40,48},{48,56},{56,64},{64,7... | collective-permute-start | bytes 46088 | tf_op jit(solution)/shard_map/ppermute | solution.py:16
  168.8 5.5 %collective-permute-start.23 = (f32[1,3,10,1,128]{4,3,2,1,0:T(1,128)S(1)}, f32[1,3,10,1,128]{4,3,2,1,0:T(1,128)S(1)}, u32[]{:S(2)}, u32[]{:S(2)}) collective-permute-start(f32[1,3,10,1,128]{4,3,2,1,0:T(1,128)S(1)} %get-tuple-element.368), channel_id=1, source_target_pairs={{8,0},{16,8},{24,16},{32,24},{40,32},{48,40},{56,48},{64,56},{72,6... | collective-permute-start | bytes 46088 | tf_op jit(solution)/shard_map/ppermute | solution.py:19
Sparse Core Ops, SparseCore 0:
  177.5 89.9 all-reduce.20
where the time goes:
time: 277 us; the launch traced here: 276 us
  waiting for transfers between devices  113 us (41%)
  starting transfers between devices  106 us (38%)
  local copies, waits for them, and re-layouts  30 us (11%)
  between operations  16 us (6%)
  other arithmetic  9.74 us (4%)
    psum x1, waiting for transfers between devices, on_device(): lax.psum((jnp.sum(rho_kernel, axis=0), jnp.sum(lambda_kernel, axis=0), jn...  89.4 us
    ppermute x12, starting transfers between devices, extended(): lax.ppermute(lax.slice_in_dim(block, block.shape[dim] - width, None, axis...  39.6 us
    all_to_all x3, starting transfers between devices, on_device(): lax.all_to_all(send_values[:, :, 3 * step:3 * step + 3], 'sy', split_axis...  26.3 us
    ppermute x12, starting transfers between devices, extended(): lax.ppermute(lax.slice_in_dim(block, 0, width, axis=dim), axis, backward)  25.4 us
    ppermute x12, waiting for transfers between devices, extended(): lax.ppermute(lax.slice_in_dim(block, 0, width, axis=dim), axis, backward)  15.3 us
    all_to_all x1, starting transfers between devices, on_device(): lax.all_to_all(send_cells, 'sy', split_axis=1, concat_axis=1, tiled=True)  14.9 us
    ppermute x12, waiting for transfers between devices, extended(): lax.ppermute(lax.slice_in_dim(block, block.shape[dim] - width, None, axis...  6.75 us
    unnamed x33, local copies, waits for them, and re-layouts  5.94 us
  transfers between devices with their start and end apart: 29, of which 13 were waited for; matrix products, arithmetic and copies ran while one was open for 9% of the time, Pallas kernels for 0%

commit v1 on v0

v1 whole, which is shorter than its diff:
```python
import functools

import jax
import jax.numpy as jnp
from jax import lax
from jax.experimental import pallas as pl
from jax.experimental.pallas import tpu as pltpu
from jax.sharding import PartitionSpec as P

DT = 0.35
W = 3
B = 8
XE = B + 2 * W
XS = XE + 2
YR = 16
FIELDS = 12
DEAD = -1.0e6
MIB = 1 << 20
VMEM = pl.BlockSpec(memory_space=pltpu.VMEM)
SMEM = pl.BlockSpec(memory_space=pltpu.SMEM)


def x_faces_kernel(
    ny, count_ref, adj_ref, rho_ref, lam_ref, mu_ref, block_ref, cell_ref, trace_ref, low_ref, high_ref
):
    for out, first in ((low_ref, 0), (high_ref, B - W)):
        out[0:9] = adj_ref[:, first : first + W]
        out[9] = rho_ref[first : first + W]
        out[10] = lam_ref[first : first + W]
        out[11] = mu_ref[first : first + W]
    rows = trace_ref.shape[0]
    wide = jnp.concatenate(
        [trace_ref[...], block_ref[...].astype(jnp.float32), jnp.zeros((rows, 118), jnp.float32)], axis=1
    )
    turned = wide.T
    cell = cell_ref[...].astype(jnp.float32)
    cell_x = jnp.floor(cell * (1.0 / B))
    key = cell_x * ny + turned[9:10] * B + (cell - B * cell_x)
    live = lax.broadcasted_iota(jnp.int32, (1, rows), 1) < count_ref[0, 0]
    key = jnp.where(live, key, DEAD)
    values = jnp.where(live, turned[0:9], 0.0)
    pack = jnp.concatenate([key, values, jnp.zeros((6, rows), jnp.float32)], axis=0)
    pack = jnp.concatenate([pack, jnp.zeros((16, 128 - rows), jnp.float32)], axis=1)
    for out in (low_ref, high_ref):
        out[12, 0] = pack[0:8]
        out[12, 1] = pack[8:16]
        out[12, 2] = jnp.zeros((8, 128), jnp.float32)


def y_faces_kernel(
    ny, adj_ref, rho_ref, lam_ref, mu_ref, own_ref, low_ref, high_ref, face_low_ref, face_high_ref, tiles_ref
):
    params = (rho_ref, lam_ref, mu_ref)
    for out, first in ((face_low_ref, 0), (face_high_ref, B - W)):
        for f in range(FIELDS):
            for r in range(W):
                y = first + r
                at = (r * FIELDS + f) * YR
                own = (
                    adj_ref[pl.ds(f * 64 + y, B, stride=8), :]
                    if f < 9
                    else params[f - 9][pl.ds(y, B, stride=8), :]
                )
                out[pl.ds(at, W), :] = low_ref[pl.ds(f * 24 + y, W, stride=8), :]
                out[pl.ds(at + W, B), :] = own
                out[pl.ds(at + W + B, W), :] = high_ref[pl.ds(f * 24 + y, W, stride=8), :]
                out[pl.ds(at + XE, YR - XE), :] = jnp.zeros((YR - XE, 128), jnp.float32)
    row = lax.broadcasted_iota(jnp.int32, (8, 128), 0)
    lane = lax.broadcasted_iota(jnp.int32, (8, 128), 1)
    tile = jnp.zeros((8, 128), jnp.float32)
    for s, (ref, shift) in enumerate(((own_ref, W), (low_ref, W - B), (high_ref, W + B))):
        head = ref[pl.ds(12 * 24, 8), :]
        head = jnp.where(row == 0, head + float(shift * ny), head)
        tail = ref[pl.ds(12 * 24 + 8, 8), :]
        head = pltpu.roll(head, 32 * s, 1) if s else head
        tail = pltpu.roll(pltpu.roll(tail, 96, 1), 2 * s, 0) if s else pltpu.roll(tail, 96, 1)
        tile = jnp.where(lane // 32 == s, head, tile)
        tile = jnp.where((lane // 32 == 3) & (row // 2 == s), tail, tile)
    for d in range(tiles_ref.shape[0]):
        tiles_ref[d] = tile


def steps_kernel(
    ny,
    steps,
    place_ref,
    adj_ref,
    rho_ref,
    lam_ref,
    mu_ref,
    forward_ref,
    low_ref,
    high_ref,
    y_low_ref,
    y_high_ref,
    tiles_ref,
    state_ref,
    kernels_ref,
    ext,
    force,
    change_ref,
    rate_ref,
):
    params = (rho_ref, lam_ref, mu_ref)
    plane = XS * YR
    zero8 = jnp.zeros((8, 128), jnp.float32)
    for f in range(FIELDS):
        for e in range(XS):
            at = f * plane + e * YR
            if e == 0 or e == XS - 1:
                ext[pl.ds(at, 8), :] = zero8
            elif e <= W:
                ext[pl.ds(at, 8), :] = low_ref[f, e - 1]
            elif e <= W + B:
                ext[pl.ds(at, 8), :] = adj_ref[f, e - 1 - W] if f < 9 else params[f - 9][e - 1 - W]
            else:
                ext[pl.ds(at, 8), :] = high_ref[f, e - 1 - W - B]
            ext[pl.ds(at + 8, 8), :] = zero8
        for r in range(W):
            src = (r * FIELDS + f) * YR
            ext[pl.ds(f * plane + YR + 8 + r, XE, stride=YR), :] = y_high_ref[pl.ds(src, XE), :]
            ext[pl.ds(f * plane + YR + 13 + r, XE, stride=YR), :] = y_low_ref[pl.ds(src, XE), :]
    cells = XE * YR
    at = lax.broadcasted_iota(jnp.int32, (cells, 128), 0)
    local = at % YR
    local = jnp.where(local < 11, local, local - YR)
    y = place_ref[0] * B + local
    ident = jnp.where((y >= 0) & (y < ny), (at // YR) * ny + y, -10000000).astype(jnp.float32)
    lane = lax.broadcasted_iota(jnp.int32, (8, 128), 1)
    sources = tiles_ref.shape[0]
    hot, packed = [], []
    for d in range(sources):
        tile = tiles_ref[d]
        key = jnp.where(lane < 96, tile, DEAD)[0:1]
        hot.append((ident == key).astype(jnp.float32))
        tails = jnp.where(
            lane < 32, pltpu.roll(tile, 32, 1), jnp.where(lane < 64, pltpu.roll(tile, 64, 1), pltpu.roll(tile, 96, 1))
        )
        packed.append(jnp.concatenate([tile, tails], axis=0))
    surface = lax.dot_general(
        jnp.concatenate(hot, axis=1),
        jnp.concatenate(packed, axis=1),
        (((1,), (1,)), ((), ())),
        precision=lax.Precision.HIGHEST,
        preferred_element_type=jnp.float32,
    )
    for s, first, count in ((1, 0, W), (0, W, B), (2, W + B, W)):
        part = surface[first * YR : (first + count) * YR]
        top = lax.broadcasted_iota(jnp.int32, (count * YR, 128), 1) == 0
        for k in range(3 * steps):
            column = 1 + k if k < 7 else 8 + 2 * s + (k - 7)
            force[k, pl.ds(first * YR, count * YR), :] = jnp.where(top, part[:, column : column + 1], 0.0)

    lanes = lax.broadcasted_iota(jnp.int32, (YR, 128), 1)

    def y_up(v):
        return pltpu.roll(v, YR - 1, 0)

    def y_down(v):
        return pltpu.roll(v, 1, 0)

    def z_up(v):
        return jnp.where(lanes == 127, 0.0, pltpu.roll(v, 127, 1))

    def z_down(v):
        return jnp.where(lanes == 0, 0.0, pltpu.roll(v, 1, 1))

    def get(f, e):
        return ext[pl.ds(pl.multiple_of(f * plane + e * YR, YR), YR), :]

    def put(f, e, v):
        ext[pl.ds(pl.multiple_of(f * plane + e * YR, YR), YR), :] = v

    for x in range(B):
        for k in range(3):
            kernels_ref[k, x] = zero8

    for step in range(steps):

        def velocity(i, e):
            sxx, syy, szz, sxy, sxz, syz = [get(3 + f, e) for f in range(6)]
            ax = (get(3, e + 1) - sxx) + (sxy - y_down(sxy)) + (sxz - z_down(sxz))
            ay = (sxy - get(6, e - 1)) + (y_up(syy) - syy) + (syz - z_down(syz))
            az = (sxz - get(7, e - 1)) + (syz - y_down(syz)) + (z_up(szz) - szz)
            scale = DT * get(9, e)
            for c, accel in enumerate((ax, ay, az)):
                pushed = accel + force[3 * step + c, pl.ds(pl.multiple_of((e - 1) * YR, YR), YR), :]
                change = scale * pushed
                put(c, e, get(c, e) + change)
                change_ref[c, e] = change[0:8]

        def stress(i, e):
            vx, vy, vz = [get(f, e) for f in range(3)]
            exx = vx - get(0, e - 1)
            eyy = vy - y_down(vy)
            ezz = vz - z_down(vz)
            exy = 0.5 * ((y_up(vx) - vx) + (get(1, e + 1) - vy))
            exz = 0.5 * ((z_up(vx) - vx) + (get(2, e + 1) - vz))
            eyz = 0.5 * ((z_up(vy) - vy) + (y_up(vz) - vz))
            trace = exx + eyy + ezz
            lam = get(10, e) * trace
            twice = 2.0 * get(11, e)
            for f, rate in enumerate((exx, eyy, ezz, exy, exz, eyz)):
                if f < 3:
                    put(3 + f, e, get(3 + f, e) + DT * (lam + twice * rate))
                else:
                    put(3 + f, e, get(3 + f, e) + DT * twice * rate)
                rate_ref[f, e] = rate[0:8]

        def pair(body, first):
            def run(i, carry):
                e = first + 2 * i
                body(i, e)
                body(i, e + 1)
                return carry

            return run

        lax.fori_loop(0, (XE - 2 * step) // 2, pair(velocity, 1 + step), 0)
        lax.fori_loop(0, (XE - 2 * step - 2) // 2, pair(stress, 2 + step), 0)

        def sensitivities(x, carry):
            e = x + 1 + W
            f = [forward_ref[step, c, x].astype(jnp.float32) for c in range(9)]
            change = [change_ref[c, e] for c in range(3)]
            rate = [rate_ref[c, e] for c in range(6)]
            kernels_ref[0, x] += f[0] * change[0] + f[1] * change[1] + f[2] * change[2]
            trace = rate[0] + rate[1] + rate[2]
            kernels_ref[1, x] += DT * (f[3] + f[4] + f[5]) * trace
            kernels_ref[2, x] += (
                DT
                * 2.0
                * (
                    (f[3] * rate[0] + f[4] * rate[1] + f[5] * rate[2])
                    + 2.0 * (f[6] * rate[3] + f[7] * rate[4] + f[8] * rate[5])
                )
            )
            return carry

        lax.fori_loop(0, B, sensitivities, 0, unroll=2)

    for f in range(9):
        for x in range(B):
            state_ref[f, x] = ext[pl.ds(f * plane + (x + 1 + W) * YR, 8), :]


def sum_kernel(events, parts_ref, out_ref):
    size = parts_ref.shape[0] // events
    total = parts_ref[0:size]
    for s in range(1, events):
        total = total + parts_ref[size * s : size * s + size]
    for s in range(events):
        out_ref[size * s : size * s + size] = total


def f32(*shape):
    return jax.ShapeDtypeStruct(shape, jnp.float32)


def on_device(
    adjoint_state,
    forward_state,
    inv_density,
    lame_lambda,
    shear_modulus,
    station_block,
    station_cell,
    station_trace,
    source_count,
):
    n_sx, n_sy, n_ev = lax.axis_size("sx"), lax.axis_size("sy"), lax.axis_size("ev")
    steps = forward_state.shape[1]
    ny = n_sy * B
    adj = adjoint_state[0]
    up_x = [(i, i + 1) for i in range(n_sx - 1)]
    up_y = [(i, i + 1) for i in range(n_sy - 1)]
    down_x = [(b, a) for a, b in up_x]
    down_y = [(b, a) for a, b in up_y]

    low_face, high_face = pl.pallas_call(
        functools.partial(x_faces_kernel, ny),
        out_shape=[f32(13, W, 8, 128)] * 2,
        in_specs=[SMEM] + [VMEM] * 7,
        out_specs=[VMEM] * 2,
        compiler_params=pltpu.CompilerParams(vmem_limit_bytes=3 * MIB),
        name="x_faces",
    )(
        source_count,
        adj,
        inv_density,
        lame_lambda,
        shear_modulus,
        station_block[0],
        station_cell,
        station_trace[0],
    )
    low = lax.ppermute(high_face, "sx", up_x)
    high = lax.ppermute(low_face, "sx", down_x)

    flat = lambda a: a.reshape(-1, 128)
    y_low_face, y_high_face, tiles = pl.pallas_call(
        functools.partial(y_faces_kernel, ny),
        out_shape=[f32(W * FIELDS * YR, 128)] * 2 + [f32(n_sy, 8, 128)],
        in_specs=[VMEM] * 7,
        out_specs=[VMEM] * 3,
        compiler_params=pltpu.CompilerParams(vmem_limit_bytes=4 * MIB),
        name="y_faces",
    )(
        flat(adj),
        flat(inv_density),
        flat(lame_lambda),
        flat(shear_modulus),
        flat(low_face),
        flat(low),
        flat(high),
    )
    y_low = lax.ppermute(y_high_face, "sy", up_y)
    y_high = lax.ppermute(y_low_face, "sy", down_y)
    tiles = lax.all_to_all(tiles, "sy", split_axis=0, concat_axis=0, tiled=True)

    place = lax.axis_index("sy").astype(jnp.int32).reshape(1)
    state, kernels = pl.pallas_call(
        functools.partial(steps_kernel, ny, steps),
        out_shape=[f32(9, B, 8, 128), f32(3, B, 8, 128)],
        in_specs=[SMEM] + [VMEM] * 10,
        out_specs=[VMEM] * 2,
        scratch_shapes=[
            pltpu.VMEM((FIELDS * XS * YR, 128), jnp.float32),
            pltpu.VMEM((3 * steps, XE * YR, 128), jnp.float32),
            pltpu.VMEM((3, XS, 8, 128), jnp.float32),
            pltpu.VMEM((6, XS, 8, 128), jnp.float32),
        ],
        compiler_params=pltpu.CompilerParams(vmem_limit_bytes=8 * MIB),
        name="steps",
    )(
        place,
        adj,
        inv_density,
        lame_lambda,
        shear_modulus,
        forward_state[0],
        low,
        high,
        y_low,
        y_high,
        tiles,
    )

    parts = lax.all_to_all(kernels.reshape(3 * B, 8, 128), "ev", split_axis=0, concat_axis=0, tiled=True)
    shared = pl.pallas_call(
        functools.partial(sum_kernel, n_ev), out_shape=f32(3 * B, 8, 128), in_specs=[VMEM], out_specs=VMEM, compiler_params=pltpu.CompilerParams(vmem_limit_bytes=1 * MIB),
        name="event_sum"
    )(parts)
    total = lax.all_to_all(shared, "ev", split_axis=0, concat_axis=0, tiled=True)
    return state[None], total.reshape(3, B, 8, 128)


def solution(mesh):
    return jax.shard_map(
        on_device,
        mesh=mesh,
        in_specs=(
            P("ev", None, "sx", "sy", None),
            P("ev", None, None, "sx", "sy", None),
            P("sx", "sy", None),
            P("sx", "sy", None),
            P("sx", "sy", None),
            P("ev", ("sx", "sy"), None),
            P("ev", ("sx", "sy")),
            P("ev", ("sx", "sy"), None),
            P("ev", ("sx", "sy")),
        ),
        out_specs=(P("ev", None, "sx", "sy", None), P(None, "sx", "sy", None)),
        check_vma=False,
    )
```

time: 277 us -> 78.5 us (0.28)
  the two profiles are of different devices: /device:TPU:16 before, /device:TPU:256 now
where the time goes in v1:
time: 78.5 us; the launch traced here: 77.9 us
  blocking collectives  26.6 us (34%)
  starting transfers between devices  21.5 us (27%)
  waiting for transfers between devices  16.1 us (21%)
  Pallas kernels  7.06 us (9%)
  local copies, waits for them, and re-layouts  5.29 us (7%)
  between operations  1.37 us (2%)
    all_to_all x1, blocking collectives, on_device(): lax.all_to_all(kernels.reshape(3 * B, 8, 128), 'ev', split_axis=0, concat...  15.5 us
    all_to_all x1, starting transfers between devices, on_device(): tiles = lax.all_to_all(tiles, 'sy', split_axis=0, concat_axis=0, tiled=True)  11.8 us
    all_to_all x1, blocking collectives, on_device(): lax.all_to_all(shared, 'ev', split_axis=0, concat_axis=0, tiled=True)  11.1 us
    all_to_all x1, waiting for transfers between devices, on_device(): tiles = lax.all_to_all(tiles, 'sy', split_axis=0, concat_axis=0, tiled=True)  7.79 us
    ppermute x1, waiting for transfers between devices, on_device(): high = lax.ppermute(low_face, 'sx', down_x)  6.88 us
    pallas_call x1, Pallas kernels, on_device(): pl.pallas_call(functools.partial(steps_kernel, ny, steps), out_shape=[f32...  6.12 us
    ppermute x1, starting transfers between devices, on_device(): low = lax.ppermute(high_face, 'sx', up_x)  5.18 us
    unnamed x20, local copies, waits for them, and re-layouts  4.56 us
  transfers between devices with their start and end apart: 5, of which 3 were waited for; matrix products, arithmetic and copies ran while one was open for 0% of the time, Pallas kernels for 0%

profile of v1, /device:TPU:256, one launch (start us, length us, event | category | flops | bytes accessed | tf_op | source)
XLA Modules:
  0.0 77.9 jit_solution(15547824518144883015)
XLA Ops:
  0.6 0.0 copy-start.3
  1.3 0.7 copy.12.block_ref
  2.0 0.8 copy.11
  2.8 0.0 copy-start.8
  2.8 0.0 copy-done.3
  2.8 0.7 copy-done.8
  3.5 0.0 copy-start
  3.5 1.0 %copy-done = f32[1,9,8,8,128]{4,3,2,1,0:T(8,128)S(1)} copy-done((f32[1,9,8,8,128]{4,3,2,1,0:T(8,128)S(1)}, f32[1,9,8,8,128]{4,3,2,1,0:T(8,128)}, u32[]{:S(2)}) %copy-start) | copy-done | bytes 294936
  4.4 0.0 copy-start.4
  4.4 0.8 copy-done.4
  5.2 0.0 copy-start.6
  5.2 0.8 copy-done.6
  5.9 0.0 copy-start.1
  5.9 0.0 copy-start.5
  5.9 0.0 copy-start.7
  5.9 0.1 x_faces.1
  6.1 5.2 %collective-permute-start = (f32[13,3,8,128]{3,2,1,0:T(8,128)S(1)}, f32[13,3,8,128]{3,2,1,0:T(8,128)S(1)}, u32[]{:S(2)}, u32[]{:S(2)}) collective-permute-start(f32[13,3,8,128]{3,2,1,0:T(8,128)S(1)} %get-tuple-element.9), channel_id=1, source_target_pairs={{0,128},{128,256},{256,384},{384,512},{512,640},{640,768},{768,896... | collective-permute-start | bytes 479240 | tf_op jit(solution)/shard_map/ppermute | solution.py:297
  11.3 1.9 %collective-permute-start.1 = (f32[13,3,8,128]{3,2,1,0:T(8,128)S(1)}, f32[13,3,8,128]{3,2,1,0:T(8,128)S(1)}, u32[]{:S(2)}, u32[]{:S(2)}) collective-permute-start(f32[13,3,8,128]{3,2,1,0:T(8,128)S(1)} %get-tuple-element.10), channel_id=1, source_target_pairs={{128,0},{256,128},{384,256},{512,384},{640,512},{768,640},{896,768... | collective-permute-start | bytes 479240 | tf_op jit(solution)/shard_map/ppermute | solution.py:298
  13.2 1.4 %collective-permute-done.low_ref = f32[13,3,8,128]{3,2,1,0:T(8,128)S(1)} collective-permute-done((f32[13,3,8,128]{3,2,1,0:T(8,128)S(1)}, f32[13,3,8,128]{3,2,1,0:T(8,128)S(1)}, u32[]{:S(2)}, u32[]{:S(2)}) %collective-permute-start) | collective-permute-done | bytes 159776 | tf_op jit(solution)/shard_map/ppermute | solution.py:297
  14.6 6.9 %collective-permute-done.1.high_ref = f32[13,3,8,128]{3,2,1,0:T(8,128)S(1)} collective-permute-done((f32[13,3,8,128]{3,2,1,0:T(8,128)S(1)}, f32[13,3,8,128]{3,2,1,0:T(8,128)S(1)}, u32[]{:S(2)}, u32[]{:S(2)}) %collective-permute-start.1) | collective-permute-done | bytes 159776 | tf_op jit(solution)/shard_map/ppermute | solution.py:298
  21.5 0.0 copy-done.1
  21.5 0.0 copy-done.5
  21.5 0.0 copy-done.7
  21.5 0.0 copy-start.2
  21.5 0.8 %y_faces.1 = (f32[576,128]{1,0:T(8,128)S(1)}, f32[576,128]{1,0:T(8,128)S(1)}, f32[16,8,128]{2,1,0:T(8,128)}) custom-call(f32[576,128]{1,0:T(8,128)S(1)} %bitcast.16, f32[64,128]{1,0:T(8,128)S(1)} %bitcast.21, f32[64,128]{1,0:T(8,128)S(1)} %bitcast.22, f32[64,128]{1,0:T(8,128)S(1)} %bitcast.23, f32[312,128]{1,0:T(8,128)S(1)} %bitcast.24, ...), custom_call_target="tpu_custom_call" | custom-call | tf_op jit(solution)/shard_map/y_faces/pallas_call | solution.py:301
  22.3 1.3 %collective-permute-start.2 = (f32[576,128]{1,0:T(8,128)S(1)}, f32[576,128]{1,0:T(8,128)S(1)}, u32[]{:S(2)}, u32[]{:S(2)}) collective-permute-start(f32[576,128]{1,0:T(8,128)S(1)} %get-tuple-element.11), channel_id=1, source_target_pairs={{0,8},{8,16},{16,24},{24,32},{32,40},{40,48},{48,56},{56,64},{64,7... | collective-permute-start | bytes 884744 | tf_op jit(solution)/shard_map/ppermute | solution.py:317
  23.6 1.3 %collective-permute-start.3 = (f32[576,128]{1,0:T(8,128)S(1)}, f32[576,128]{1,0:T(8,128)S(1)}, u32[]{:S(2)}, u32[]{:S(2)}) collective-permute-start(f32[576,128]{1,0:T(8,128)S(1)} %get-tuple-element.12), channel_id=1, source_target_pairs={{8,0},{16,8},{24,16},{32,24},{40,32},{48,40},{56,48},{64,56},{72,6... | collective-permute-start | bytes 884744 | tf_op jit(solution)/shard_map/ppermute | solution.py:318
  24.9 11.8 %all-to-all-start = ((f32[16,8,128]{2,1,0:T(8,128)}), f32[16,8,128]{2,1,0:T(8,128)S(1)}, u32[]{:S(2)}, u32[]{:S(2)}) async-start(f32[16,8,128]{2,1,0:T(8,128)} %get-tuple-element.13), calls=%async_computation | async-start | bytes 131072 | tf_op jit(solution)/shard_map/all_to_all | solution.py:319
  36.8 7.8 %all-to-all-done.tiles_ref = f32[16,8,128]{2,1,0:T(8,128)S(1)} async-done(((f32[16,8,128]{2,1,0:T(8,128)}), f32[16,8,128]{2,1,0:T(8,128)S(1)}, u32[]{:S(2)}, u32[]{:S(2)}) %all-to-all-start) | async-done | bytes 65568 | tf_op jit(solution)/shard_map/all_to_all | solution.py:319
  44.5 0.0 collective-permute-done.2.y_low_ref
  44.6 0.0 collective-permute-done.3.y_high_ref
  44.6 0.0 copy-done.2
  44.6 6.1 %steps.1 = (f32[9,8,8,128]{3,2,1,0:T(8,128)}, f32[3,8,8,128]{3,2,1,0:T(8,128)S(1)}) custom-call(s32[1]{0:T(128)} %bitcast.place_ref, f32[9,8,8,128]{3,2,1,0:T(8,128)S(1)} %bitcast.17, f32[8,8,128]{2,1,0:T(8,128)S(1)} %copy-done.3, f32[8,8,128]{2,1,0:T(8,128)S(1)} %copy-done.5, f32[8,8,128]{2,1,0:T(8,128)S(1)} %copy-done.7, ...), custom_call_target="tpu_custom_call" | custom-call | tf_op jit(solution)/shard_map/steps/pallas_call | solution.py:322
  50.7 15.5 %all_to_all.15.parts_ref = f32[24,8,128]{2,1,0:T(8,128)S(1)} all-to-all(f32[24,8,128]{2,1,0:T(8,128)S(1)} %bitcast.25), channel_id=1, replica_groups=mesh['sx'=8,'sy'=16,'ev'=8] {'ev'}, dimensions={0} | all-to-all | bytes 196608 | tf_op jit(solution)/shard_map/all_to_all | solution.py:349
  66.2 11.1 %all_to_all.16 = f32[24,8,128]{2,1,0:T(8,128)S(1)} all-to-all(f32[24,8,128]{2,1,0:T(8,128)S(1)} %event_sum.1), channel_id=1, replica_groups=mesh['sx'=8,'sy'=16,'ev'=8] {'ev'}, dimensions={0} | all-to-all | bytes 196608 | tf_op jit(solution)/shard_map/all_to_all | solution.py:354
  77.3 0.6 copy.15
  (1 shorter events, 0.0 us)
Async XLA Ops:
  0.6 2.2 %copy-start.3 = (f32[8,8,128]{2,1,0:T(8,128)S(1)}, f32[8,8,128]{2,1,0:T(8,128)}, u32[]{:S(2)}) copy-start(f32[8,8,128]{2,1,0:T(8,128)} %rho_ref.3) | copy-start | bytes 98308
  2.8 0.7 copy-start.8
  3.5 1.0 %copy-start = (f32[1,9,8,8,128]{4,3,2,1,0:T(8,128)S(1)}, f32[1,9,8,8,128]{4,3,2,1,0:T(8,128)}, u32[]{:S(2)}) copy-start(f32[1,9,8,8,128]{4,3,2,1,0:T(8,128)} %param.9) | copy-start | bytes 884740
  4.4 0.8 copy-start.4
  5.2 0.8 copy-start.6
  5.9 15.6 %copy-start.1 = (f32[1,9,8,8,128]{4,3,2,1,0:T(8,128)S(1)}, f32[1,9,8,8,128]{4,3,2,1,0:T(8,128)}, u32[]{:S(2)}) copy-start(f32[1,9,8,8,128]{4,3,2,1,0:T(8,128)} %param.9) | copy-start | bytes 884740
  5.9 15.6 %copy-start.5 = (f32[8,8,128]{2,1,0:T(8,128)S(1)}, f32[8,8,128]{2,1,0:T(8,128)}, u32[]{:S(2)}) copy-start(f32[8,8,128]{2,1,0:T(8,128)} %lam_ref.3) | copy-start | bytes 98308
  5.9 15.6 %copy-start.7 = (f32[8,8,128]{2,1,0:T(8,128)S(1)}, f32[8,8,128]{2,1,0:T(8,128)}, u32[]{:S(2)}) copy-start(f32[8,8,128]{2,1,0:T(8,128)} %mu_ref.3) | copy-start | bytes 98308
  6.1 8.5 %collective-permute-start = (f32[13,3,8,128]{3,2,1,0:T(8,128)S(1)}, f32[13,3,8,128]{3,2,1,0:T(8,128)S(1)}, u32[]{:S(2)}, u32[]{:S(2)}) collective-permute-start(f32[13,3,8,128]{3,2,1,0:T(8,128)S(1)} %get-tuple-element.9), channel_id=1, source_target_pairs={{0,128},{128,256},{256,384},{384,512},{512,640},{640,768},{768,896... | collective-permute-start | bytes 479240 | tf_op jit(solution)/shard_map/ppermute | solution.py:297
  11.3 10.2 %collective-permute-start.1 = (f32[13,3,8,128]{3,2,1,0:T(8,128)S(1)}, f32[13,3,8,128]{3,2,1,0:T(8,128)S(1)}, u32[]{:S(2)}, u32[]{:S(2)}) collective-permute-start(f32[13,3,8,128]{3,2,1,0:T(8,128)S(1)} %get-tuple-element.10), channel_id=1, source_target_pairs={{128,0},{256,128},{384,256},{512,384},{640,512},{768,640},{896,768... | collective-permute-start | bytes 479240 | tf_op jit(solution)/shard_map/ppermute | solution.py:298
  21.5 23.0 %copy-start.2 = (bf16[1,3,9,8,8,128]{5,4,3,2,1,0:T(8,128)(2,1)S(1)}, bf16[1,3,9,8,8,128]{5,4,3,2,1,0:T(8,128)(2,1)}, u32[]{:S(2)}) copy-start(bf16[1,3,9,8,8,128]{5,4,3,2,1,0:T(8,128)(2,1)} %param.10) | copy-start | bytes 1327108
  22.3 22.3 %collective-permute-start.2 = (f32[576,128]{1,0:T(8,128)S(1)}, f32[576,128]{1,0:T(8,128)S(1)}, u32[]{:S(2)}, u32[]{:S(2)}) collective-permute-start(f32[576,128]{1,0:T(8,128)S(1)} %get-tuple-element.11), channel_id=1, source_target_pairs={{0,8},{8,16},{16,24},{24,32},{32,40},{40,48},{48,56},{56,64},{64,7... | collective-permute-start | bytes 884744 | tf_op jit(solution)/shard_map/ppermute | solution.py:317
  23.6 21.0 %collective-permute-start.3 = (f32[576,128]{1,0:T(8,128)S(1)}, f32[576,128]{1,0:T(8,128)S(1)}, u32[]{:S(2)}, u32[]{:S(2)}) collective-permute-start(f32[576,128]{1,0:T(8,128)S(1)} %get-tuple-element.12), channel_id=1, source_target_pairs={{8,0},{16,8},{24,16},{32,24},{40,32},{48,40},{56,48},{64,56},{72,6... | collective-permute-start | bytes 884744 | tf_op jit(solution)/shard_map/ppermute | solution.py:318
  24.9 19.6 %all-to-all-start = ((f32[16,8,128]{2,1,0:T(8,128)}), f32[16,8,128]{2,1,0:T(8,128)S(1)}, u32[]{:S(2)}, u32[]{:S(2)}) async-start(f32[16,8,128]{2,1,0:T(8,128)} %get-tuple-element.13), calls=%async_computation | async-start | bytes 131072 | tf_op jit(solution)/shard_map/all_to_all | solution.py:319

commit v2 on v1

v2 whole, which is shorter than its diff:
```python
import functools

import jax
import jax.numpy as jnp
from jax import lax
from jax.experimental import pallas as pl
from jax.experimental.pallas import tpu as pltpu
from jax.sharding import PartitionSpec as P

DT = 0.35
W = 3
B = 8
XE = B + 2 * W
XS = XE + 2
YR = 16
FIELDS = 12
PLANE = XS * YR
DEAD = -1.0e6
MIB = 1 << 20
VMEM = pl.BlockSpec(memory_space=pltpu.VMEM)
SMEM = pl.BlockSpec(memory_space=pltpu.SMEM)
HBM = pl.BlockSpec(memory_space=pltpu.HBM)


def x_faces_kernel(adj_ref, rho_ref, lam_ref, mu_ref, low_ref, high_ref, base_ref, sems):
    copies = []
    for side, (out, first) in enumerate(((low_ref, 0), (high_ref, B - W))):
        pieces = [(adj_ref.at[:, pl.ds(first, W)], out.at[pl.ds(0, 9)])]
        pieces += [(p.at[pl.ds(first, W)], out.at[9 + i]) for i, p in enumerate((rho_ref, lam_ref, mu_ref))]
        for i, (source, target) in enumerate(pieces):
            copies.append(pltpu.make_async_copy(source, target, sems.at[side, i]))
    copies.append(pltpu.make_async_copy(adj_ref, base_ref.at[pl.ds(0, 9)], sems.at[2, 0]))
    for i, p in enumerate((rho_ref, lam_ref, mu_ref)):
        copies.append(pltpu.make_async_copy(p, base_ref.at[9 + i], sems.at[2, 1 + i]))
    for copy in copies:
        copy.start()
    for copy in copies:
        copy.wait()


def stations_kernel(ny, count_ref, block_hbm, cell_hbm, trace_hbm, tiles_ref, block_ref, cell_ref, trace_ref, sems):
    moves = ((block_hbm, block_ref), (cell_hbm, cell_ref), (trace_hbm, trace_ref))
    copies = [pltpu.make_async_copy(source, target, sems.at[i]) for i, (source, target) in enumerate(moves)]
    for copy in copies:
        copy.start()
    for copy in copies:
        copy.wait()
    rows = cell_ref.shape[1]
    cell = cell_ref[...]
    key = ((cell // B) * ny + block_ref[...] * B + cell % B).astype(jnp.float32)
    live = lax.broadcasted_iota(jnp.int32, (1, rows), 1) < count_ref[0, 0]
    parts = [jnp.where(live, key, DEAD)] + [jnp.where(live, trace_ref[k], 0.0) for k in range(9)]
    parts += [jnp.zeros((1, rows), jnp.float32)] * 6
    tile = jnp.concatenate(
        [jnp.concatenate(parts[:8], axis=0), jnp.concatenate(parts[8:], axis=0), jnp.zeros((8, 128 - 2 * rows), jnp.float32)],
        axis=1,
    )
    for d in range(tiles_ref.shape[0]):
        tiles_ref[d] = tile


def y_faces_kernel(base_ref, low_ref, high_ref, face_low_ref, face_high_ref):
    for out, first in ((face_low_ref, 0), (face_high_ref, B - W)):
        for f in range(FIELDS):
            for r in range(W):
                y = first + r
                at = (r * FIELDS + f) * YR
                out[pl.ds(at, W), :] = low_ref[pl.ds(f * 24 + y, W, stride=8), :]
                out[pl.ds(at + W, B), :] = base_ref[pl.ds(f * 64 + y, B, stride=8), :]
                out[pl.ds(at + W + B, W), :] = high_ref[pl.ds(f * 24 + y, W, stride=8), :]
                out[pl.ds(at + XE, YR - XE), :] = jnp.zeros((YR - XE, 128), jnp.float32)


def surface_kernel(ny, place_ref, tiles_ref, own_ref, low_ref, high_ref):
    cells = B * YR
    at = lax.broadcasted_iota(jnp.int32, (cells, 128), 0)
    local = at % YR
    local = jnp.where(local < 11, local, local - YR)
    y = place_ref[0] * B + local
    ident = jnp.where((y >= 0) & (y < ny), (at // YR) * ny + y, -10000000).astype(jnp.float32)
    group = lax.broadcasted_iota(jnp.int32, (8, 128), 1) // 32
    hot, packed = [], []
    for first in range(0, tiles_ref.shape[0], 4):
        heads = jnp.where(group == 0, tiles_ref[first], 0.0)
        tails = jnp.where(group == 0, pltpu.roll(tiles_ref[first], 96, 1), 0.0)
        for i in range(1, 4):
            tile = tiles_ref[first + i]
            heads = jnp.where(group == i, pltpu.roll(tile, 32 * i, 1), heads)
            tails = jnp.where(group == i, pltpu.roll(tile, (96 + 32 * i) % 128, 1) if i > 1 else tile, tails)
        hot.append((ident == heads[0:1]).astype(jnp.float32))
        packed.append(jnp.concatenate([heads, tails], axis=0))
    packed = jnp.concatenate(packed, axis=1)
    packed = jnp.concatenate([packed, jnp.zeros((112, packed.shape[1]), jnp.float32)], axis=0)
    surface = lax.dot_general(
        jnp.concatenate(hot, axis=1),
        packed,
        (((1,), (1,)), ((), ())),
        precision=lax.Precision.HIGHEST,
        preferred_element_type=jnp.float32,
    )
    own_ref[...] = surface
    low_ref[...] = surface[0 : W * YR]
    high_ref[...] = surface[(B - W) * YR :]


def block_kernel(base_ref, low_ref, high_ref, ext):
    zero8 = jnp.zeros((8, 128), jnp.float32)
    for f in range(FIELDS):
        for e in range(XS):
            at = f * PLANE + e * YR
            if e == 0 or e == XS - 1:
                ext[pl.ds(at, 8), :] = zero8
            elif e <= W:
                ext[pl.ds(at, 8), :] = low_ref[f, e - 1]
            elif e <= W + B:
                ext[pl.ds(at, 8), :] = base_ref[f, e - 1 - W]
            else:
                ext[pl.ds(at, 8), :] = high_ref[f, e - 1 - W - B]
            ext[pl.ds(at + 8, 8), :] = zero8


def steps_kernel(
    steps,
    _,
    forward_ref,
    y_low_ref,
    y_high_ref,
    own_ref,
    low_ref,
    high_ref,
    ext,
    state_ref,
    kernels_ref,
    force_ref,
    change_ref,
    rate_ref,
    sem,
):
    for f in range(FIELDS):
        for r in range(W):
            src = (r * FIELDS + f) * YR
            ext[pl.ds(f * PLANE + YR + 8 + r, XE, stride=YR), :] = y_high_ref[pl.ds(src, XE), :]
            ext[pl.ds(f * PLANE + YR + 13 + r, XE, stride=YR), :] = y_low_ref[pl.ds(src, XE), :]
    force_ref[pl.ds(0, W * YR), :] = low_ref[...]
    force_ref[pl.ds(W * YR, B * YR), :] = own_ref[...]
    force_ref[pl.ds((W + B) * YR, W * YR), :] = high_ref[...]

    lanes = lax.broadcasted_iota(jnp.int32, (YR, 128), 1)

    def y_up(v):
        return pltpu.roll(v, YR - 1, 0)

    def y_down(v):
        return pltpu.roll(v, 1, 0)

    def z_up(v):
        return jnp.where(lanes == 127, 0.0, pltpu.roll(v, 127, 1))

    def z_down(v):
        return jnp.where(lanes == 0, 0.0, pltpu.roll(v, 1, 1))

    def get(f, e):
        return ext[pl.ds(pl.multiple_of(f * PLANE + e * YR, YR), YR), :]

    def put(f, e, v):
        ext[pl.ds(pl.multiple_of(f * PLANE + e * YR, YR), YR), :] = v

    for step in range(steps):

        def velocity(e):
            sxx, syy, szz, sxy, sxz, syz = [get(3 + f, e) for f in range(6)]
            ax = (get(3, e + 1) - sxx) + (sxy - y_down(sxy)) + (sxz - z_down(sxz))
            ay = (sxy - get(6, e - 1)) + (y_up(syy) - syy) + (syz - z_down(syz))
            az = (sxz - get(7, e - 1)) + (syz - y_down(syz)) + (z_up(szz) - szz)
            scale = DT * get(9, e)
            surface = force_ref[pl.ds(pl.multiple_of((e - 1) * YR, YR), YR), :]
            for c, accel in enumerate((ax, ay, az)):
                force = jnp.where(lanes == 0, pltpu.roll(surface, 127 - 3 * step - c, 1), 0.0)
                change = scale * (accel + force)
                put(c, e, get(c, e) + change)
                change_ref[c, e] = change[0:8]

        def stress(e):
            vx, vy, vz = [get(f, e) for f in range(3)]
            exx = vx - get(0, e - 1)
            eyy = vy - y_down(vy)
            ezz = vz - z_down(vz)
            exy = 0.5 * ((y_up(vx) - vx) + (get(1, e + 1) - vy))
            exz = 0.5 * ((z_up(vx) - vx) + (get(2, e + 1) - vz))
            eyz = 0.5 * ((z_up(vy) - vy) + (y_up(vz) - vz))
            trace = exx + eyy + ezz
            lam = get(10, e) * trace
            twice = 2.0 * get(11, e)
            for f, rate in enumerate((exx, eyy, ezz, exy, exz, eyz)):
                if f < 3:
                    put(3 + f, e, get(3 + f, e) + DT * (lam + twice * rate))
                else:
                    put(3 + f, e, get(3 + f, e) + DT * twice * rate)
                rate_ref[f, e] = rate[0:8]

        def pair(body, first):
            def run(i, carry):
                e = first + 2 * i
                body(e)
                body(e + 1)
                return carry

            return run

        lax.fori_loop(0, (XE - 2 * step) // 2, pair(velocity, 1 + step), 0)
        lax.fori_loop(0, (XE - 2 * step - 2) // 2, pair(stress, 2 + step), 0)
        if step == steps - 1:
            copies = [
                pltpu.make_async_copy(
                    ext.reshape(FIELDS, XS, YR, 128).at[f, pl.ds(1 + W, B), pl.ds(0, B)], state_ref.at[f], sem.at[f]
                )
                for f in range(9)
            ]
            for copy in copies:
                copy.start()

        def sensitivities(x, carry):
            e = x + 1 + W
            f = [forward_ref[step, c, x].astype(jnp.float32) for c in range(9)]
            change = [change_ref[c, e] for c in range(3)]
            rate = [rate_ref[c, e] for c in range(6)]
            trace = rate[0] + rate[1] + rate[2]
            terms = (
                f[0] * change[0] + f[1] * change[1] + f[2] * change[2],
                DT * (f[3] + f[4] + f[5]) * trace,
                DT
                * 2.0
                * (
                    (f[3] * rate[0] + f[4] * rate[1] + f[5] * rate[2])
                    + 2.0 * (f[6] * rate[3] + f[7] * rate[4] + f[8] * rate[5])
                ),
            )
            for k, term in enumerate(terms):
                kernels_ref[k, x] = kernels_ref[k, x] + term if step else term
            return carry

        lax.fori_loop(0, B, sensitivities, 0, unroll=4)

    for copy in copies:
        copy.wait()


def sum_kernel(events, parts_ref, out_ref):
    size = parts_ref.shape[0] // events
    total = parts_ref[0:size]
    for s in range(1, events):
        total = total + parts_ref[size * s : size * s + size]
    for s in range(events):
        out_ref[size * s : size * s + size] = total


def f32(*shape):
    return jax.ShapeDtypeStruct(shape, jnp.float32)


def in_hbm(a):
    return pltpu.with_memory_space_constraint(a, pltpu.HBM)


def on_device(
    adjoint_state,
    forward_state,
    inv_density,
    lame_lambda,
    shear_modulus,
    station_block,
    station_cell,
    station_trace,
    source_count,
):
    n_sx, n_sy, n_ev = lax.axis_size("sx"), lax.axis_size("sy"), lax.axis_size("ev")
    steps = forward_state.shape[1]
    ny = n_sy * B
    adj = adjoint_state[0]
    up_x = [(i, i + 1) for i in range(n_sx - 1)]
    up_y = [(i, i + 1) for i in range(n_sy - 1)]
    down_x = [(b, a) for a, b in up_x]
    down_y = [(b, a) for a, b in up_y]

    low_face, high_face, base = pl.pallas_call(
        x_faces_kernel,
        out_shape=[f32(FIELDS, W, 8, 128)] * 2 + [f32(FIELDS, B, 8, 128)],
        in_specs=[HBM] * 4,
        out_specs=[VMEM] * 3,
        scratch_shapes=[pltpu.SemaphoreType.DMA((3, 4))],
        compiler_params=pltpu.CompilerParams(vmem_limit_bytes=3 * MIB),
        name="x_faces",
    )(in_hbm(adj), in_hbm(inv_density), in_hbm(lame_lambda), in_hbm(shear_modulus))
    low = lax.ppermute(high_face, "sx", up_x)
    high = lax.ppermute(low_face, "sx", down_x)

    rows = station_cell.shape[1]
    tiles = pl.pallas_call(
        functools.partial(stations_kernel, ny),
        out_shape=f32(n_sy, 8, 128),
        in_specs=[SMEM] + [HBM] * 3,
        out_specs=VMEM,
        scratch_shapes=[
            pltpu.VMEM((1, rows), jnp.int32),
            pltpu.VMEM((1, rows), jnp.int32),
            pltpu.VMEM((9, 1, rows), jnp.float32),
            pltpu.SemaphoreType.DMA((3,)),
        ],
        compiler_params=pltpu.CompilerParams(vmem_limit_bytes=MIB),
        name="stations",
    )(
        source_count,
        in_hbm(station_block[:, :, 0]),
        in_hbm(station_cell),
        in_hbm(jnp.transpose(station_trace, (2, 0, 1))),
    )
    tiles = lax.all_to_all(tiles, "sy", split_axis=0, concat_axis=0, tiled=True)

    flat = lambda a: a.reshape(-1, 128)
    y_low_face, y_high_face = pl.pallas_call(
        y_faces_kernel,
        out_shape=[f32(W * FIELDS * YR, 128)] * 2,
        in_specs=[VMEM] * 3,
        out_specs=[VMEM] * 2,
        compiler_params=pltpu.CompilerParams(vmem_limit_bytes=4 * MIB),
        name="y_faces",
    )(flat(base), flat(low), flat(high))
    y_low = lax.ppermute(y_high_face, "sy", up_y)
    y_high = lax.ppermute(y_low_face, "sy", down_y)

    place = lax.axis_index("sy").astype(jnp.int32).reshape(1)
    own_surface, low_surface, high_surface = pl.pallas_call(
        functools.partial(surface_kernel, ny),
        out_shape=[f32(B * YR, 128), f32(W * YR, 128), f32(W * YR, 128)],
        in_specs=[SMEM, VMEM],
        out_specs=[VMEM] * 3,
        compiler_params=pltpu.CompilerParams(vmem_limit_bytes=4 * MIB),
        name="surface",
    )(place, tiles)
    below = lax.ppermute(high_surface, "sx", up_x)
    above = lax.ppermute(low_surface, "sx", down_x)

    ext = pl.pallas_call(
        block_kernel,
        out_shape=f32(FIELDS * PLANE, 128),
        in_specs=[VMEM] * 3,
        out_specs=VMEM,
        compiler_params=pltpu.CompilerParams(vmem_limit_bytes=4 * MIB),
        name="block",
    )(base, low, high)

    _, state, kernels = pl.pallas_call(
        functools.partial(steps_kernel, steps),
        out_shape=[f32(FIELDS * PLANE, 128), f32(9, B, 8, 128), f32(3, B, 8, 128)],
        in_specs=[VMEM] * 7,
        out_specs=[VMEM, HBM, VMEM],
        input_output_aliases={0: 0},
        scratch_shapes=[
            pltpu.VMEM((XE * YR, 128), jnp.float32),
            pltpu.VMEM((3, XS, 8, 128), jnp.float32),
            pltpu.VMEM((6, XS, 8, 128), jnp.float32),
            pltpu.SemaphoreType.DMA((9,)),
        ],
        compiler_params=pltpu.CompilerParams(vmem_limit_bytes=8 * MIB),
        name="steps",
    )(ext, forward_state[0], y_low, y_high, own_surface, below, above)

    parts = lax.all_to_all(kernels.reshape(3 * B, 8, 128), "ev", split_axis=0, concat_axis=0, tiled=True)
    shared = pl.pallas_call(
        functools.partial(sum_kernel, n_ev), out_shape=f32(3 * B, 8, 128), in_specs=[VMEM], out_specs=VMEM, compiler_params=pltpu.CompilerParams(vmem_limit_bytes=1 * MIB),
        name="event_sum"
    )(parts)
    total = lax.all_to_all(shared, "ev", split_axis=0, concat_axis=0, tiled=True)
    return state[None], total.reshape(3, B, 8, 128)


def solution(mesh):
    return jax.shard_map(
        on_device,
        mesh=mesh,
        in_specs=(
            P("ev", None, "sx", "sy", None),
            P("ev", None, None, "sx", "sy", None),
            P("sx", "sy", None),
            P("sx", "sy", None),
            P("sx", "sy", None),
            P("ev", ("sx", "sy"), None),
            P("ev", ("sx", "sy")),
            P("ev", ("sx", "sy"), None),
            P("ev", ("sx", "sy")),
        ),
        out_specs=(P("ev", None, "sx", "sy", None), P(None, "sx", "sy", None)),
        check_vma=False,
    )
```

time: 78.5 us -> 85.5 us (1.089)
  the two profiles are of different devices: /device:TPU:256 before, /device:TPU:128 now
where the time goes in v2:
time: 85.5 us; the launch traced here: 85.1 us
  starting transfers between devices  34 us (40%)
  blocking collectives  26.4 us (31%)
  waiting for transfers between devices  15 us (18%)
  Pallas kernels  7.53 us (9%)
  between operations  1.4 us (2%)
    all_to_all x1, blocking collectives, on_device(): lax.all_to_all(kernels.reshape(3 * B, 8, 128), 'ev', split_axis=0, concat...  15.3 us
    all_to_all x1, blocking collectives, on_device(): lax.all_to_all(shared, 'ev', split_axis=0, concat_axis=0, tiled=True)  11.1 us
    ppermute x1, starting transfers between devices, on_device(): high = lax.ppermute(low_face, 'sx', down_x)  9.38 us
    all_to_all x1, starting transfers between devices, on_device(): tiles = lax.all_to_all(tiles, 'sy', split_axis=0, concat_axis=0, tiled=True)  8.55 us
    all_to_all x1, waiting for transfers between devices, on_device(): tiles = lax.all_to_all(tiles, 'sy', split_axis=0, concat_axis=0, tiled=True)  7.79 us
    ppermute x1, starting transfers between devices, on_device(): below = lax.ppermute(high_surface, 'sx', up_x)  6.4 us
    ppermute x1, starting transfers between devices, on_device(): low = lax.ppermute(high_face, 'sx', up_x)  5.19 us
    ppermute x1, waiting for transfers between devices, on_device(): above = lax.ppermute(low_surface, 'sx', down_x)  4.6 us
  transfers between devices with their start and end apart: 7, of which 4 were waited for; matrix products, arithmetic and copies ran while one was open for 0% of the time, Pallas kernels for 2%

profile of v2, /device:TPU:128, one launch (start us, length us, event | category | flops | bytes accessed | tf_op | source)
XLA Modules:
  0.0 85.1 jit_solution(877316936319445733)
XLA Ops:
  0.6 1.3 %x_faces.1 = (f32[12,3,8,128]{3,2,1,0:T(8,128)S(1)}, f32[12,3,8,128]{3,2,1,0:T(8,128)S(1)}, f32[12,8,8,128]{3,2,1,0:T(8,128)S(1)}) custom-call(f32[9,8,8,128]{3,2,1,0:T(8,128)} %bitcast.17, f32[8,8,128]{2,1,0:T(8,128)} %rho_ref.1, f32[8,8,128]{2,1,0:T(8,128)} %lam_ref.1, f32[8,8,128]{2,1,0:T(8,128)} %mu_ref.1), custom_call_target="tpu_custom_call" | custom-call | tf_op jit(solution)/shard_map/x_faces/pallas_call | solution.py:285
  1.9 5.2 %collective-permute-start = (f32[12,3,8,128]{3,2,1,0:T(8,128)S(1)}, f32[12,3,8,128]{3,2,1,0:T(8,128)S(1)}, u32[]{:S(2)}, u32[]{:S(2)}) collective-permute-start(f32[12,3,8,128]{3,2,1,0:T(8,128)S(1)} %get-tuple-element.13), channel_id=1, source_target_pairs={{0,128},{128,256},{256,384},{384,512},{512,640},{640,768},{768,896... | collective-permute-start | bytes 442376 | tf_op jit(solution)/shard_map/ppermute | solution.py:294
  7.1 9.4 %collective-permute-start.1 = (f32[12,3,8,128]{3,2,1,0:T(8,128)S(1)}, f32[12,3,8,128]{3,2,1,0:T(8,128)S(1)}, u32[]{:S(2)}, u32[]{:S(2)}) collective-permute-start(f32[12,3,8,128]{3,2,1,0:T(8,128)S(1)} %get-tuple-element.14), channel_id=1, source_target_pairs={{128,0},{256,128},{384,256},{512,384},{640,512},{768,640},{896,768... | collective-permute-start | bytes 442376 | tf_op jit(solution)/shard_map/ppermute | solution.py:295
  16.5 1.2 %collective-permute-done.low_ref = f32[12,3,8,128]{3,2,1,0:T(8,128)S(1)} collective-permute-done((f32[12,3,8,128]{3,2,1,0:T(8,128)S(1)}, f32[12,3,8,128]{3,2,1,0:T(8,128)S(1)}, u32[]{:S(2)}, u32[]{:S(2)}) %collective-permute-start) | collective-permute-done | bytes 147488 | tf_op jit(solution)/shard_map/ppermute | solution.py:294
  17.7 1.5 %collective-permute-done.1.high_ref = f32[12,3,8,128]{3,2,1,0:T(8,128)S(1)} collective-permute-done((f32[12,3,8,128]{3,2,1,0:T(8,128)S(1)}, f32[12,3,8,128]{3,2,1,0:T(8,128)S(1)}, u32[]{:S(2)}, u32[]{:S(2)}) %collective-permute-start.1) | collective-permute-done | bytes 147488 | tf_op jit(solution)/shard_map/ppermute | solution.py:295
  19.2 0.0 copy-start
  19.2 0.1 y_faces.1
  19.3 1.3 %collective-permute-start.2 = (f32[576,128]{1,0:T(8,128)S(1)}, f32[576,128]{1,0:T(8,128)S(1)}, u32[]{:S(2)}, u32[]{:S(2)}) collective-permute-start(f32[576,128]{1,0:T(8,128)S(1)} %get-tuple-element.15), channel_id=1, source_target_pairs={{0,8},{8,16},{16,24},{24,32},{32,40},{40,48},{48,56},{56,64},{64,7... | collective-permute-start | bytes 884744 | tf_op jit(solution)/shard_map/ppermute | solution.py:328
  20.6 1.3 %collective-permute-start.3 = (f32[576,128]{1,0:T(8,128)S(1)}, f32[576,128]{1,0:T(8,128)S(1)}, u32[]{:S(2)}, u32[]{:S(2)}) collective-permute-start(f32[576,128]{1,0:T(8,128)S(1)} %get-tuple-element.16), channel_id=1, source_target_pairs={{8,0},{16,8},{24,16},{32,24},{40,32},{48,40},{56,48},{64,56},{72,6... | collective-permute-start | bytes 884744 | tf_op jit(solution)/shard_map/ppermute | solution.py:329
  22.6 1.5 %stations.1 = f32[16,8,128]{2,1,0:T(8,128)} custom-call(s32[1,1]{1,0:T(1,128)S(6)} %copy.14.count_ref, s32[1,32]{1,0:T(1,128)} %bitcast.19, s32[1,32]{1,0:T(1,128)} %cell_hbm.1, f32[9,1,32]{2,1,0:T(1,128)} %bitcast.18), custom_call_target="tpu_custom_call" | custom-call | tf_op jit(solution)/shard_map/stations/pallas_call | solution.py:298
  24.0 8.6 %all-to-all-start = ((f32[16,8,128]{2,1,0:T(8,128)}), f32[16,8,128]{2,1,0:T(8,128)S(1)}, u32[]{:S(2)}, u32[]{:S(2)}) async-start(f32[16,8,128]{2,1,0:T(8,128)} %stations.1), calls=%async_computation | async-start | bytes 131072 | tf_op jit(solution)/shard_map/all_to_all | solution.py:317
  32.6 7.8 %all-to-all-done.tiles_ref = f32[16,8,128]{2,1,0:T(8,128)S(1)} async-done(((f32[16,8,128]{2,1,0:T(8,128)}), f32[16,8,128]{2,1,0:T(8,128)S(1)}, u32[]{:S(2)}, u32[]{:S(2)}) %all-to-all-start) | async-done | bytes 65568 | tf_op jit(solution)/shard_map/all_to_all | solution.py:317
  40.4 0.4 surface.1
  40.8 6.4 %collective-permute-start.4 = (f32[48,128]{1,0:T(8,128)S(1)}, f32[48,128]{1,0:T(8,128)S(1)}, u32[]{:S(2)}, u32[]{:S(2)}) collective-permute-start(f32[48,128]{1,0:T(8,128)S(1)} %get-tuple-element.18), channel_id=1, source_target_pairs={{0,128},{128,256},{256,384},{384,512},{512,640},{640,768},{768,896... | collective-permute-start | bytes 73736 | tf_op jit(solution)/shard_map/ppermute | solution.py:340
  47.2 1.9 %collective-permute-start.5 = (f32[48,128]{1,0:T(8,128)S(1)}, f32[48,128]{1,0:T(8,128)S(1)}, u32[]{:S(2)}, u32[]{:S(2)}) collective-permute-start(f32[48,128]{1,0:T(8,128)S(1)} %get-tuple-element.19), channel_id=1, source_target_pairs={{128,0},{256,128},{384,256},{512,384},{640,512},{768,640},{896,768... | collective-permute-start | bytes 73736 | tf_op jit(solution)/shard_map/ppermute | solution.py:341
  49.2 0.1 block.1._
  49.3 0.0 collective-permute-done.4.low_ref
  49.3 4.6 %collective-permute-done.5.high_ref = f32[48,128]{1,0:T(8,128)S(1)} collective-permute-done((f32[48,128]{1,0:T(8,128)S(1)}, f32[48,128]{1,0:T(8,128)S(1)}, u32[]{:S(2)}, u32[]{:S(2)}) %collective-permute-start.5) | collective-permute-done | bytes 24608 | tf_op jit(solution)/shard_map/ppermute | solution.py:341
  53.9 0.0 collective-permute-done.2.y_low_ref
  53.9 0.0 collective-permute-done.3.y_high_ref
  53.9 0.0 copy-done
  53.9 4.1 %steps.1 = (f32[3072,128]{1,0:T(8,128)S(1)}, f32[9,8,8,128]{3,2,1,0:T(8,128)}, f32[3,8,8,128]{3,2,1,0:T(8,128)S(1)}) custom-call(f32[3072,128]{1,0:T(8,128)S(1)} %block.1._, bf16[3,9,8,8,128]{4,3,2,1,0:T(8,128)(2,1)S(1)} %bitcast.14, f32[576,128]{1,0:T(8,128)S(1)} %collective-permute-done.2.y_low_ref, ...), custom_call_target="tpu_custom_call", output_to_operand_aliasing={{0}: (0, {})} | custom-call | tf_op jit(solution)/shard_map/steps/pallas_call | solution.py:352
  58.0 15.3 %all_to_all.15.parts_ref = f32[24,8,128]{2,1,0:T(8,128)S(1)} all-to-all(f32[24,8,128]{2,1,0:T(8,128)S(1)} %bitcast.15), channel_id=1, replica_groups=mesh['sx'=8,'sy'=16,'ev'=8] {'ev'}, dimensions={0} | all-to-all | bytes 196608 | tf_op jit(solution)/shard_map/all_to_all | solution.py:368
  73.3 11.1 %all_to_all.16 = f32[24,8,128]{2,1,0:T(8,128)S(1)} all-to-all(f32[24,8,128]{2,1,0:T(8,128)S(1)} %event_sum.1), channel_id=1, replica_groups=mesh['sx'=8,'sy'=16,'ev'=8] {'ev'}, dimensions={0} | all-to-all | bytes 196608 | tf_op jit(solution)/shard_map/all_to_all | solution.py:373
  84.4 0.6 copy.15
  (1 shorter events, 0.0 us)
Async XLA Ops:
  1.9 15.8 %collective-permute-start = (f32[12,3,8,128]{3,2,1,0:T(8,128)S(1)}, f32[12,3,8,128]{3,2,1,0:T(8,128)S(1)}, u32[]{:S(2)}, u32[]{:S(2)}) collective-permute-start(f32[12,3,8,128]{3,2,1,0:T(8,128)S(1)} %get-tuple-element.13), channel_id=1, source_target_pairs={{0,128},{128,256},{256,384},{384,512},{512,640},{640,768},{768,896... | collective-permute-start | bytes 442376 | tf_op jit(solution)/shard_map/ppermute | solution.py:294
  7.1 12.0 %collective-permute-start.1 = (f32[12,3,8,128]{3,2,1,0:T(8,128)S(1)}, f32[12,3,8,128]{3,2,1,0:T(8,128)S(1)}, u32[]{:S(2)}, u32[]{:S(2)}) collective-permute-start(f32[12,3,8,128]{3,2,1,0:T(8,128)S(1)} %get-tuple-element.14), channel_id=1, source_target_pairs={{128,0},{256,128},{384,256},{512,384},{640,512},{768,640},{896,768... | collective-permute-start | bytes 442376 | tf_op jit(solution)/shard_map/ppermute | solution.py:295
  19.2 34.7 %copy-start = (bf16[1,3,9,8,8,128]{5,4,3,2,1,0:T(8,128)(2,1)S(1)}, bf16[1,3,9,8,8,128]{5,4,3,2,1,0:T(8,128)(2,1)}, u32[]{:S(2)}) copy-start(bf16[1,3,9,8,8,128]{5,4,3,2,1,0:T(8,128)(2,1)} %param.10) | copy-start | bytes 1327108
  19.3 34.6 %collective-permute-start.2 = (f32[576,128]{1,0:T(8,128)S(1)}, f32[576,128]{1,0:T(8,128)S(1)}, u32[]{:S(2)}, u32[]{:S(2)}) collective-permute-start(f32[576,128]{1,0:T(8,128)S(1)} %get-tuple-element.15), channel_id=1, source_target_pairs={{0,8},{8,16},{16,24},{24,32},{32,40},{40,48},{48,56},{56,64},{64,7... | collective-permute-start | bytes 884744 | tf_op jit(solution)/shard_map/ppermute | solution.py:328
  20.6 33.3 %collective-permute-start.3 = (f32[576,128]{1,0:T(8,128)S(1)}, f32[576,128]{1,0:T(8,128)S(1)}, u32[]{:S(2)}, u32[]{:S(2)}) collective-permute-start(f32[576,128]{1,0:T(8,128)S(1)} %get-tuple-element.16), channel_id=1, source_target_pairs={{8,0},{16,8},{24,16},{32,24},{40,32},{48,40},{56,48},{64,56},{72,6... | collective-permute-start | bytes 884744 | tf_op jit(solution)/shard_map/ppermute | solution.py:329
  24.0 16.4 %all-to-all-start = ((f32[16,8,128]{2,1,0:T(8,128)}), f32[16,8,128]{2,1,0:T(8,128)S(1)}, u32[]{:S(2)}, u32[]{:S(2)}) async-start(f32[16,8,128]{2,1,0:T(8,128)} %stations.1), calls=%async_computation | async-start | bytes 131072 | tf_op jit(solution)/shard_map/all_to_all | solution.py:317
  40.8 8.5 %collective-permute-start.4 = (f32[48,128]{1,0:T(8,128)S(1)}, f32[48,128]{1,0:T(8,128)S(1)}, u32[]{:S(2)}, u32[]{:S(2)}) collective-permute-start(f32[48,128]{1,0:T(8,128)S(1)} %get-tuple-element.18), channel_id=1, source_target_pairs={{0,128},{128,256},{256,384},{384,512},{512,640},{640,768},{768,896... | collective-permute-start | bytes 73736 | tf_op jit(solution)/shard_map/ppermute | solution.py:340
  47.2 6.7 %collective-permute-start.5 = (f32[48,128]{1,0:T(8,128)S(1)}, f32[48,128]{1,0:T(8,128)S(1)}, u32[]{:S(2)}, u32[]{:S(2)}) collective-permute-start(f32[48,128]{1,0:T(8,128)S(1)} %get-tuple-element.19), channel_id=1, source_target_pairs={{128,0},{256,128},{384,256},{512,384},{640,512},{768,640},{896,768... | collective-permute-start | bytes 73736 | tf_op jit(solution)/shard_map/ppermute | solution.py:341

commit v3 on v2

--- a/solution.py
+++ b/solution.py
@@ -22,28 +22,41 @@
 HBM = pl.BlockSpec(memory_space=pltpu.HBM)
 
 
-def x_faces_kernel(adj_ref, rho_ref, lam_ref, mu_ref, low_ref, high_ref, base_ref, sems):
+def x_faces_kernel(
+    ny,
+    adj_hbm,
+    rho_hbm,
+    lam_hbm,
+    mu_hbm,
+    count_ref,
+    block_hbm,
+    cell_hbm,
+    trace_hbm,
+    low_ref,
+    high_ref,
+    base_ref,
+    block_ref,
+    cell_ref,
+    trace_ref,
+    sems,
+):
+    params = (rho_hbm, lam_hbm, mu_hbm)
+    rows_in = [
+        pltpu.make_async_copy(source, target, sems.at[3, i])
+        for i, (source, target) in enumerate(((block_hbm, block_ref), (cell_hbm, cell_ref), (trace_hbm, trace_ref)))
+    ]
     copies = []
     for side, (out, first) in enumerate(((low_ref, 0), (high_ref, B - W))):
-        pieces = [(adj_ref.at[:, pl.ds(first, W)], out.at[pl.ds(0, 9)])]
-        pieces += [(p.at[pl.ds(first, W)], out.at[9 + i]) for i, p in enumerate((rho_ref, lam_ref, mu_ref))]
+        pieces = [(adj_hbm.at[:, pl.ds(first, W)], out.at[pl.ds(0, 9)])]
+        pieces += [(p.at[pl.ds(first, W)], out.at[9 + i]) for i, p in enumerate(params)]
         for i, (source, target) in enumerate(pieces):
             copies.append(pltpu.make_async_copy(source, target, sems.at[side, i]))
-    copies.append(pltpu.make_async_copy(adj_ref, base_ref.at[pl.ds(0, 9)], sems.at[2, 0]))
-    for i, p in enumerate((rho_ref, lam_ref, mu_ref)):
+    copies.append(pltpu.make_async_copy(adj_hbm, base_ref.at[pl.ds(0, 9)], sems.at[2, 0]))
+    for i, p in enumerate(params):
         copies.append(pltpu.make_async_copy(p, base_ref.at[9 + i], sems.at[2, 1 + i]))
-    for copy in copies:
+    for copy in rows_in + copies:
         copy.start()
-    for copy in copies:
-        copy.wait()
-
-
-def stations_kernel(ny, count_ref, block_hbm, cell_hbm, trace_hbm, tiles_ref, block_ref, cell_ref, trace_ref, sems):
-    moves = ((block_hbm, block_ref), (cell_hbm, cell_ref), (trace_hbm, trace_ref))
-    copies = [pltpu.make_async_copy(source, target, sems.at[i]) for i, (source, target) in enumerate(moves)]
-    for copy in copies:
-        copy.start()
-    for copy in copies:
+    for copy in rows_in:
         copy.wait()
     rows = cell_ref.shape[1]
     cell = cell_ref[...]
@@ -51,10 +64,30 @@
     live = lax.broadcasted_iota(jnp.int32, (1, rows), 1) < count_ref[0, 0]
     parts = [jnp.where(live, key, DEAD)] + [jnp.where(live, trace_ref[k], 0.0) for k in range(9)]
     parts += [jnp.zeros((1, rows), jnp.float32)] * 6
-    tile = jnp.concatenate(
+    pack = jnp.concatenate(
         [jnp.concatenate(parts[:8], axis=0), jnp.concatenate(parts[8:], axis=0), jnp.zeros((8, 128 - 2 * rows), jnp.float32)],
         axis=1,
     )
+    for out in (low_ref, high_ref):
+        out[FIELDS, 0] = pack
+        for spare in range(1, W):
+            out[FIELDS, spare] = jnp.zeros((8, 128), jnp.float32)
+    for copy in copies:
+        copy.wait()
+
+
+def tiles_kernel(ny, own_ref, low_ref, high_ref, tiles_ref):
+    row = lax.broadcasted_iota(jnp.int32, (8, 128), 0)
+    group = lax.broadcasted_iota(jnp.int32, (8, 128), 1) // 32
+    tile = jnp.zeros((8, 128), jnp.float32)
+    for s, (ref, shift) in enumerate(((own_ref, W), (low_ref, W - B), (high_ref, W + B))):
+        pack = ref[FIELDS, 0]
+        head = jnp.where(row == 0, pack + float(shift * ny), pack)
+        head = pltpu.roll(head, 32 * s, 1) if s else head
+        tail = pltpu.roll(pack, 64, 1)
+        tail = pltpu.roll(tail, 2 * s, 0) if s else tail
+        tile = jnp.where(group == s, head, tile)
+        tile = jnp.where((group == 3) & (row // 2 == s), tail, tile)
     for d in range(tiles_ref.shape[0]):
         tiles_ref[d] = tile
 
@@ -71,36 +104,34 @@
                 out[pl.ds(at + XE, YR - XE), :] = jnp.zeros((YR - XE, 128), jnp.float32)
 
 
-def surface_kernel(ny, place_ref, tiles_ref, own_ref, low_ref, high_ref):
-    cells = B * YR
-    at = lax.broadcasted_iota(jnp.int32, (cells, 128), 0)
-    local = at % YR
-    local = jnp.where(local < 11, local, local - YR)
-    y = place_ref[0] * B + local
-    ident = jnp.where((y >= 0) & (y < ny), (at // YR) * ny + y, -10000000).astype(jnp.float32)
+def surface_kernel(ny, place_ref, tiles_ref, surface_ref):
     group = lax.broadcasted_iota(jnp.int32, (8, 128), 1) // 32
-    hot, packed = [], []
-    for first in range(0, tiles_ref.shape[0], 4):
-        heads = jnp.where(group == 0, tiles_ref[first], 0.0)
-        tails = jnp.where(group == 0, pltpu.roll(tiles_ref[first], 96, 1), 0.0)
-        for i in range(1, 4):
-            tile = tiles_ref[first + i]
-            heads = jnp.where(group == i, pltpu.roll(tile, 32 * i, 1), heads)
-            tails = jnp.where(group == i, pltpu.roll(tile, (96 + 32 * i) % 128, 1) if i > 1 else tile, tails)
-        hot.append((ident == heads[0:1]).astype(jnp.float32))
-        packed.append(jnp.concatenate([heads, tails], axis=0))
-    packed = jnp.concatenate(packed, axis=1)
-    packed = jnp.concatenate([packed, jnp.zeros((112, packed.shape[1]), jnp.float32)], axis=0)
-    surface = lax.dot_general(
-        jnp.concatenate(hot, axis=1),
-        packed,
-        (((1,), (1,)), ((), ())),
-        precision=lax.Precision.HIGHEST,
-        preferred_element_type=jnp.float32,
-    )
-    own_ref[...] = surface
-    low_ref[...] = surface[0 : W * YR]
-    high_ref[...] = surface[(B - W) * YR :]
+    for s, first, count in ((0, W, B), (1, 0, W), (2, W + B, W)):
+        cells = count * YR
+        at = lax.broadcasted_iota(jnp.int32, (cells, 128), 0)
+        local = at % YR
+        local = jnp.where(local < 11, local, local - YR)
+        y = place_ref[0] * B + local
+        ident = jnp.where((y >= 0) & (y < ny), (first + at // YR) * ny + y, -10000000).astype(jnp.float32)
+        hot, packed = [], []
+        for source in range(0, tiles_ref.shape[0], 4):
+            heads = tails = jnp.zeros((8, 128), jnp.float32)
+            for i in range(4):
+                tile = tiles_ref[source + i]
+                head, tail = (32 * (i - s)) % 128, (32 * (i - 3)) % 128
+                heads = jnp.where(group == i, pltpu.roll(tile, head, 1) if head else tile, heads)
+                tails = jnp.where(group == i, pltpu.roll(tile, tail, 1) if tail else tile, tails)
+            hot.append((ident == heads[0:1]).astype(jnp.float32))
+            packed.append(jnp.concatenate([heads, pltpu.roll(tails, 8 - 2 * s, 0) if s else tails], axis=0))
+        packed = jnp.concatenate(packed, axis=1)
+        packed = jnp.concatenate([packed, jnp.zeros((112, packed.shape[1]), jnp.float32)], axis=0)
+        surface_ref[pl.ds(first * YR, cells), :] = lax.dot_general(
+            jnp.concatenate(hot, axis=1),
+            packed,
+            (((1,), (1,)), ((), ())),
+            precision=lax.Precision.HIGHEST,
+            preferred_element_type=jnp.float32,
+        )
 
 
 def block_kernel(base_ref, low_ref, high_ref, ext):
@@ -125,13 +156,10 @@
     forward_ref,
     y_low_ref,
     y_high_ref,
-    own_ref,
-    low_ref,
-    high_ref,
+    force_ref,
     ext,
     state_ref,
     kernels_ref,
-    force_ref,
     change_ref,
     rate_ref,
     sem,
@@ -141,9 +169,6 @@
             src = (r * FIELDS + f) * YR
             ext[pl.ds(f * PLANE + YR + 8 + r, XE, stride=YR), :] = y_high_ref[pl.ds(src, XE), :]
             ext[pl.ds(f * PLANE + YR + 13 + r, XE, stride=YR), :] = y_low_ref[pl.ds(src, XE), :]
-    force_ref[pl.ds(0, W * YR), :] = low_ref[...]
-    force_ref[pl.ds(W * YR, B * YR), :] = own_ref[...]
-    force_ref[pl.ds((W + B) * YR, W * YR), :] = high_ref[...]
 
     lanes = lax.broadcasted_iota(jnp.int32, (YR, 128), 1)
 
@@ -282,38 +307,41 @@
     down_x = [(b, a) for a, b in up_x]
     down_y = [(b, a) for a, b in up_y]
 
+    rows = station_cell.shape[1]
     low_face, high_face, base = pl.pallas_call(
-        x_faces_kernel,
-        out_shape=[f32(FIELDS, W, 8, 128)] * 2 + [f32(FIELDS, B, 8, 128)],
-        in_specs=[HBM] * 4,
+        functools.partial(x_faces_kernel, ny),
+        out_shape=[f32(FIELDS + 1, W, 8, 128)] * 2 + [f32(FIELDS, B, 8, 128)],
+        in_specs=[HBM] * 4 + [SMEM] + [HBM] * 3,
         out_specs=[VMEM] * 3,
-        scratch_shapes=[pltpu.SemaphoreType.DMA((3, 4))],
-        compiler_params=pltpu.CompilerParams(vmem_limit_bytes=3 * MIB),
-        name="x_faces",
-    )(in_hbm(adj), in_hbm(inv_density), in_hbm(lame_lambda), in_hbm(shear_modulus))
-    low = lax.ppermute(high_face, "sx", up_x)
-    high = lax.ppermute(low_face, "sx", down_x)
-
-    rows = station_cell.shape[1]
-    tiles = pl.pallas_call(
-        functools.partial(stations_kernel, ny),
-        out_shape=f32(n_sy, 8, 128),
-        in_specs=[SMEM] + [HBM] * 3,
-        out_specs=VMEM,
         scratch_shapes=[
             pltpu.VMEM((1, rows), jnp.int32),
             pltpu.VMEM((1, rows), jnp.int32),
             pltpu.VMEM((9, 1, rows), jnp.float32),
-            pltpu.SemaphoreType.DMA((3,)),
+            pltpu.SemaphoreType.DMA((4, 4)),
         ],
-        compiler_params=pltpu.CompilerParams(vmem_limit_bytes=MIB),
-        name="stations",
+        compiler_params=pltpu.CompilerParams(vmem_limit_bytes=3 * MIB),
+        name="x_faces",
     )(
+        in_hbm(adj),
+        in_hbm(inv_density),
+        in_hbm(lame_lambda),
+        in_hbm(shear_modulus),
         source_count,
         in_hbm(station_block[:, :, 0]),
         in_hbm(station_cell),
         in_hbm(jnp.transpose(station_trace, (2, 0, 1))),
     )
+    low = lax.ppermute(high_face, "sx", up_x)
+    high = lax.ppermute(low_face, "sx", down_x)
+
+    tiles = pl.pallas_call(
+        functools.partial(tiles_kernel, ny),
+        out_shape=f32(n_sy, 8, 128),
+        in_specs=[VMEM] * 3,
+        out_specs=VMEM,
+        compiler_params=pltpu.CompilerParams(vmem_limit_bytes=2 * MIB),
+        name="tiles",
+    )(low_face, low, high)
     tiles = lax.all_to_all(tiles, "sy", split_axis=0, concat_axis=0, tiled=True)
 
     flat = lambda a: a.reshape(-1, 128)
@@ -329,16 +357,14 @@
     y_high = lax.ppermute(y_low_face, "sy", down_y)
 
     place = lax.axis_index("sy").astype(jnp.int32).reshape(1)
-    own_surface, low_surface, high_surface = pl.pallas_call(
+    surface = pl.pallas_call(
         functools.partial(surface_kernel, ny),
-        out_shape=[f32(B * YR, 128), f32(W * YR, 128), f32(W * YR, 128)],
+        out_shape=f32(XE * YR, 128),
         in_specs=[SMEM, VMEM],
-        out_specs=[VMEM] * 3,
+        out_specs=VMEM,
         compiler_params=pltpu.CompilerParams(vmem_limit_bytes=4 * MIB),
         name="surface",
     )(place, tiles)
-    below = lax.ppermute(high_surface, "sx", up_x)
-    above = lax.ppermute(low_surface, "sx", down_x)
 
     ext = pl.pallas_call(
         block_kernel,
@@ -352,18 +378,17 @@
     _, state, kernels = pl.pallas_call(
         functools.partial(steps_kernel, steps),
         out_shape=[f32(FIELDS * PLANE, 128), f32(9, B, 8, 128), f32(3, B, 8, 128)],
-        in_specs=[VMEM] * 7,
+        in_specs=[VMEM] * 5,
         out_specs=[VMEM, HBM, VMEM],
         input_output_aliases={0: 0},
         scratch_shapes=[
-            pltpu.VMEM((XE * YR, 128), jnp.float32),
             pltpu.VMEM((3, XS, 8, 128), jnp.float32),
             pltpu.VMEM((6, XS, 8, 128), jnp.float32),
             pltpu.SemaphoreType.DMA((9,)),
         ],
         compiler_params=pltpu.CompilerParams(vmem_limit_bytes=8 * MIB),
         name="steps",
-    )(ext, forward_state[0], y_low, y_high, own_surface, below, above)
+    )(ext, forward_state[0], y_low, y_high, surface)
 
     parts = lax.all_to_all(kernels.reshape(3 * B, 8, 128), "ev", split_axis=0, concat_axis=0, tiled=True)
     shared = pl.pallas_call(

time: 85.5 us -> 74.4 us (0.87)
  the two profiles are of different devices: /device:TPU:128 before, /device:TPU:256 now
where the time goes in v3:
time: 74.4 us; the launch traced here: 74.1 us
  blocking collectives  26.6 us (36%)
  starting transfers between devices  21.7 us (29%)
  waiting for transfers between devices  16 us (22%)
  Pallas kernels  7.8 us (10%)
  between operations  1.39 us (2%)
    all_to_all x1, blocking collectives, on_device(): lax.all_to_all(kernels.reshape(3 * B, 8, 128), 'ev', split_axis=0, concat...  15.5 us
    all_to_all x1, starting transfers between devices, on_device(): tiles = lax.all_to_all(tiles, 'sy', split_axis=0, concat_axis=0, tiled=True)  11.8 us
    all_to_all x1, blocking collectives, on_device(): lax.all_to_all(shared, 'ev', split_axis=0, concat_axis=0, tiled=True)  11.1 us
    all_to_all x1, waiting for transfers between devices, on_device(): tiles = lax.all_to_all(tiles, 'sy', split_axis=0, concat_axis=0, tiled=True)  7.67 us
    ppermute x1, waiting for transfers between devices, on_device(): high = lax.ppermute(low_face, 'sx', down_x)  6.88 us
    ppermute x1, starting transfers between devices, on_device(): low = lax.ppermute(high_face, 'sx', up_x)  5.19 us
    pallas_call x1, Pallas kernels, on_device(): pl.pallas_call(functools.partial(steps_kernel, steps), out_shape=[f32(FIE...  4.1 us
    ppermute x1, starting transfers between devices, on_device(): high = lax.ppermute(low_face, 'sx', down_x)  1.92 us
  transfers between devices with their start and end apart: 5, of which 3 were waited for; matrix products, arithmetic and copies ran while one was open for 0% of the time, Pallas kernels for 2%

profile of v3, /device:TPU:256, one launch (start us, length us, event | category | flops | bytes accessed | tf_op | source)
XLA Modules:
  0.0 74.1 jit_solution(12559518769775008274)
XLA Ops:
  1.3 1.3 %x_faces.1 = (f32[13,3,8,128]{3,2,1,0:T(8,128)S(1)}, f32[13,3,8,128]{3,2,1,0:T(8,128)S(1)}, f32[12,8,8,128]{3,2,1,0:T(8,128)S(1)}) custom-call(f32[9,8,8,128]{3,2,1,0:T(8,128)} %bitcast.17, f32[8,8,128]{2,1,0:T(8,128)} %rho_hbm.1, f32[8,8,128]{2,1,0:T(8,128)} %lam_hbm.1, f32[8,8,128]{2,1,0:T(8,128)} %mu_hbm.1, s32[1,1]{1,0:T(1,128)S(6)} %copy.14.count_ref, ...), custom_call_target="tpu_custom_call" | custom-call | tf_op jit(solution)/shard_map/x_faces/pallas_call | solution.py:311
  2.6 5.2 %collective-permute-start = (f32[13,3,8,128]{3,2,1,0:T(8,128)S(1)}, f32[13,3,8,128]{3,2,1,0:T(8,128)S(1)}, u32[]{:S(2)}, u32[]{:S(2)}) collective-permute-start(f32[13,3,8,128]{3,2,1,0:T(8,128)S(1)} %get-tuple-element.10), channel_id=1, source_target_pairs={{0,128},{128,256},{256,384},{384,512},{512,640},{640,768},{768,896... | collective-permute-start | bytes 479240 | tf_op jit(solution)/shard_map/ppermute | solution.py:334
  7.8 1.9 %collective-permute-start.1 = (f32[13,3,8,128]{3,2,1,0:T(8,128)S(1)}, f32[13,3,8,128]{3,2,1,0:T(8,128)S(1)}, u32[]{:S(2)}, u32[]{:S(2)}) collective-permute-start(f32[13,3,8,128]{3,2,1,0:T(8,128)S(1)} %get-tuple-element.11.own_ref), channel_id=1, source_target_pairs={{128,0},{256,128},{384,256},{512,384},{640,512},{768,640},{896,768... | collective-permute-start | bytes 479240 | tf_op jit(solution)/shard_map/ppermute | solution.py:335
  9.7 1.4 %collective-permute-done.low_ref = f32[13,3,8,128]{3,2,1,0:T(8,128)S(1)} collective-permute-done((f32[13,3,8,128]{3,2,1,0:T(8,128)S(1)}, f32[13,3,8,128]{3,2,1,0:T(8,128)S(1)}, u32[]{:S(2)}, u32[]{:S(2)}) %collective-permute-start) | collective-permute-done | bytes 159776 | tf_op jit(solution)/shard_map/ppermute | solution.py:334
  11.2 6.9 %collective-permute-done.1.high_ref = f32[13,3,8,128]{3,2,1,0:T(8,128)S(1)} collective-permute-done((f32[13,3,8,128]{3,2,1,0:T(8,128)S(1)}, f32[13,3,8,128]{3,2,1,0:T(8,128)S(1)}, u32[]{:S(2)}, u32[]{:S(2)}) %collective-permute-start.1) | collective-permute-done | bytes 159776 | tf_op jit(solution)/shard_map/ppermute | solution.py:335
  18.0 1.0 %y_faces.1 = (f32[576,128]{1,0:T(8,128)}, f32[576,128]{1,0:T(8,128)}) custom-call(f32[768,128]{1,0:T(8,128)S(1)} %bitcast.11, f32[312,128]{1,0:T(8,128)S(1)} %bitcast.12, f32[312,128]{1,0:T(8,128)S(1)} %bitcast.13), custom_call_target="tpu_custom_call" | custom-call | tf_op jit(solution)/shard_map/y_faces/pallas_call | solution.py:348
  19.0 1.3 %collective-permute-start.2 = (f32[576,128]{1,0:T(8,128)}, f32[576,128]{1,0:T(8,128)S(1)}, u32[]{:S(2)}, u32[]{:S(2)}) collective-permute-start(f32[576,128]{1,0:T(8,128)} %get-tuple-element.12), channel_id=1, source_target_pairs={{0,8},{8,16},{16,24},{24,32},{32,40},{40,48},{48,56},{56,64},{64,7... | collective-permute-start | bytes 884744 | tf_op jit(solution)/shard_map/ppermute | solution.py:356
  20.3 0.0 copy-start
  20.3 1.4 %collective-permute-start.3 = (f32[576,128]{1,0:T(8,128)}, f32[576,128]{1,0:T(8,128)S(1)}, u32[]{:S(2)}, u32[]{:S(2)}) collective-permute-start(f32[576,128]{1,0:T(8,128)} %get-tuple-element.13), channel_id=1, source_target_pairs={{8,0},{16,8},{24,16},{32,24},{40,32},{48,40},{56,48},{64,56},{72,6... | collective-permute-start | bytes 884744 | tf_op jit(solution)/shard_map/ppermute | solution.py:357
  21.8 0.7 tiles.1
  22.5 11.8 %all-to-all-start = ((f32[16,8,128]{2,1,0:T(8,128)}), f32[16,8,128]{2,1,0:T(8,128)S(1)}, u32[]{:S(2)}, u32[]{:S(2)}) async-start(f32[16,8,128]{2,1,0:T(8,128)} %tiles.1), calls=%async_computation | async-start | bytes 131072 | tf_op jit(solution)/shard_map/all_to_all | solution.py:345
  34.3 0.1 block.1._
  34.4 7.7 %all-to-all-done.tiles_ref = f32[16,8,128]{2,1,0:T(8,128)S(1)} async-done(((f32[16,8,128]{2,1,0:T(8,128)}), f32[16,8,128]{2,1,0:T(8,128)S(1)}, u32[]{:S(2)}, u32[]{:S(2)}) %all-to-all-start) | async-done | bytes 65568 | tf_op jit(solution)/shard_map/all_to_all | solution.py:345
  42.1 0.6 surface.1.force_ref
  42.7 0.0 collective-permute-done.2.y_low_ref
  42.7 0.0 collective-permute-done.3.y_high_ref
  42.7 0.0 copy-done
  42.7 4.1 %steps.1 = (f32[3072,128]{1,0:T(8,128)S(1)}, f32[9,8,8,128]{3,2,1,0:T(8,128)}, f32[3,8,8,128]{3,2,1,0:T(8,128)S(1)}) custom-call(f32[3072,128]{1,0:T(8,128)S(1)} %block.1._, bf16[3,9,8,8,128]{4,3,2,1,0:T(8,128)(2,1)S(1)} %bitcast.14, f32[576,128]{1,0:T(8,128)S(1)} %collective-permute-done.2.y_low_ref, ...), custom_call_target="tpu_custom_call", output_to_operand_aliasing={{0}: (0, {})} | custom-call | tf_op jit(solution)/shard_map/steps/pallas_call | solution.py:378
  46.8 15.5 %all_to_all.15.parts_ref = f32[24,8,128]{2,1,0:T(8,128)S(1)} all-to-all(f32[24,8,128]{2,1,0:T(8,128)S(1)} %bitcast.15), channel_id=1, replica_groups=mesh['sx'=8,'sy'=16,'ev'=8] {'ev'}, dimensions={0} | all-to-all | bytes 196608 | tf_op jit(solution)/shard_map/all_to_all | solution.py:393
  62.3 11.1 %all_to_all.16 = f32[24,8,128]{2,1,0:T(8,128)S(1)} all-to-all(f32[24,8,128]{2,1,0:T(8,128)S(1)} %event_sum.1), channel_id=1, replica_groups=mesh['sx'=8,'sy'=16,'ev'=8] {'ev'}, dimensions={0} | all-to-all | bytes 196608 | tf_op jit(solution)/shard_map/all_to_all | solution.py:398
  73.4 0.6 copy.15
  (1 shorter events, 0.0 us)
Async XLA Ops:
  2.6 8.5 %collective-permute-start = (f32[13,3,8,128]{3,2,1,0:T(8,128)S(1)}, f32[13,3,8,128]{3,2,1,0:T(8,128)S(1)}, u32[]{:S(2)}, u32[]{:S(2)}) collective-permute-start(f32[13,3,8,128]{3,2,1,0:T(8,128)S(1)} %get-tuple-element.10), channel_id=1, source_target_pairs={{0,128},{128,256},{256,384},{384,512},{512,640},{640,768},{768,896... | collective-permute-start | bytes 479240 | tf_op jit(solution)/shard_map/ppermute | solution.py:334
  7.8 10.2 %collective-permute-start.1 = (f32[13,3,8,128]{3,2,1,0:T(8,128)S(1)}, f32[13,3,8,128]{3,2,1,0:T(8,128)S(1)}, u32[]{:S(2)}, u32[]{:S(2)}) collective-permute-start(f32[13,3,8,128]{3,2,1,0:T(8,128)S(1)} %get-tuple-element.11.own_ref), channel_id=1, source_target_pairs={{128,0},{256,128},{384,256},{512,384},{640,512},{768,640},{896,768... | collective-permute-start | bytes 479240 | tf_op jit(solution)/shard_map/ppermute | solution.py:335
  19.0 23.7 %collective-permute-start.2 = (f32[576,128]{1,0:T(8,128)}, f32[576,128]{1,0:T(8,128)S(1)}, u32[]{:S(2)}, u32[]{:S(2)}) collective-permute-start(f32[576,128]{1,0:T(8,128)} %get-tuple-element.12), channel_id=1, source_target_pairs={{0,8},{8,16},{16,24},{24,32},{32,40},{40,48},{48,56},{56,64},{64,7... | collective-permute-start | bytes 884744 | tf_op jit(solution)/shard_map/ppermute | solution.py:356
  20.3 22.4 %copy-start = (bf16[1,3,9,8,8,128]{5,4,3,2,1,0:T(8,128)(2,1)S(1)}, bf16[1,3,9,8,8,128]{5,4,3,2,1,0:T(8,128)(2,1)}, u32[]{:S(2)}) copy-start(bf16[1,3,9,8,8,128]{5,4,3,2,1,0:T(8,128)(2,1)} %param.10) | copy-start | bytes 1327108
  20.3 22.4 %collective-permute-start.3 = (f32[576,128]{1,0:T(8,128)}, f32[576,128]{1,0:T(8,128)S(1)}, u32[]{:S(2)}, u32[]{:S(2)}) collective-permute-start(f32[576,128]{1,0:T(8,128)} %get-tuple-element.13), channel_id=1, source_target_pairs={{8,0},{16,8},{24,16},{32,24},{40,32},{48,40},{56,48},{64,56},{72,6... | collective-permute-start | bytes 884744 | tf_op jit(solution)/shard_map/ppermute | solution.py:357
  22.5 19.6 %all-to-all-start = ((f32[16,8,128]{2,1,0:T(8,128)}), f32[16,8,128]{2,1,0:T(8,128)S(1)}, u32[]{:S(2)}, u32[]{:S(2)}) async-start(f32[16,8,128]{2,1,0:T(8,128)} %tiles.1), calls=%async_computation | async-start | bytes 131072 | tf_op jit(solution)/shard_map/all_to_all | solution.py:345

commit v4 on v3

--- a/solution.py
+++ b/solution.py
@@ -15,6 +15,16 @@
 YR = 16
 FIELDS = 12
 PLANE = XS * YR
+X_HIGH = (2, 3, 3, 3, 3, 3, 3, 3, 3, 3, 2, 2)
+X_LOW = (3, 2, 2, 3, 2, 2, 3, 3, 2, 3, 2, 2)
+Y_HIGH = (3, 2, 3, 3, 3, 3, 3, 3, 3, 3, 2, 2)
+Y_LOW = (2, 3, 2, 2, 3, 2, 3, 2, 3, 3, 2, 2)
+
+
+def starts(counts):
+    return [sum(counts[:f]) for f in range(len(counts) + 1)]
+
+
 DEAD = -1.0e6
 MIB = 1 << 20
 VMEM = pl.BlockSpec(memory_space=pltpu.VMEM)
@@ -46,11 +56,11 @@
         for i, (source, target) in enumerate(((block_hbm, block_ref), (cell_hbm, cell_ref), (trace_hbm, trace_ref)))
     ]
     copies = []
-    for side, (out, first) in enumerate(((low_ref, 0), (high_ref, B - W))):
-        pieces = [(adj_hbm.at[:, pl.ds(first, W)], out.at[pl.ds(0, 9)])]
-        pieces += [(p.at[pl.ds(first, W)], out.at[9 + i]) for i, p in enumerate(params)]
-        for i, (source, target) in enumerate(pieces):
-            copies.append(pltpu.make_async_copy(source, target, sems.at[side, i]))
+    for side, (out, counts) in enumerate(((low_ref, X_HIGH), (high_ref, X_LOW))):
+        for f, (at, count) in enumerate(zip(starts(counts), counts)):
+            planes = pl.ds(B - count if side else 0, count)
+            source = adj_hbm.at[f, planes] if f < 9 else params[f - 9].at[planes]
+            copies.append(pltpu.make_async_copy(source, out.at[pl.ds(at, count)], sems.at[side, f]))
     copies.append(pltpu.make_async_copy(adj_hbm, base_ref.at[pl.ds(0, 9)], sems.at[2, 0]))
     for i, p in enumerate(params):
         copies.append(pltpu.make_async_copy(p, base_ref.at[9 + i], sems.at[2, 1 + i]))
@@ -68,10 +78,8 @@
         [jnp.concatenate(parts[:8], axis=0), jnp.concatenate(parts[8:], axis=0), jnp.zeros((8, 128 - 2 * rows), jnp.float32)],
         axis=1,
     )
-    for out in (low_ref, high_ref):
-        out[FIELDS, 0] = pack
-        for spare in range(1, W):
-            out[FIELDS, spare] = jnp.zeros((8, 128), jnp.float32)
+    low_ref[sum(X_HIGH)] = pack
+    high_ref[sum(X_LOW)] = pack
     for copy in copies:
         copy.wait()
 
@@ -81,7 +89,7 @@
     group = lax.broadcasted_iota(jnp.int32, (8, 128), 1) // 32
     tile = jnp.zeros((8, 128), jnp.float32)
     for s, (ref, shift) in enumerate(((own_ref, W), (low_ref, W - B), (high_ref, W + B))):
-        pack = ref[FIELDS, 0]
+        pack = ref[ref.shape[0] - 1]
         head = jnp.where(row == 0, pack + float(shift * ny), pack)
         head = pltpu.roll(head, 32 * s, 1) if s else head
         tail = pltpu.roll(pack, 64, 1)
@@ -93,15 +101,20 @@
 
 
 def y_faces_kernel(base_ref, low_ref, high_ref, face_low_ref, face_high_ref):
-    for out, first in ((face_low_ref, 0), (face_high_ref, B - W)):
-        for f in range(FIELDS):
-            for r in range(W):
-                y = first + r
-                at = (r * FIELDS + f) * YR
-                out[pl.ds(at, W), :] = low_ref[pl.ds(f * 24 + y, W, stride=8), :]
-                out[pl.ds(at + W, B), :] = base_ref[pl.ds(f * 64 + y, B, stride=8), :]
-                out[pl.ds(at + W + B, W), :] = high_ref[pl.ds(f * 24 + y, W, stride=8), :]
-                out[pl.ds(at + XE, YR - XE), :] = jnp.zeros((YR - XE, 128), jnp.float32)
+    x_low, x_high = starts(X_LOW), starts(X_HIGH)
+    for side, (out, counts) in enumerate(((face_low_ref, Y_HIGH), (face_high_ref, Y_LOW))):
+        for f, (at, count) in enumerate(zip(starts(counts), counts)):
+            for r in range(count):
+                y = B - count + r if side else r
+                row = (at + r) * XE
+                below, above = X_LOW[f], X_HIGH[f]
+                if below < W:
+                    out[pl.ds(row, W - below), :] = jnp.zeros((W - below, 128), jnp.float32)
+                out[pl.ds(row + W - below, below), :] = low_ref[pl.ds(x_low[f] * 8 + y, below, stride=8), :]
+                out[pl.ds(row + W, B), :] = base_ref[pl.ds(f * 64 + y, B, stride=8), :]
+                out[pl.ds(row + W + B, above), :] = high_ref[pl.ds(x_high[f] * 8 + y, above, stride=8), :]
+                if above < W:
+                    out[pl.ds(row + W + B + above, W - above), :] = jnp.zeros((W - above, 128), jnp.float32)
 
 
 def surface_kernel(ny, place_ref, tiles_ref, surface_ref):
@@ -136,24 +149,26 @@
 
 def block_kernel(base_ref, low_ref, high_ref, ext):
     zero8 = jnp.zeros((8, 128), jnp.float32)
+    x_low, x_high = starts(X_LOW), starts(X_HIGH)
     for f in range(FIELDS):
         for e in range(XS):
-            at = f * PLANE + e * YR
-            if e == 0 or e == XS - 1:
-                ext[pl.ds(at, 8), :] = zero8
-            elif e <= W:
-                ext[pl.ds(at, 8), :] = low_ref[f, e - 1]
-            elif e <= W + B:
-                ext[pl.ds(at, 8), :] = base_ref[f, e - 1 - W]
+            x = e - 1 - W
+            if 0 <= x < B:
+                plane = base_ref[f, x]
+            elif -X_LOW[f] <= x < 0:
+                plane = low_ref[x_low[f] + X_LOW[f] + x]
+            elif B <= x < B + X_HIGH[f]:
+                plane = high_ref[x_high[f] + x - B]
             else:
-                ext[pl.ds(at, 8), :] = high_ref[f, e - 1 - W - B]
-            ext[pl.ds(at + 8, 8), :] = zero8
+                plane = zero8
+            ext[pl.ds(f * PLANE + e * YR, 8), :] = plane
+            ext[pl.ds(f * PLANE + e * YR + 8, 8), :] = zero8
 
 
 def steps_kernel(
     steps,
     _,
-    forward_ref,
+    forward_hbm,
     y_low_ref,
     y_high_ref,
     force_ref,
@@ -162,13 +177,18 @@
     kernels_ref,
     change_ref,
     rate_ref,
+    forward_ref,
     sem,
+    load_sem,
 ):
-    for f in range(FIELDS):
-        for r in range(W):
-            src = (r * FIELDS + f) * YR
-            ext[pl.ds(f * PLANE + YR + 8 + r, XE, stride=YR), :] = y_high_ref[pl.ds(src, XE), :]
-            ext[pl.ds(f * PLANE + YR + 13 + r, XE, stride=YR), :] = y_low_ref[pl.ds(src, XE), :]
+    loads = [pltpu.make_async_copy(forward_hbm.at[t], forward_ref.at[t], load_sem.at[t]) for t in range(steps)]
+    for load in loads:
+        load.start()
+    for ref, counts, first in ((y_high_ref, Y_HIGH, 8), (y_low_ref, Y_LOW, YR)):
+        for f, (at, count) in enumerate(zip(starts(counts), counts)):
+            for r in range(count):
+                row = f * PLANE + YR + (first + r if first == 8 else first - count + r)
+                ext[pl.ds(row, XE, stride=YR), :] = ref[pl.ds((at + r) * XE, XE), :]
 
     lanes = lax.broadcasted_iota(jnp.int32, (YR, 128), 1)
 
@@ -243,6 +263,8 @@
             ]
             for copy in copies:
                 copy.start()
+
+        loads[step].wait()
 
         def sensitivities(x, carry):
             e = x + 1 + W
@@ -310,14 +332,14 @@
     rows = station_cell.shape[1]
     low_face, high_face, base = pl.pallas_call(
         functools.partial(x_faces_kernel, ny),
-        out_shape=[f32(FIELDS + 1, W, 8, 128)] * 2 + [f32(FIELDS, B, 8, 128)],
+        out_shape=[f32(sum(X_HIGH) + 1, 8, 128), f32(sum(X_LOW) + 1, 8, 128), f32(FIELDS, B, 8, 128)],
         in_specs=[HBM] * 4 + [SMEM] + [HBM] * 3,
         out_specs=[VMEM] * 3,
         scratch_shapes=[
             pltpu.VMEM((1, rows), jnp.int32),
             pltpu.VMEM((1, rows), jnp.int32),
             pltpu.VMEM((9, 1, rows), jnp.float32),
-            pltpu.SemaphoreType.DMA((4, 4)),
+            pltpu.SemaphoreType.DMA((4, FIELDS)),
         ],
         compiler_params=pltpu.CompilerParams(vmem_limit_bytes=3 * MIB),
         name="x_faces",
@@ -347,7 +369,7 @@
     flat = lambda a: a.reshape(-1, 128)
     y_low_face, y_high_face = pl.pallas_call(
         y_faces_kernel,
-        out_shape=[f32(W * FIELDS * YR, 128)] * 2,
+        out_shape=[f32(-(-XE * sum(c) // 8) * 8, 128) for c in (Y_HIGH, Y_LOW)],
         in_specs=[VMEM] * 3,
         out_specs=[VMEM] * 2,
         compiler_params=pltpu.CompilerParams(vmem_limit_bytes=4 * MIB),
@@ -378,17 +400,19 @@
     _, state, kernels = pl.pallas_call(
         functools.partial(steps_kernel, steps),
         out_shape=[f32(FIELDS * PLANE, 128), f32(9, B, 8, 128), f32(3, B, 8, 128)],
-        in_specs=[VMEM] * 5,
+        in_specs=[VMEM, HBM, VMEM, VMEM, VMEM],
         out_specs=[VMEM, HBM, VMEM],
         input_output_aliases={0: 0},
         scratch_shapes=[
             pltpu.VMEM((3, XS, 8, 128), jnp.float32),
             pltpu.VMEM((6, XS, 8, 128), jnp.float32),
+            pltpu.VMEM(forward_state.shape[1:], forward_state.dtype),
             pltpu.SemaphoreType.DMA((9,)),
+            pltpu.SemaphoreType.DMA((steps,)),
         ],
         compiler_params=pltpu.CompilerParams(vmem_limit_bytes=8 * MIB),
         name="steps",
-    )(ext, forward_state[0], y_low, y_high, surface)
+    )(ext, in_hbm(forward_state[0]), y_low, y_high, surface)
 
     parts = lax.all_to_all(kernels.reshape(3 * B, 8, 128), "ev", split_axis=0, concat_axis=0, tiled=True)
     shared = pl.pallas_call(

time: 74.4 us -> 67.8 us (0.911)
  the two profiles are of different devices: /device:TPU:256 before, /device:TPU:128 now
where the time goes in v4:
time: 67.8 us; the launch traced here: 67.5 us
  starting transfers between devices  23 us (34%)
  blocking collectives  22.6 us (33%)
  waiting for transfers between devices  12.5 us (18%)
  Pallas kernels  7.26 us (11%)
  between operations  1.38 us (2%)
    ppermute x1, starting transfers between devices, on_device(): high = lax.ppermute(low_face, 'sx', down_x)  13.3 us
    all_to_all x1, blocking collectives, on_device(): lax.all_to_all(kernels.reshape(3 * B, 8, 128), 'ev', split_axis=0, concat...  11.5 us
    all_to_all x1, blocking collectives, on_device(): lax.all_to_all(shared, 'ev', split_axis=0, concat_axis=0, tiled=True)  11.1 us
    all_to_all x1, waiting for transfers between devices, on_device(): tiles = lax.all_to_all(tiles, 'sy', split_axis=0, concat_axis=0, tiled=True)  7.65 us
    ppermute x1, waiting for transfers between devices, on_device(): low = lax.ppermute(high_face, 'sx', up_x)  4.85 us
    pallas_call x1, Pallas kernels, on_device(): pl.pallas_call(functools.partial(steps_kernel, steps), out_shape=[f32(FIE...  4.12 us
    all_to_all x1, starting transfers between devices, on_device(): tiles = lax.all_to_all(tiles, 'sy', split_axis=0, concat_axis=0, tiled=True)  3.5 us
    ppermute x1, starting transfers between devices, on_device(): y_low = lax.ppermute(y_high_face, 'sy', up_y)  3.04 us
  transfers between devices with their start and end apart: 5, of which 2 were waited for; matrix products, arithmetic and copies ran while one was open for 0% of the time, Pallas kernels for 2%

profile of v4, /device:TPU:128, one launch (start us, length us, event | category | flops | bytes accessed | tf_op | source)
XLA Modules:
  0.0 67.5 jit_solution(1132492049556395637)
XLA Ops:
  1.3 1.6 %x_faces.1 = (f32[34,8,128]{2,1,0:T(8,128)S(1)}, f32[30,8,128]{2,1,0:T(8,128)S(1)}, f32[12,8,8,128]{3,2,1,0:T(8,128)S(1)}) custom-call(f32[9,8,8,128]{3,2,1,0:T(8,128)} %bitcast.17, f32[8,8,128]{2,1,0:T(8,128)} %rho_hbm.1, f32[8,8,128]{2,1,0:T(8,128)} %lam_hbm.1, f32[8,8,128]{2,1,0:T(8,128)} %mu_hbm.1, s32[1,1]{1,0:T(1,128)S(6)} %copy.14.count_ref, ...), custom_call_target="tpu_custom_call" | custom-call | tf_op jit(solution)/shard_map/x_faces/pallas_call | solution.py:333
  2.9 13.3 %collective-permute-start.1 = (f32[34,8,128]{2,1,0:T(8,128)S(1)}, f32[34,8,128]{2,1,0:T(8,128)S(1)}, u32[]{:S(2)}, u32[]{:S(2)}) collective-permute-start(f32[34,8,128]{2,1,0:T(8,128)S(1)} %get-tuple-element.11.own_ref), channel_id=1, source_target_pairs={{128,0},{256,128},{384,256},{512,384},{640,512},{768,640},{896,768... | collective-permute-start | bytes 417800 | tf_op jit(solution)/shard_map/ppermute | solution.py:357
  16.2 1.9 %collective-permute-start = (f32[30,8,128]{2,1,0:T(8,128)S(1)}, f32[30,8,128]{2,1,0:T(8,128)S(1)}, u32[]{:S(2)}, u32[]{:S(2)}) collective-permute-start(f32[30,8,128]{2,1,0:T(8,128)S(1)} %get-tuple-element.10), channel_id=1, source_target_pairs={{0,128},{128,256},{256,384},{384,512},{512,640},{640,768},{768,896... | collective-permute-start | bytes 368648 | tf_op jit(solution)/shard_map/ppermute | solution.py:356
  18.1 4.8 %collective-permute-done.low_ref = f32[30,8,128]{2,1,0:T(8,128)S(1)} collective-permute-done((f32[30,8,128]{2,1,0:T(8,128)S(1)}, f32[30,8,128]{2,1,0:T(8,128)S(1)}, u32[]{:S(2)}, u32[]{:S(2)}) %collective-permute-start) | collective-permute-done | bytes 122912 | tf_op jit(solution)/shard_map/ppermute | solution.py:356
  23.0 0.0 collective-permute-done.1.high_ref
  23.0 0.1 y_faces.1
  23.1 1.3 %collective-permute-start.3 = (f32[464,128]{1,0:T(8,128)S(1)}, f32[464,128]{1,0:T(8,128)S(1)}, u32[]{:S(2)}, u32[]{:S(2)}) collective-permute-start(f32[464,128]{1,0:T(8,128)S(1)} %get-tuple-element.13), channel_id=1, source_target_pairs={{8,0},{16,8},{24,16},{32,24},{40,32},{48,40},{56,48},{64,56},{72,6... | collective-permute-start | bytes 712712 | tf_op jit(solution)/shard_map/ppermute | solution.py:379
  24.4 3.0 %collective-permute-start.2 = (f32[408,128]{1,0:T(8,128)S(1)}, f32[408,128]{1,0:T(8,128)S(1)}, u32[]{:S(2)}, u32[]{:S(2)}) collective-permute-start(f32[408,128]{1,0:T(8,128)S(1)} %get-tuple-element.12), channel_id=1, source_target_pairs={{0,8},{8,16},{16,24},{24,32},{32,40},{40,48},{48,56},{56,64},{64,7... | collective-permute-start | bytes 626696 | tf_op jit(solution)/shard_map/ppermute | solution.py:378
  27.4 0.7 %tiles.1 = f32[16,8,128]{2,1,0:T(8,128)} custom-call(f32[34,8,128]{2,1,0:T(8,128)S(1)} %get-tuple-element.11.own_ref, f32[30,8,128]{2,1,0:T(8,128)S(1)} %collective-permute-done.low_ref, f32[34,8,128]{2,1,0:T(8,128)S(1)} %collective-permute-done.1.high_ref), custom_call_target="tpu_custom_call" | custom-call | tf_op jit(solution)/shard_map/tiles/pallas_call | solution.py:359
  28.1 3.5 %all-to-all-start = ((f32[16,8,128]{2,1,0:T(8,128)}), f32[16,8,128]{2,1,0:T(8,128)S(1)}, u32[]{:S(2)}, u32[]{:S(2)}) async-start(f32[16,8,128]{2,1,0:T(8,128)} %tiles.1), calls=%async_computation | async-start | bytes 131072 | tf_op jit(solution)/shard_map/all_to_all | solution.py:367
  31.7 0.1 block.1._
  31.8 7.7 %all-to-all-done.tiles_ref = f32[16,8,128]{2,1,0:T(8,128)S(1)} async-done(((f32[16,8,128]{2,1,0:T(8,128)}), f32[16,8,128]{2,1,0:T(8,128)S(1)}, u32[]{:S(2)}, u32[]{:S(2)}) %all-to-all-start) | async-done | bytes 65568 | tf_op jit(solution)/shard_map/all_to_all | solution.py:367
  39.4 0.6 surface.1.force_ref
  40.0 0.0 collective-permute-done.2.y_low_ref
  40.0 0.0 collective-permute-done.3.y_high_ref
  40.0 4.1 %steps.1 = (f32[3072,128]{1,0:T(8,128)S(1)}, f32[9,8,8,128]{3,2,1,0:T(8,128)}, f32[3,8,8,128]{3,2,1,0:T(8,128)S(1)}) custom-call(f32[3072,128]{1,0:T(8,128)S(1)} %block.1._, bf16[3,9,8,8,128]{4,3,2,1,0:T(8,128)(2,1)} %bitcast.15, f32[408,128]{1,0:T(8,128)S(1)} %collective-permute-done.2.y_low_ref, ...), custom_call_target="tpu_custom_call", output_to_operand_aliasing={{0}: (0, {})} | custom-call | tf_op jit(solution)/shard_map/steps/pallas_call | solution.py:400
  44.2 11.5 %all_to_all.15.parts_ref = f32[24,8,128]{2,1,0:T(8,128)S(1)} all-to-all(f32[24,8,128]{2,1,0:T(8,128)S(1)} %bitcast.14), channel_id=1, replica_groups=mesh['sx'=8,'sy'=16,'ev'=8] {'ev'}, dimensions={0} | all-to-all | bytes 196608 | tf_op jit(solution)/shard_map/all_to_all | solution.py:417
  55.7 11.1 %all_to_all.16 = f32[24,8,128]{2,1,0:T(8,128)S(1)} all-to-all(f32[24,8,128]{2,1,0:T(8,128)S(1)} %event_sum.1), channel_id=1, replica_groups=mesh['sx'=8,'sy'=16,'ev'=8] {'ev'}, dimensions={0} | all-to-all | bytes 196608 | tf_op jit(solution)/shard_map/all_to_all | solution.py:422
  66.8 0.6 copy.15
  (1 shorter events, 0.0 us)
Async XLA Ops:
  2.9 20.1 %collective-permute-start.1 = (f32[34,8,128]{2,1,0:T(8,128)S(1)}, f32[34,8,128]{2,1,0:T(8,128)S(1)}, u32[]{:S(2)}, u32[]{:S(2)}) collective-permute-start(f32[34,8,128]{2,1,0:T(8,128)S(1)} %get-tuple-element.11.own_ref), channel_id=1, source_target_pairs={{128,0},{256,128},{384,256},{512,384},{640,512},{768,640},{896,768... | collective-permute-start | bytes 417800 | tf_op jit(solution)/shard_map/ppermute | solution.py:357
  16.2 6.8 %collective-permute-start = (f32[30,8,128]{2,1,0:T(8,128)S(1)}, f32[30,8,128]{2,1,0:T(8,128)S(1)}, u32[]{:S(2)}, u32[]{:S(2)}) collective-permute-start(f32[30,8,128]{2,1,0:T(8,128)S(1)} %get-tuple-element.10), channel_id=1, source_target_pairs={{0,128},{128,256},{256,384},{384,512},{512,640},{640,768},{768,896... | collective-permute-start | bytes 368648 | tf_op jit(solution)/shard_map/ppermute | solution.py:356
  23.1 16.9 %collective-permute-start.3 = (f32[464,128]{1,0:T(8,128)S(1)}, f32[464,128]{1,0:T(8,128)S(1)}, u32[]{:S(2)}, u32[]{:S(2)}) collective-permute-start(f32[464,128]{1,0:T(8,128)S(1)} %get-tuple-element.13), channel_id=1, source_target_pairs={{8,0},{16,8},{24,16},{32,24},{40,32},{48,40},{56,48},{64,56},{72,6... | collective-permute-start | bytes 712712 | tf_op jit(solution)/shard_map/ppermute | solution.py:379
  24.4 15.6 %collective-permute-start.2 = (f32[408,128]{1,0:T(8,128)S(1)}, f32[408,128]{1,0:T(8,128)S(1)}, u32[]{:S(2)}, u32[]{:S(2)}) collective-permute-start(f32[408,128]{1,0:T(8,128)S(1)} %get-tuple-element.12), channel_id=1, source_target_pairs={{0,8},{8,16},{16,24},{24,32},{32,40},{40,48},{48,56},{56,64},{64,7... | collective-permute-start | bytes 626696 | tf_op jit(solution)/shard_map/ppermute | solution.py:378
  28.1 11.3 %all-to-all-start = ((f32[16,8,128]{2,1,0:T(8,128)}), f32[16,8,128]{2,1,0:T(8,128)S(1)}, u32[]{:S(2)}, u32[]{:S(2)}) async-start(f32[16,8,128]{2,1,0:T(8,128)} %tiles.1), calls=%async_computation | async-start | bytes 131072 | tf_op jit(solution)/shard_map/all_to_all | solution.py:367

commit v5 on v4

--- a/solution.py
+++ b/solution.py
@@ -21,6 +21,9 @@
 Y_LOW = (2, 3, 2, 2, 3, 2, 3, 2, 3, 3, 2, 2)
 
 
+PLANES = max(sum(X_HIGH), sum(X_LOW)) + 1
+
+
 def starts(counts):
     return [sum(counts[:f]) for f in range(len(counts) + 1)]
 
@@ -34,6 +37,7 @@
 
 def x_faces_kernel(
     ny,
+    odd_ref,
     adj_hbm,
     rho_hbm,
     lam_hbm,
@@ -42,8 +46,8 @@
     block_hbm,
     cell_hbm,
     trace_hbm,
-    low_ref,
-    high_ref,
+    first_ref,
+    second_ref,
     base_ref,
     block_ref,
     cell_ref,
@@ -55,16 +59,33 @@
         pltpu.make_async_copy(source, target, sems.at[3, i])
         for i, (source, target) in enumerate(((block_hbm, block_ref), (cell_hbm, cell_ref), (trace_hbm, trace_ref)))
     ]
-    copies = []
-    for side, (out, counts) in enumerate(((low_ref, X_HIGH), (high_ref, X_LOW))):
-        for f, (at, count) in enumerate(zip(starts(counts), counts)):
-            planes = pl.ds(B - count if side else 0, count)
-            source = adj_hbm.at[f, planes] if f < 9 else params[f - 9].at[planes]
-            copies.append(pltpu.make_async_copy(source, out.at[pl.ds(at, count)], sems.at[side, f]))
-    copies.append(pltpu.make_async_copy(adj_hbm, base_ref.at[pl.ds(0, 9)], sems.at[2, 0]))
+
+    def faces(low_ref, high_ref):
+        copies = []
+        for side, (out, counts) in enumerate(((low_ref, X_HIGH), (high_ref, X_LOW))):
+            for f, (at, count) in enumerate(zip(starts(counts), counts)):
+                planes = pl.ds(B - count if side else 0, count)
+                source = adj_hbm.at[f, planes] if f < 9 else params[f - 9].at[planes]
+                copies.append(pltpu.make_async_copy(source, out.at[pl.ds(at, count)], sems.at[side, f]))
+        return copies
+
+    own = [pltpu.make_async_copy(adj_hbm, base_ref.at[pl.ds(0, 9)], sems.at[2, 0])]
     for i, p in enumerate(params):
-        copies.append(pltpu.make_async_copy(p, base_ref.at[9 + i], sems.at[2, 1 + i]))
-    for copy in rows_in + copies:
+        own.append(pltpu.make_async_copy(p, base_ref.at[9 + i], sems.at[2, 1 + i]))
+    for copy in rows_in:
+        copy.start()
+
+    @pl.when(odd_ref[0] == 0)
+    def _():
+        for copy in faces(second_ref, first_ref):
+            copy.start()
+
+    @pl.when(odd_ref[0] == 1)
+    def _():
+        for copy in faces(first_ref, second_ref):
+            copy.start()
+
+    for copy in own:
         copy.start()
     for copy in rows_in:
         copy.wait()
@@ -78,18 +99,41 @@
         [jnp.concatenate(parts[:8], axis=0), jnp.concatenate(parts[8:], axis=0), jnp.zeros((8, 128 - 2 * rows), jnp.float32)],
         axis=1,
     )
-    low_ref[sum(X_HIGH)] = pack
-    high_ref[sum(X_LOW)] = pack
-    for copy in copies:
+    first_ref[PLANES - 1] = pack
+    second_ref[PLANES - 1] = pack
+
+    @pl.when(odd_ref[0] == 0)
+    def _():
+        for copy in faces(second_ref, first_ref):
+            copy.wait()
+
+    @pl.when(odd_ref[0] == 1)
+    def _():
+        for copy in faces(first_ref, second_ref):
+            copy.wait()
+
+    for copy in own:
         copy.wait()
 
 
-def tiles_kernel(ny, own_ref, low_ref, high_ref, tiles_ref):
+def by_side(odd_ref, first_ref, second_ref, body):
+    @pl.when(odd_ref[0] == 0)
+    def _():
+        body(second_ref, first_ref)
+
+    @pl.when(odd_ref[0] == 1)
+    def _():
+        body(first_ref, second_ref)
+
+
+def tiles_kernel(ny, odd_ref, own_ref, first_ref, second_ref, tiles_ref):
     row = lax.broadcasted_iota(jnp.int32, (8, 128), 0)
     group = lax.broadcasted_iota(jnp.int32, (8, 128), 1) // 32
     tile = jnp.zeros((8, 128), jnp.float32)
-    for s, (ref, shift) in enumerate(((own_ref, W), (low_ref, W - B), (high_ref, W + B))):
-        pack = ref[ref.shape[0] - 1]
+    even = odd_ref[0] == 0
+    one, two = first_ref[PLANES - 1], second_ref[PLANES - 1]
+    packs = (own_ref[PLANES - 1], jnp.where(even, two, one), jnp.where(even, one, two))
+    for s, (pack, shift) in enumerate(zip(packs, (W, W - B, W + B))):
         head = jnp.where(row == 0, pack + float(shift * ny), pack)
         head = pltpu.roll(head, 32 * s, 1) if s else head
         tail = pltpu.roll(pack, 64, 1)
@@ -100,7 +144,11 @@
         tiles_ref[d] = tile
 
 
-def y_faces_kernel(base_ref, low_ref, high_ref, face_low_ref, face_high_ref):
+def y_faces_kernel(odd_ref, base_ref, first_ref, second_ref, face_low_ref, face_high_ref):
+    by_side(odd_ref, first_ref, second_ref, functools.partial(y_faces, base_ref, face_low_ref, face_high_ref))
+
+
+def y_faces(base_ref, face_low_ref, face_high_ref, low_ref, high_ref):
     x_low, x_high = starts(X_LOW), starts(X_HIGH)
     for side, (out, counts) in enumerate(((face_low_ref, Y_HIGH), (face_high_ref, Y_LOW))):
         for f, (at, count) in enumerate(zip(starts(counts), counts)):
@@ -147,7 +195,11 @@
         )
 
 
-def block_kernel(base_ref, low_ref, high_ref, ext):
+def block_kernel(odd_ref, base_ref, first_ref, second_ref, ext):
+    by_side(odd_ref, first_ref, second_ref, functools.partial(extend, base_ref, ext))
+
+
+def extend(base_ref, ext, low_ref, high_ref):
     zero8 = jnp.zeros((8, 128), jnp.float32)
     x_low, x_high = starts(X_LOW), starts(X_HIGH)
     for f in range(FIELDS):
@@ -305,6 +357,11 @@
     return jax.ShapeDtypeStruct(shape, jnp.float32)
 
 
+def swaps(start, count):
+    pairs = [(i, i + 1) for i in range(start, count - 1, 2)]
+    return pairs + [(b, a) for a, b in pairs]
+
+
 def in_hbm(a):
     return pltpu.with_memory_space_constraint(a, pltpu.HBM)
 
@@ -324,16 +381,15 @@
     steps = forward_state.shape[1]
     ny = n_sy * B
     adj = adjoint_state[0]
-    up_x = [(i, i + 1) for i in range(n_sx - 1)]
     up_y = [(i, i + 1) for i in range(n_sy - 1)]
-    down_x = [(b, a) for a, b in up_x]
     down_y = [(b, a) for a, b in up_y]
 
     rows = station_cell.shape[1]
-    low_face, high_face, base = pl.pallas_call(
+    odd = (lax.axis_index("sx") & 1).astype(jnp.int32).reshape(1)
+    first_face, second_face, base = pl.pallas_call(
         functools.partial(x_faces_kernel, ny),
-        out_shape=[f32(sum(X_HIGH) + 1, 8, 128), f32(sum(X_LOW) + 1, 8, 128), f32(FIELDS, B, 8, 128)],
-        in_specs=[HBM] * 4 + [SMEM] + [HBM] * 3,
+        out_shape=[f32(PLANES, 8, 128)] * 2 + [f32(FIELDS, B, 8, 128)],
+        in_specs=[SMEM] + [HBM] * 4 + [SMEM] + [HBM] * 3,
         out_specs=[VMEM] * 3,
         scratch_shapes=[
             pltpu.VMEM((1, rows), jnp.int32),
@@ -344,6 +400,7 @@
         compiler_params=pltpu.CompilerParams(vmem_limit_bytes=3 * MIB),
         name="x_faces",
     )(
+        odd,
         in_hbm(adj),
         in_hbm(inv_density),
         in_hbm(lame_lambda),
@@ -353,28 +410,28 @@
         in_hbm(station_cell),
         in_hbm(jnp.transpose(station_trace, (2, 0, 1))),
     )
-    low = lax.ppermute(high_face, "sx", up_x)
-    high = lax.ppermute(low_face, "sx", down_x)
+    first = lax.ppermute(first_face, "sx", swaps(0, n_sx))
+    second = lax.ppermute(second_face, "sx", swaps(1, n_sx))
 
     tiles = pl.pallas_call(
         functools.partial(tiles_kernel, ny),
         out_shape=f32(n_sy, 8, 128),
-        in_specs=[VMEM] * 3,
+        in_specs=[SMEM] + [VMEM] * 3,
         out_specs=VMEM,
         compiler_params=pltpu.CompilerParams(vmem_limit_bytes=2 * MIB),
         name="tiles",
-    )(low_face, low, high)
+    )(odd, first_face, first, second)
     tiles = lax.all_to_all(tiles, "sy", split_axis=0, concat_axis=0, tiled=True)
 
     flat = lambda a: a.reshape(-1, 128)
     y_low_face, y_high_face = pl.pallas_call(
         y_faces_kernel,
         out_shape=[f32(-(-XE * sum(c) // 8) * 8, 128) for c in (Y_HIGH, Y_LOW)],
-        in_specs=[VMEM] * 3,
+        in_specs=[SMEM] + [VMEM] * 3,
         out_specs=[VMEM] * 2,
         compiler_params=pltpu.CompilerParams(vmem_limit_bytes=4 * MIB),
         name="y_faces",
-    )(flat(base), flat(low), flat(high))
+    )(odd, flat(base), flat(first), flat(second))
     y_low = lax.ppermute(y_high_face, "sy", up_y)
     y_high = lax.ppermute(y_low_face, "sy", down_y)
 
@@ -391,11 +448,11 @@
     ext = pl.pallas_call(
         block_kernel,
         out_shape=f32(FIELDS * PLANE, 128),
-        in_specs=[VMEM] * 3,
+        in_specs=[SMEM] + [VMEM] * 3,
         out_specs=VMEM,
         compiler_params=pltpu.CompilerParams(vmem_limit_bytes=4 * MIB),
         name="block",
-    )(base, low, high)
+    )(odd, base, first, second)
 
     _, state, kernels = pl.pallas_call(
         functools.partial(steps_kernel, steps),

time: 67.8 us -> 70.9 us (1.046)
  the two profiles are of different devices: /device:TPU:128 before, /device:TPU:256 now
where the time goes in v5:
time: 70.9 us; the launch traced here: 70.5 us
  blocking collectives  26.6 us (38%)
  starting transfers between devices  23.6 us (33%)
  waiting for transfers between devices  11 us (16%)
  Pallas kernels  7.3 us (10%)
  between operations  1.4 us (2%)
    all_to_all x1, blocking collectives, on_device(): lax.all_to_all(kernels.reshape(3 * B, 8, 128), 'ev', split_axis=0, concat...  15.5 us
    all_to_all x1, blocking collectives, on_device(): lax.all_to_all(shared, 'ev', split_axis=0, concat_axis=0, tiled=True)  11.1 us
    ppermute x1, starting transfers between devices, on_device(): first = lax.ppermute(first_face, 'sx', swaps(0, n_sx))  9.67 us
    all_to_all x1, starting transfers between devices, on_device(): tiles = lax.all_to_all(tiles, 'sy', split_axis=0, concat_axis=0, tiled=True)  7.66 us
    all_to_all x1, waiting for transfers between devices, on_device(): tiles = lax.all_to_all(tiles, 'sy', split_axis=0, concat_axis=0, tiled=True)  7.66 us
    pallas_call x1, Pallas kernels, on_device(): pl.pallas_call(functools.partial(steps_kernel, steps), out_shape=[f32(FIE...  4.12 us
    ppermute x1, waiting for transfers between devices, on_device(): first = lax.ppermute(first_face, 'sx', swaps(0, n_sx))  3.37 us
    ppermute x1, starting transfers between devices, on_device(): y_low = lax.ppermute(y_high_face, 'sy', up_y)  3.04 us
  transfers between devices with their start and end apart: 5, of which 2 were waited for; matrix products, arithmetic and copies ran while one was open for 0% of the time, Pallas kernels for 2%

profile of v5, /device:TPU:256, one launch (start us, length us, event | category | flops | bytes accessed | tf_op | source)
XLA Modules:
  0.0 70.5 jit_solution(8980319642202846683)
XLA Ops:
  1.3 1.6 %x_faces.1 = (f32[34,8,128]{2,1,0:T(8,128)S(1)}, f32[34,8,128]{2,1,0:T(8,128)S(1)}, f32[12,8,8,128]{3,2,1,0:T(8,128)S(1)}) custom-call(s32[1]{0:T(128)} %bitcast.odd_ref, f32[9,8,8,128]{3,2,1,0:T(8,128)} %bitcast.18, f32[8,8,128]{2,1,0:T(8,128)} %rho_hbm.1, f32[8,8,128]{2,1,0:T(8,128)} %lam_hbm.1, f32[8,8,128]{2,1,0:T(8,128)} %mu_hbm.1, ...), custom_call_target="tpu_custom_call" | custom-call | tf_op jit(solution)/shard_map/x_faces/pallas_call | solution.py:389
  2.9 1.9 %collective-permute-start.1 = (f32[34,8,128]{2,1,0:T(8,128)S(1)}, f32[34,8,128]{2,1,0:T(8,128)S(1)}, u32[]{:S(2)}, u32[]{:S(2)}) collective-permute-start(f32[34,8,128]{2,1,0:T(8,128)S(1)} %get-tuple-element.11), channel_id=1, source_target_pairs={{128,256},{384,512},{640,768},{256,128},{512,384},{768,640},{129,2... | collective-permute-start | bytes 417800 | tf_op jit(solution)/shard_map/ppermute | solution.py:414
  4.8 9.7 %collective-permute-start = (f32[34,8,128]{2,1,0:T(8,128)S(1)}, f32[34,8,128]{2,1,0:T(8,128)S(1)}, u32[]{:S(2)}, u32[]{:S(2)}) collective-permute-start(f32[34,8,128]{2,1,0:T(8,128)S(1)} %get-tuple-element.10.own_ref), channel_id=1, source_target_pairs={{0,128},{256,384},{512,640},{768,896},{128,0},{384,256},{640,512},... | collective-permute-start | bytes 417800 | tf_op jit(solution)/shard_map/ppermute | solution.py:413
  14.5 0.0 collective-permute-done.1.second_ref
  14.5 3.4 %collective-permute-done.first_ref = f32[34,8,128]{2,1,0:T(8,128)S(1)} collective-permute-done((f32[34,8,128]{2,1,0:T(8,128)S(1)}, f32[34,8,128]{2,1,0:T(8,128)S(1)}, u32[]{:S(2)}, u32[]{:S(2)}) %collective-permute-start) | collective-permute-done | bytes 139296 | tf_op jit(solution)/shard_map/ppermute | solution.py:413
  17.9 0.1 y_faces.1
  18.0 1.3 %collective-permute-start.3 = (f32[464,128]{1,0:T(8,128)S(1)}, f32[464,128]{1,0:T(8,128)S(1)}, u32[]{:S(2)}, u32[]{:S(2)}) collective-permute-start(f32[464,128]{1,0:T(8,128)S(1)} %get-tuple-element.13), channel_id=1, source_target_pairs={{8,0},{16,8},{24,16},{32,24},{40,32},{48,40},{56,48},{64,56},{72,6... | collective-permute-start | bytes 712712 | tf_op jit(solution)/shard_map/ppermute | solution.py:436
  19.3 3.0 %collective-permute-start.2 = (f32[408,128]{1,0:T(8,128)S(1)}, f32[408,128]{1,0:T(8,128)S(1)}, u32[]{:S(2)}, u32[]{:S(2)}) collective-permute-start(f32[408,128]{1,0:T(8,128)S(1)} %get-tuple-element.12), channel_id=1, source_target_pairs={{0,8},{8,16},{16,24},{24,32},{32,40},{40,48},{48,56},{56,64},{64,7... | collective-permute-start | bytes 626696 | tf_op jit(solution)/shard_map/ppermute | solution.py:435
  22.4 0.7 %tiles.1 = f32[16,8,128]{2,1,0:T(8,128)} custom-call(s32[1]{0:T(128)} %bitcast.odd_ref, f32[34,8,128]{2,1,0:T(8,128)S(1)} %get-tuple-element.10.own_ref, f32[34,8,128]{2,1,0:T(8,128)S(1)} %collective-permute-done.first_ref, f32[34,8,128]{2,1,0:T(8,128)S(1)} %collective-permute-done.1.second_ref), custom_call_target="tpu_custom_call" | custom-call | tf_op jit(solution)/shard_map/tiles/pallas_call | solution.py:416
  23.1 7.7 %all-to-all-start = ((f32[16,8,128]{2,1,0:T(8,128)}), f32[16,8,128]{2,1,0:T(8,128)S(1)}, u32[]{:S(2)}, u32[]{:S(2)}) async-start(f32[16,8,128]{2,1,0:T(8,128)} %tiles.1), calls=%async_computation | async-start | bytes 131072 | tf_op jit(solution)/shard_map/all_to_all | solution.py:424
  30.8 0.1 block.1._
  30.9 7.7 %all-to-all-done.tiles_ref = f32[16,8,128]{2,1,0:T(8,128)S(1)} async-done(((f32[16,8,128]{2,1,0:T(8,128)}), f32[16,8,128]{2,1,0:T(8,128)S(1)}, u32[]{:S(2)}, u32[]{:S(2)}) %all-to-all-start) | async-done | bytes 65568 | tf_op jit(solution)/shard_map/all_to_all | solution.py:424
  38.6 0.6 surface.1.force_ref
  39.2 0.0 collective-permute-done.2.y_low_ref
  39.2 0.0 collective-permute-done.3.y_high_ref
  39.2 4.1 %steps.1 = (f32[3072,128]{1,0:T(8,128)S(1)}, f32[9,8,8,128]{3,2,1,0:T(8,128)}, f32[3,8,8,128]{3,2,1,0:T(8,128)S(1)}) custom-call(f32[3072,128]{1,0:T(8,128)S(1)} %block.1._, bf16[3,9,8,8,128]{4,3,2,1,0:T(8,128)(2,1)} %bitcast.16, f32[408,128]{1,0:T(8,128)S(1)} %collective-permute-done.2.y_low_ref, ...), custom_call_target="tpu_custom_call", output_to_operand_aliasing={{0}: (0, {})} | custom-call | tf_op jit(solution)/shard_map/steps/pallas_call | solution.py:457
  43.3 15.5 %all_to_all.15.parts_ref = f32[24,8,128]{2,1,0:T(8,128)S(1)} all-to-all(f32[24,8,128]{2,1,0:T(8,128)S(1)} %bitcast.15), channel_id=1, replica_groups=mesh['sx'=8,'sy'=16,'ev'=8] {'ev'}, dimensions={0} | all-to-all | bytes 196608 | tf_op jit(solution)/shard_map/all_to_all | solution.py:474
  58.8 11.1 %all_to_all.16 = f32[24,8,128]{2,1,0:T(8,128)S(1)} all-to-all(f32[24,8,128]{2,1,0:T(8,128)S(1)} %event_sum.1), channel_id=1, replica_groups=mesh['sx'=8,'sy'=16,'ev'=8] {'ev'}, dimensions={0} | all-to-all | bytes 196608 | tf_op jit(solution)/shard_map/all_to_all | solution.py:479
  69.9 0.6 copy.15
  (1 shorter events, 0.0 us)
Async XLA Ops:
  2.9 11.6 %collective-permute-start.1 = (f32[34,8,128]{2,1,0:T(8,128)S(1)}, f32[34,8,128]{2,1,0:T(8,128)S(1)}, u32[]{:S(2)}, u32[]{:S(2)}) collective-permute-start(f32[34,8,128]{2,1,0:T(8,128)S(1)} %get-tuple-element.11), channel_id=1, source_target_pairs={{128,256},{384,512},{640,768},{256,128},{512,384},{768,640},{129,2... | collective-permute-start | bytes 417800 | tf_op jit(solution)/shard_map/ppermute | solution.py:414
  4.8 13.1 %collective-permute-start = (f32[34,8,128]{2,1,0:T(8,128)S(1)}, f32[34,8,128]{2,1,0:T(8,128)S(1)}, u32[]{:S(2)}, u32[]{:S(2)}) collective-permute-start(f32[34,8,128]{2,1,0:T(8,128)S(1)} %get-tuple-element.10.own_ref), channel_id=1, source_target_pairs={{0,128},{256,384},{512,640},{768,896},{128,0},{384,256},{640,512},... | collective-permute-start | bytes 417800 | tf_op jit(solution)/shard_map/ppermute | solution.py:413
  18.0 21.1 %collective-permute-start.3 = (f32[464,128]{1,0:T(8,128)S(1)}, f32[464,128]{1,0:T(8,128)S(1)}, u32[]{:S(2)}, u32[]{:S(2)}) collective-permute-start(f32[464,128]{1,0:T(8,128)S(1)} %get-tuple-element.13), channel_id=1, source_target_pairs={{8,0},{16,8},{24,16},{32,24},{40,32},{48,40},{56,48},{64,56},{72,6... | collective-permute-start | bytes 712712 | tf_op jit(solution)/shard_map/ppermute | solution.py:436
  19.3 19.8 %collective-permute-start.2 = (f32[408,128]{1,0:T(8,128)S(1)}, f32[408,128]{1,0:T(8,128)S(1)}, u32[]{:S(2)}, u32[]{:S(2)}) collective-permute-start(f32[408,128]{1,0:T(8,128)S(1)} %get-tuple-element.12), channel_id=1, source_target_pairs={{0,8},{8,16},{16,24},{24,32},{32,40},{40,48},{48,56},{56,64},{64,7... | collective-permute-start | bytes 626696 | tf_op jit(solution)/shard_map/ppermute | solution.py:435
  23.1 15.5 %all-to-all-start = ((f32[16,8,128]{2,1,0:T(8,128)}), f32[16,8,128]{2,1,0:T(8,128)S(1)}, u32[]{:S(2)}, u32[]{:S(2)}) async-start(f32[16,8,128]{2,1,0:T(8,128)} %tiles.1), calls=%async_computation | async-start | bytes 131072 | tf_op jit(solution)/shard_map/all_to_all | solution.py:424

commit v6 on v5

--- a/solution.py
+++ b/solution.py
@@ -21,7 +21,7 @@
 Y_LOW = (2, 3, 2, 2, 3, 2, 3, 2, 3, 3, 2, 2)
 
 
-PLANES = max(sum(X_HIGH), sum(X_LOW)) + 1
+PLANES = max(sum(X_HIGH), sum(X_LOW))
 
 
 def starts(counts):
@@ -49,6 +49,7 @@
     first_ref,
     second_ref,
     base_ref,
+    tiles_ref,
     block_ref,
     cell_ref,
     trace_ref,
@@ -99,8 +100,8 @@
         [jnp.concatenate(parts[:8], axis=0), jnp.concatenate(parts[8:], axis=0), jnp.zeros((8, 128 - 2 * rows), jnp.float32)],
         axis=1,
     )
-    first_ref[PLANES - 1] = pack
-    second_ref[PLANES - 1] = pack
+    for d in range(tiles_ref.shape[0]):
+        tiles_ref[d] = pack
 
     @pl.when(odd_ref[0] == 0)
     def _():
@@ -124,24 +125,6 @@
     @pl.when(odd_ref[0] == 1)
     def _():
         body(first_ref, second_ref)
-
-
-def tiles_kernel(ny, odd_ref, own_ref, first_ref, second_ref, tiles_ref):
-    row = lax.broadcasted_iota(jnp.int32, (8, 128), 0)
-    group = lax.broadcasted_iota(jnp.int32, (8, 128), 1) // 32
-    tile = jnp.zeros((8, 128), jnp.float32)
-    even = odd_ref[0] == 0
-    one, two = first_ref[PLANES - 1], second_ref[PLANES - 1]
-    packs = (own_ref[PLANES - 1], jnp.where(even, two, one), jnp.where(even, one, two))
-    for s, (pack, shift) in enumerate(zip(packs, (W, W - B, W + B))):
-        head = jnp.where(row == 0, pack + float(shift * ny), pack)
-        head = pltpu.roll(head, 32 * s, 1) if s else head
-        tail = pltpu.roll(pack, 64, 1)
-        tail = pltpu.roll(tail, 2 * s, 0) if s else tail
-        tile = jnp.where(group == s, head, tile)
-        tile = jnp.where((group == 3) & (row // 2 == s), tail, tile)
-    for d in range(tiles_ref.shape[0]):
-        tiles_ref[d] = tile
 
 
 def y_faces_kernel(odd_ref, base_ref, first_ref, second_ref, face_low_ref, face_high_ref):
@@ -165,34 +148,38 @@
                     out[pl.ds(row + W + B + above, W - above), :] = jnp.zeros((W - above, 128), jnp.float32)
 
 
-def surface_kernel(ny, place_ref, tiles_ref, surface_ref):
+def surface_kernel(ny, place_ref, odd_ref, tiles_ref, own_ref, first_ref, second_ref):
+    cells = B * YR
+    at = lax.broadcasted_iota(jnp.int32, (cells, 128), 0)
+    local = at % YR
+    local = jnp.where(local < 11, local, local - YR)
+    y = place_ref[0] * B + local
+    ident = jnp.where((y >= 0) & (y < ny), (at // YR) * ny + y, -10000000).astype(jnp.float32)
     group = lax.broadcasted_iota(jnp.int32, (8, 128), 1) // 32
-    for s, first, count in ((0, W, B), (1, 0, W), (2, W + B, W)):
-        cells = count * YR
-        at = lax.broadcasted_iota(jnp.int32, (cells, 128), 0)
-        local = at % YR
-        local = jnp.where(local < 11, local, local - YR)
-        y = place_ref[0] * B + local
-        ident = jnp.where((y >= 0) & (y < ny), (first + at // YR) * ny + y, -10000000).astype(jnp.float32)
-        hot, packed = [], []
-        for source in range(0, tiles_ref.shape[0], 4):
-            heads = tails = jnp.zeros((8, 128), jnp.float32)
-            for i in range(4):
-                tile = tiles_ref[source + i]
-                head, tail = (32 * (i - s)) % 128, (32 * (i - 3)) % 128
-                heads = jnp.where(group == i, pltpu.roll(tile, head, 1) if head else tile, heads)
-                tails = jnp.where(group == i, pltpu.roll(tile, tail, 1) if tail else tile, tails)
-            hot.append((ident == heads[0:1]).astype(jnp.float32))
-            packed.append(jnp.concatenate([heads, pltpu.roll(tails, 8 - 2 * s, 0) if s else tails], axis=0))
-        packed = jnp.concatenate(packed, axis=1)
-        packed = jnp.concatenate([packed, jnp.zeros((112, packed.shape[1]), jnp.float32)], axis=0)
-        surface_ref[pl.ds(first * YR, cells), :] = lax.dot_general(
-            jnp.concatenate(hot, axis=1),
-            packed,
-            (((1,), (1,)), ((), ())),
-            precision=lax.Precision.HIGHEST,
-            preferred_element_type=jnp.float32,
-        )
+    hot, packed = [], []
+    for first in range(0, tiles_ref.shape[0], 4):
+        heads = jnp.where(group == 0, tiles_ref[first], 0.0)
+        tails = jnp.where(group == 0, pltpu.roll(tiles_ref[first], 96, 1), 0.0)
+        for i in range(1, 4):
+            tile = tiles_ref[first + i]
+            heads = jnp.where(group == i, pltpu.roll(tile, 32 * i, 1), heads)
+            tails = jnp.where(group == i, pltpu.roll(tile, (96 + 32 * i) % 128, 1) if i > 1 else tile, tails)
+        hot.append((ident == heads[0:1]).astype(jnp.float32))
+        packed.append(jnp.concatenate([heads, tails], axis=0))
+    packed = jnp.concatenate(packed, axis=1)
+    packed = jnp.concatenate([packed, jnp.zeros((112, packed.shape[1]), jnp.float32)], axis=0)
+    surface = lax.dot_general(
+        jnp.concatenate(hot, axis=1),
+        packed,
+        (((1,), (1,)), ((), ())),
+        precision=lax.Precision.HIGHEST,
+        preferred_element_type=jnp.float32,
+    )
+    own_ref[...] = surface
+    low, high = surface[0 : W * YR], surface[(B - W) * YR :]
+    even = odd_ref[0] == 0
+    first_ref[...] = jnp.where(even, high, low)
+    second_ref[...] = jnp.where(even, low, high)
 
 
 def block_kernel(odd_ref, base_ref, first_ref, second_ref, ext):
@@ -219,17 +206,21 @@
 
 def steps_kernel(
     steps,
+    odd_ref,
     _,
     forward_hbm,
     y_low_ref,
     y_high_ref,
-    force_ref,
+    own_ref,
+    first_ref,
+    second_ref,
     ext,
     state_ref,
     kernels_ref,
     change_ref,
     rate_ref,
     forward_ref,
+    force_ref,
     sem,
     load_sem,
 ):
@@ -242,6 +233,10 @@
                 row = f * PLANE + YR + (first + r if first == 8 else first - count + r)
                 ext[pl.ds(row, XE, stride=YR), :] = ref[pl.ds((at + r) * XE, XE), :]
 
+    even = odd_ref[0] == 0
+    force_ref[pl.ds(0, W * YR), :] = jnp.where(even, second_ref[...], first_ref[...])
+    force_ref[pl.ds(W * YR, B * YR), :] = own_ref[...]
+    force_ref[pl.ds((W + B) * YR, W * YR), :] = jnp.where(even, first_ref[...], second_ref[...])
     lanes = lax.broadcasted_iota(jnp.int32, (YR, 128), 1)
 
     def y_up(v):
@@ -386,11 +381,11 @@
 
     rows = station_cell.shape[1]
     odd = (lax.axis_index("sx") & 1).astype(jnp.int32).reshape(1)
-    first_face, second_face, base = pl.pallas_call(
+    first_face, second_face, base, tiles = pl.pallas_call(
         functools.partial(x_faces_kernel, ny),
-        out_shape=[f32(PLANES, 8, 128)] * 2 + [f32(FIELDS, B, 8, 128)],
+        out_shape=[f32(PLANES, 8, 128)] * 2 + [f32(FIELDS, B, 8, 128), f32(n_sy, 8, 128)],
         in_specs=[SMEM] + [HBM] * 4 + [SMEM] + [HBM] * 3,
-        out_specs=[VMEM] * 3,
+        out_specs=[VMEM] * 4,
         scratch_shapes=[
             pltpu.VMEM((1, rows), jnp.int32),
             pltpu.VMEM((1, rows), jnp.int32),
@@ -413,14 +408,6 @@
     first = lax.ppermute(first_face, "sx", swaps(0, n_sx))
     second = lax.ppermute(second_face, "sx", swaps(1, n_sx))
 
-    tiles = pl.pallas_call(
-        functools.partial(tiles_kernel, ny),
-        out_shape=f32(n_sy, 8, 128),
-        in_specs=[SMEM] + [VMEM] * 3,
-        out_specs=VMEM,
-        compiler_params=pltpu.CompilerParams(vmem_limit_bytes=2 * MIB),
-        name="tiles",
-    )(odd, first_face, first, second)
     tiles = lax.all_to_all(tiles, "sy", split_axis=0, concat_axis=0, tiled=True)
 
     flat = lambda a: a.reshape(-1, 128)
@@ -436,14 +423,16 @@
     y_high = lax.ppermute(y_low_face, "sy", down_y)
 
     place = lax.axis_index("sy").astype(jnp.int32).reshape(1)
-    surface = pl.pallas_call(
+    surface, first_edge, second_edge = pl.pallas_call(
         functools.partial(surface_kernel, ny),
-        out_shape=f32(XE * YR, 128),
-        in_specs=[SMEM, VMEM],
-        out_specs=VMEM,
+        out_shape=[f32(B * YR, 128), f32(W * YR, 128), f32(W * YR, 128)],
+        in_specs=[SMEM, SMEM, VMEM],
+        out_specs=[VMEM] * 3,
         compiler_params=pltpu.CompilerParams(vmem_limit_bytes=4 * MIB),
         name="surface",
-    )(place, tiles)
+    )(place, odd, tiles)
+    first_surface = lax.ppermute(first_edge, "sx", swaps(0, n_sx))
+    second_surface = lax.ppermute(second_edge, "sx", swaps(1, n_sx))
 
     ext = pl.pallas_call(
         block_kernel,
@@ -457,19 +446,20 @@
     _, state, kernels = pl.pallas_call(
         functools.partial(steps_kernel, steps),
         out_shape=[f32(FIELDS * PLANE, 128), f32(9, B, 8, 128), f32(3, B, 8, 128)],
-        in_specs=[VMEM, HBM, VMEM, VMEM, VMEM],
+        in_specs=[SMEM, VMEM, HBM] + [VMEM] * 5,
         out_specs=[VMEM, HBM, VMEM],
-        input_output_aliases={0: 0},
+        input_output_aliases={1: 0},
         scratch_shapes=[
             pltpu.VMEM((3, XS, 8, 128), jnp.float32),
             pltpu.VMEM((6, XS, 8, 128), jnp.float32),
             pltpu.VMEM(forward_state.shape[1:], forward_state.dtype),
+            pltpu.VMEM((XE * YR, 128), jnp.float32),
             pltpu.SemaphoreType.DMA((9,)),
             pltpu.SemaphoreType.DMA((steps,)),
         ],
         compiler_params=pltpu.CompilerParams(vmem_limit_bytes=8 * MIB),
         name="steps",
-    )(ext, in_hbm(forward_state[0]), y_low, y_high, surface)
+    )(odd, ext, in_hbm(forward_state[0]), y_low, y_high, surface, first_surface, second_surface)
 
     parts = lax.all_to_all(kernels.reshape(3 * B, 8, 128), "ev", split_axis=0, concat_axis=0, tiled=True)
     shared = pl.pallas_call(

time: 70.9 us -> 81.8 us (1.15)
  the two profiles are of different devices: /device:TPU:256 before, /device:TPU:128 now
where the time goes in v6:
time: 81.8 us; the launch traced here: 81.4 us
  starting transfers between devices  31.4 us (38%)
  blocking collectives  26.4 us (32%)
  waiting for transfers between devices  14.4 us (18%)
  Pallas kernels  7.11 us (9%)
  between operations  1.39 us (2%)
    all_to_all x1, blocking collectives, on_device(): lax.all_to_all(kernels.reshape(3 * B, 8, 128), 'ev', split_axis=0, concat...  15.3 us
    ppermute x1, starting transfers between devices, on_device(): first = lax.ppermute(first_face, 'sx', swaps(0, n_sx))  13.2 us
    all_to_all x1, blocking collectives, on_device(): lax.all_to_all(shared, 'ev', split_axis=0, concat_axis=0, tiled=True)  11.1 us
    all_to_all x1, waiting for transfers between devices, on_device(): tiles = lax.all_to_all(tiles, 'sy', split_axis=0, concat_axis=0, tiled=True)  7.76 us
    ppermute x1, starting transfers between devices, on_device(): second_surface = lax.ppermute(second_edge, 'sx', swaps(1, n_sx))  6.48 us
    pallas_call x1, Pallas kernels, on_device(): pl.pallas_call(functools.partial(steps_kernel, steps), out_shape=[f32(FIE...  4.14 us
    ppermute x1, waiting for transfers between devices, on_device(): second = lax.ppermute(second_face, 'sx', swaps(1, n_sx))  3.93 us
    all_to_all x1, starting transfers between devices, on_device(): tiles = lax.all_to_all(tiles, 'sy', split_axis=0, concat_axis=0, tiled=True)  3.51 us
  transfers between devices with their start and end apart: 7, of which 4 were waited for; matrix products, arithmetic and copies ran while one was open for 0% of the time, Pallas kernels for 1%

profile of v6, /device:TPU:128, one launch (start us, length us, event | category | flops | bytes accessed | tf_op | source)
XLA Modules:
  0.0 81.4 jit_solution(2029559933855527020)
XLA Ops:
  1.3 2.3 %x_faces.1 = (f32[33,8,128]{2,1,0:T(8,128)S(1)}, f32[33,8,128]{2,1,0:T(8,128)S(1)}, f32[12,8,8,128]{3,2,1,0:T(8,128)S(1)}, f32[16,8,128]{2,1,0:T(8,128)}) custom-call(s32[1]{0:T(128)} %bitcast.odd_ref, f32[9,8,8,128]{3,2,1,0:T(8,128)} %bitcast.18, f32[8,8,128]{2,1,0:T(8,128)} %rho_hbm.1, f32[8,8,128]{2,1,0:T(8,128)} %lam_hbm.1, f32[8,8,128]{2,1,0:T(8,128)} %mu_hbm.1, ...), custom_call_target="tpu_custom_call" | custom-call | tf_op jit(solution)/shard_map/x_faces/pallas_call | solution.py:384
  3.6 13.2 %collective-permute-start = (f32[33,8,128]{2,1,0:T(8,128)S(1)}, f32[33,8,128]{2,1,0:T(8,128)S(1)}, u32[]{:S(2)}, u32[]{:S(2)}) collective-permute-start(f32[33,8,128]{2,1,0:T(8,128)S(1)} %get-tuple-element.14), channel_id=1, source_target_pairs={{0,128},{256,384},{512,640},{768,896},{128,0},{384,256},{640,512},... | collective-permute-start | bytes 405512 | tf_op jit(solution)/shard_map/ppermute | solution.py:408
  16.8 1.9 %collective-permute-start.1 = (f32[33,8,128]{2,1,0:T(8,128)S(1)}, f32[33,8,128]{2,1,0:T(8,128)S(1)}, u32[]{:S(2)}, u32[]{:S(2)}) collective-permute-start(f32[33,8,128]{2,1,0:T(8,128)S(1)} %get-tuple-element.15), channel_id=1, source_target_pairs={{128,256},{384,512},{640,768},{256,128},{512,384},{768,640},{129,2... | collective-permute-start | bytes 405512 | tf_op jit(solution)/shard_map/ppermute | solution.py:409
  18.7 1.0 %collective-permute-done.first_ref = f32[33,8,128]{2,1,0:T(8,128)S(1)} collective-permute-done((f32[33,8,128]{2,1,0:T(8,128)S(1)}, f32[33,8,128]{2,1,0:T(8,128)S(1)}, u32[]{:S(2)}, u32[]{:S(2)}) %collective-permute-start) | collective-permute-done | bytes 135200 | tf_op jit(solution)/shard_map/ppermute | solution.py:408
  19.8 3.9 %collective-permute-done.1.second_ref = f32[33,8,128]{2,1,0:T(8,128)S(1)} collective-permute-done((f32[33,8,128]{2,1,0:T(8,128)S(1)}, f32[33,8,128]{2,1,0:T(8,128)S(1)}, u32[]{:S(2)}, u32[]{:S(2)}) %collective-permute-start.1) | collective-permute-done | bytes 135200 | tf_op jit(solution)/shard_map/ppermute | solution.py:409
  23.7 0.1 y_faces.1
  23.9 1.3 %collective-permute-start.3 = (f32[464,128]{1,0:T(8,128)S(1)}, f32[464,128]{1,0:T(8,128)S(1)}, u32[]{:S(2)}, u32[]{:S(2)}) collective-permute-start(f32[464,128]{1,0:T(8,128)S(1)} %get-tuple-element.17), channel_id=1, source_target_pairs={{8,0},{16,8},{24,16},{32,24},{40,32},{48,40},{56,48},{64,56},{72,6... | collective-permute-start | bytes 712712 | tf_op jit(solution)/shard_map/ppermute | solution.py:423
  25.2 3.0 %collective-permute-start.2 = (f32[408,128]{1,0:T(8,128)S(1)}, f32[408,128]{1,0:T(8,128)S(1)}, u32[]{:S(2)}, u32[]{:S(2)}) collective-permute-start(f32[408,128]{1,0:T(8,128)S(1)} %get-tuple-element.16), channel_id=1, source_target_pairs={{0,8},{8,16},{16,24},{24,32},{32,40},{40,48},{48,56},{56,64},{64,7... | collective-permute-start | bytes 626696 | tf_op jit(solution)/shard_map/ppermute | solution.py:422
  28.2 3.5 %all-to-all-start = ((f32[16,8,128]{2,1,0:T(8,128)}), f32[16,8,128]{2,1,0:T(8,128)S(1)}, u32[]{:S(2)}, u32[]{:S(2)}) async-start(f32[16,8,128]{2,1,0:T(8,128)} %get-tuple-element.18), calls=%async_computation | async-start | bytes 131072 | tf_op jit(solution)/shard_map/all_to_all | solution.py:411
  31.7 7.8 %all-to-all-done.tiles_ref = f32[16,8,128]{2,1,0:T(8,128)S(1)} async-done(((f32[16,8,128]{2,1,0:T(8,128)}), f32[16,8,128]{2,1,0:T(8,128)S(1)}, u32[]{:S(2)}, u32[]{:S(2)}) %all-to-all-start) | async-done | bytes 65568 | tf_op jit(solution)/shard_map/all_to_all | solution.py:411
  39.5 0.4 surface.1
  39.9 1.9 %collective-permute-start.4 = (f32[48,128]{1,0:T(8,128)S(1)}, f32[48,128]{1,0:T(8,128)S(1)}, u32[]{:S(2)}, u32[]{:S(2)}) collective-permute-start(f32[48,128]{1,0:T(8,128)S(1)} %get-tuple-element.20), channel_id=1, source_target_pairs={{0,128},{256,384},{512,640},{768,896},{128,0},{384,256},{640,512},... | collective-permute-start | bytes 73736 | tf_op jit(solution)/shard_map/ppermute | solution.py:434
  41.9 6.5 %collective-permute-start.5 = (f32[48,128]{1,0:T(8,128)S(1)}, f32[48,128]{1,0:T(8,128)S(1)}, u32[]{:S(2)}, u32[]{:S(2)}) collective-permute-start(f32[48,128]{1,0:T(8,128)S(1)} %get-tuple-element.21), channel_id=1, source_target_pairs={{128,256},{384,512},{640,768},{256,128},{512,384},{768,640},{129,2... | collective-permute-start | bytes 73736 | tf_op jit(solution)/shard_map/ppermute | solution.py:435
  48.4 0.1 block.1._
  48.5 0.0 collective-permute-done.4.first_ref
  48.5 1.7 %collective-permute-done.5.second_ref = f32[48,128]{1,0:T(8,128)S(1)} collective-permute-done((f32[48,128]{1,0:T(8,128)S(1)}, f32[48,128]{1,0:T(8,128)S(1)}, u32[]{:S(2)}, u32[]{:S(2)}) %collective-permute-start.5) | collective-permute-done | bytes 24608 | tf_op jit(solution)/shard_map/ppermute | solution.py:435
  50.1 0.0 collective-permute-done.2.y_low_ref
  50.2 0.0 collective-permute-done.3.y_high_ref
  50.2 4.1 %steps.1 = (f32[3072,128]{1,0:T(8,128)S(1)}, f32[9,8,8,128]{3,2,1,0:T(8,128)}, f32[3,8,8,128]{3,2,1,0:T(8,128)S(1)}) custom-call(s32[1]{0:T(128)} %bitcast.odd_ref, f32[3072,128]{1,0:T(8,128)S(1)} %block.1._, bf16[3,9,8,8,128]{4,3,2,1,0:T(8,128)(2,1)} %bitcast.16, f32[408,128]{1,0:T(8,128)S(1)} %collective-permute-done.2.y_low_ref, ...), custom_call_target="tpu_custom_call", output_to_operand_aliasing={{0}: (1, {})} | custom-call | tf_op jit(solution)/shard_map/steps/pallas_call | solution.py:446
  54.3 15.3 %all_to_all.15.parts_ref = f32[24,8,128]{2,1,0:T(8,128)S(1)} all-to-all(f32[24,8,128]{2,1,0:T(8,128)S(1)} %bitcast.15), channel_id=1, replica_groups=mesh['sx'=8,'sy'=16,'ev'=8] {'ev'}, dimensions={0} | all-to-all | bytes 196608 | tf_op jit(solution)/shard_map/all_to_all | solution.py:464
  69.6 11.1 %all_to_all.16 = f32[24,8,128]{2,1,0:T(8,128)S(1)} all-to-all(f32[24,8,128]{2,1,0:T(8,128)S(1)} %event_sum.1), channel_id=1, replica_groups=mesh['sx'=8,'sy'=16,'ev'=8] {'ev'}, dimensions={0} | all-to-all | bytes 196608 | tf_op jit(solution)/shard_map/all_to_all | solution.py:469
  80.7 0.6 copy.15
  (1 shorter events, 0.0 us)
Async XLA Ops:
  3.6 16.2 %collective-permute-start = (f32[33,8,128]{2,1,0:T(8,128)S(1)}, f32[33,8,128]{2,1,0:T(8,128)S(1)}, u32[]{:S(2)}, u32[]{:S(2)}) collective-permute-start(f32[33,8,128]{2,1,0:T(8,128)S(1)} %get-tuple-element.14), channel_id=1, source_target_pairs={{0,128},{256,384},{512,640},{768,896},{128,0},{384,256},{640,512},... | collective-permute-start | bytes 405512 | tf_op jit(solution)/shard_map/ppermute | solution.py:408
  16.8 6.9 %collective-permute-start.1 = (f32[33,8,128]{2,1,0:T(8,128)S(1)}, f32[33,8,128]{2,1,0:T(8,128)S(1)}, u32[]{:S(2)}, u32[]{:S(2)}) collective-permute-start(f32[33,8,128]{2,1,0:T(8,128)S(1)} %get-tuple-element.15), channel_id=1, source_target_pairs={{128,256},{384,512},{640,768},{256,128},{512,384},{768,640},{129,2... | collective-permute-start | bytes 405512 | tf_op jit(solution)/shard_map/ppermute | solution.py:409
  23.9 26.3 %collective-permute-start.3 = (f32[464,128]{1,0:T(8,128)S(1)}, f32[464,128]{1,0:T(8,128)S(1)}, u32[]{:S(2)}, u32[]{:S(2)}) collective-permute-start(f32[464,128]{1,0:T(8,128)S(1)} %get-tuple-element.17), channel_id=1, source_target_pairs={{8,0},{16,8},{24,16},{32,24},{40,32},{48,40},{56,48},{64,56},{72,6... | collective-permute-start | bytes 712712 | tf_op jit(solution)/shard_map/ppermute | solution.py:423
  25.2 25.0 %collective-permute-start.2 = (f32[408,128]{1,0:T(8,128)S(1)}, f32[408,128]{1,0:T(8,128)S(1)}, u32[]{:S(2)}, u32[]{:S(2)}) collective-permute-start(f32[408,128]{1,0:T(8,128)S(1)} %get-tuple-element.16), channel_id=1, source_target_pairs={{0,8},{8,16},{16,24},{24,32},{32,40},{40,48},{48,56},{56,64},{64,7... | collective-permute-start | bytes 626696 | tf_op jit(solution)/shard_map/ppermute | solution.py:422
  28.2 11.3 %all-to-all-start = ((f32[16,8,128]{2,1,0:T(8,128)}), f32[16,8,128]{2,1,0:T(8,128)S(1)}, u32[]{:S(2)}, u32[]{:S(2)}) async-start(f32[16,8,128]{2,1,0:T(8,128)} %get-tuple-element.18), calls=%async_computation | async-start | bytes 131072 | tf_op jit(solution)/shard_map/all_to_all | solution.py:411
  39.9 8.5 %collective-permute-start.4 = (f32[48,128]{1,0:T(8,128)S(1)}, f32[48,128]{1,0:T(8,128)S(1)}, u32[]{:S(2)}, u32[]{:S(2)}) collective-permute-start(f32[48,128]{1,0:T(8,128)S(1)} %get-tuple-element.20), channel_id=1, source_target_pairs={{0,128},{256,384},{512,640},{768,896},{128,0},{384,256},{640,512},... | collective-permute-start | bytes 73736 | tf_op jit(solution)/shard_map/ppermute | solution.py:434
  41.9 8.3 %collective-permute-start.5 = (f32[48,128]{1,0:T(8,128)S(1)}, f32[48,128]{1,0:T(8,128)S(1)}, u32[]{:S(2)}, u32[]{:S(2)}) collective-permute-start(f32[48,128]{1,0:T(8,128)S(1)} %get-tuple-element.21), channel_id=1, source_target_pairs={{128,256},{384,512},{640,768},{256,128},{512,384},{768,640},{129,2... | collective-permute-start | bytes 73736 | tf_op jit(solution)/shard_map/ppermute | solution.py:435

commit v7 on v5

--- a/solution.py
+++ b/solution.py
@@ -60,30 +60,11 @@
         for i, (source, target) in enumerate(((block_hbm, block_ref), (cell_hbm, cell_ref), (trace_hbm, trace_ref)))
     ]
 
-    def faces(low_ref, high_ref):
-        copies = []
-        for side, (out, counts) in enumerate(((low_ref, X_HIGH), (high_ref, X_LOW))):
-            for f, (at, count) in enumerate(zip(starts(counts), counts)):
-                planes = pl.ds(B - count if side else 0, count)
-                source = adj_hbm.at[f, planes] if f < 9 else params[f - 9].at[planes]
-                copies.append(pltpu.make_async_copy(source, out.at[pl.ds(at, count)], sems.at[side, f]))
-        return copies
-
     own = [pltpu.make_async_copy(adj_hbm, base_ref.at[pl.ds(0, 9)], sems.at[2, 0])]
     for i, p in enumerate(params):
         own.append(pltpu.make_async_copy(p, base_ref.at[9 + i], sems.at[2, 1 + i]))
     for copy in rows_in:
         copy.start()
-
-    @pl.when(odd_ref[0] == 0)
-    def _():
-        for copy in faces(second_ref, first_ref):
-            copy.start()
-
-    @pl.when(odd_ref[0] == 1)
-    def _():
-        for copy in faces(first_ref, second_ref):
-            copy.start()
 
     for copy in own:
         copy.start()
@@ -102,18 +83,16 @@
     first_ref[PLANES - 1] = pack
     second_ref[PLANES - 1] = pack
 
-    @pl.when(odd_ref[0] == 0)
-    def _():
-        for copy in faces(second_ref, first_ref):
-            copy.wait()
-
-    @pl.when(odd_ref[0] == 1)
-    def _():
-        for copy in faces(first_ref, second_ref):
-            copy.wait()
-
     for copy in own:
         copy.wait()
+
+    def faces(low_ref, high_ref):
+        for out, counts, side in ((low_ref, X_HIGH, 0), (high_ref, X_LOW, 1)):
+            for f, (at, count) in enumerate(zip(starts(counts), counts)):
+                first = B - count if side else 0
+                out[pl.ds(at, count)] = base_ref[f, pl.ds(first, count)]
+
+    by_side(odd_ref, first_ref, second_ref, faces)
 
 
 def by_side(odd_ref, first_ref, second_ref, body):

time: 70.9 us -> 70.8 us (level)
  no operation moved by 1% of the time
where the time goes in v7:
time: 70.8 us; the launch traced here: 70.4 us
  blocking collectives  26.6 us (38%)
  starting transfers between devices  23.6 us (33%)
  waiting for transfers between devices  11 us (16%)
  Pallas kernels  7.14 us (10%)
  between operations  1.4 us (2%)
    all_to_all x1, blocking collectives, on_device(): lax.all_to_all(kernels.reshape(3 * B, 8, 128), 'ev', split_axis=0, concat...  15.5 us
    all_to_all x1, blocking collectives, on_device(): lax.all_to_all(shared, 'ev', split_axis=0, concat_axis=0, tiled=True)  11.1 us
    ppermute x1, starting transfers between devices, on_device(): first = lax.ppermute(first_face, 'sx', swaps(0, n_sx))  9.67 us
    all_to_all x1, starting transfers between devices, on_device(): tiles = lax.all_to_all(tiles, 'sy', split_axis=0, concat_axis=0, tiled=True)  7.66 us
    all_to_all x1, waiting for transfers between devices, on_device(): tiles = lax.all_to_all(tiles, 'sy', split_axis=0, concat_axis=0, tiled=True)  7.66 us
    pallas_call x1, Pallas kernels, on_device(): pl.pallas_call(functools.partial(steps_kernel, steps), out_shape=[f32(FIE...  4.12 us
    ppermute x1, waiting for transfers between devices, on_device(): first = lax.ppermute(first_face, 'sx', swaps(0, n_sx))  3.37 us
    ppermute x1, starting transfers between devices, on_device(): y_low = lax.ppermute(y_high_face, 'sy', up_y)  3.04 us
  transfers between devices with their start and end apart: 5, of which 2 were waited for; matrix products, arithmetic and copies ran while one was open for 0% of the time, Pallas kernels for 2%

profile of v7, /device:TPU:256, one launch (start us, length us, event | category | flops | bytes accessed | tf_op | source)
XLA Modules:
  0.0 70.4 jit_solution(15544648957938116050)
XLA Ops:
  1.3 1.5 %x_faces.1 = (f32[34,8,128]{2,1,0:T(8,128)S(1)}, f32[34,8,128]{2,1,0:T(8,128)S(1)}, f32[12,8,8,128]{3,2,1,0:T(8,128)S(1)}) custom-call(s32[1]{0:T(128)} %bitcast.odd_ref, f32[9,8,8,128]{3,2,1,0:T(8,128)} %bitcast.18, f32[8,8,128]{2,1,0:T(8,128)} %rho_hbm.1, f32[8,8,128]{2,1,0:T(8,128)} %lam_hbm.1, f32[8,8,128]{2,1,0:T(8,128)} %mu_hbm.1, ...), custom_call_target="tpu_custom_call" | custom-call | tf_op jit(solution)/shard_map/x_faces/pallas_call | solution.py:368
  2.8 1.9 %collective-permute-start.1 = (f32[34,8,128]{2,1,0:T(8,128)S(1)}, f32[34,8,128]{2,1,0:T(8,128)S(1)}, u32[]{:S(2)}, u32[]{:S(2)}) collective-permute-start(f32[34,8,128]{2,1,0:T(8,128)S(1)} %get-tuple-element.11), channel_id=1, source_target_pairs={{128,256},{384,512},{640,768},{256,128},{512,384},{768,640},{129,2... | collective-permute-start | bytes 417800 | tf_op jit(solution)/shard_map/ppermute | solution.py:393
  4.7 9.7 %collective-permute-start = (f32[34,8,128]{2,1,0:T(8,128)S(1)}, f32[34,8,128]{2,1,0:T(8,128)S(1)}, u32[]{:S(2)}, u32[]{:S(2)}) collective-permute-start(f32[34,8,128]{2,1,0:T(8,128)S(1)} %get-tuple-element.10.own_ref), channel_id=1, source_target_pairs={{0,128},{256,384},{512,640},{768,896},{128,0},{384,256},{640,512},... | collective-permute-start | bytes 417800 | tf_op jit(solution)/shard_map/ppermute | solution.py:392
  14.4 0.0 collective-permute-done.1.second_ref
  14.4 3.4 %collective-permute-done.first_ref = f32[34,8,128]{2,1,0:T(8,128)S(1)} collective-permute-done((f32[34,8,128]{2,1,0:T(8,128)S(1)}, f32[34,8,128]{2,1,0:T(8,128)S(1)}, u32[]{:S(2)}, u32[]{:S(2)}) %collective-permute-start) | collective-permute-done | bytes 139296 | tf_op jit(solution)/shard_map/ppermute | solution.py:392
  17.7 0.1 y_faces.1
  17.9 1.3 %collective-permute-start.3 = (f32[464,128]{1,0:T(8,128)S(1)}, f32[464,128]{1,0:T(8,128)S(1)}, u32[]{:S(2)}, u32[]{:S(2)}) collective-permute-start(f32[464,128]{1,0:T(8,128)S(1)} %get-tuple-element.13), channel_id=1, source_target_pairs={{8,0},{16,8},{24,16},{32,24},{40,32},{48,40},{56,48},{64,56},{72,6... | collective-permute-start | bytes 712712 | tf_op jit(solution)/shard_map/ppermute | solution.py:415
  19.2 3.0 %collective-permute-start.2 = (f32[408,128]{1,0:T(8,128)S(1)}, f32[408,128]{1,0:T(8,128)S(1)}, u32[]{:S(2)}, u32[]{:S(2)}) collective-permute-start(f32[408,128]{1,0:T(8,128)S(1)} %get-tuple-element.12), channel_id=1, source_target_pairs={{0,8},{8,16},{16,24},{24,32},{32,40},{40,48},{48,56},{56,64},{64,7... | collective-permute-start | bytes 626696 | tf_op jit(solution)/shard_map/ppermute | solution.py:414
  22.2 0.7 %tiles.1 = f32[16,8,128]{2,1,0:T(8,128)} custom-call(s32[1]{0:T(128)} %bitcast.odd_ref, f32[34,8,128]{2,1,0:T(8,128)S(1)} %get-tuple-element.10.own_ref, f32[34,8,128]{2,1,0:T(8,128)S(1)} %collective-permute-done.first_ref, f32[34,8,128]{2,1,0:T(8,128)S(1)} %collective-permute-done.1.second_ref), custom_call_target="tpu_custom_call" | custom-call | tf_op jit(solution)/shard_map/tiles/pallas_call | solution.py:395
  22.9 7.7 %all-to-all-start = ((f32[16,8,128]{2,1,0:T(8,128)}), f32[16,8,128]{2,1,0:T(8,128)S(1)}, u32[]{:S(2)}, u32[]{:S(2)}) async-start(f32[16,8,128]{2,1,0:T(8,128)} %tiles.1), calls=%async_computation | async-start | bytes 131072 | tf_op jit(solution)/shard_map/all_to_all | solution.py:403
  30.6 0.1 block.1._
  30.7 7.7 %all-to-all-done.tiles_ref = f32[16,8,128]{2,1,0:T(8,128)S(1)} async-done(((f32[16,8,128]{2,1,0:T(8,128)}), f32[16,8,128]{2,1,0:T(8,128)S(1)}, u32[]{:S(2)}, u32[]{:S(2)}) %all-to-all-start) | async-done | bytes 65568 | tf_op jit(solution)/shard_map/all_to_all | solution.py:403
  38.4 0.6 surface.1.force_ref
  39.0 0.0 collective-permute-done.2.y_low_ref
  39.0 0.0 collective-permute-done.3.y_high_ref
  39.0 4.1 %steps.1 = (f32[3072,128]{1,0:T(8,128)S(1)}, f32[9,8,8,128]{3,2,1,0:T(8,128)}, f32[3,8,8,128]{3,2,1,0:T(8,128)S(1)}) custom-call(f32[3072,128]{1,0:T(8,128)S(1)} %block.1._, bf16[3,9,8,8,128]{4,3,2,1,0:T(8,128)(2,1)} %bitcast.16, f32[408,128]{1,0:T(8,128)S(1)} %collective-permute-done.2.y_low_ref, ...), custom_call_target="tpu_custom_call", output_to_operand_aliasing={{0}: (0, {})} | custom-call | tf_op jit(solution)/shard_map/steps/pallas_call | solution.py:436
  43.1 15.5 %all_to_all.15.parts_ref = f32[24,8,128]{2,1,0:T(8,128)S(1)} all-to-all(f32[24,8,128]{2,1,0:T(8,128)S(1)} %bitcast.15), channel_id=1, replica_groups=mesh['sx'=8,'sy'=16,'ev'=8] {'ev'}, dimensions={0} | all-to-all | bytes 196608 | tf_op jit(solution)/shard_map/all_to_all | solution.py:453
  58.6 11.1 %all_to_all.16 = f32[24,8,128]{2,1,0:T(8,128)S(1)} all-to-all(f32[24,8,128]{2,1,0:T(8,128)S(1)} %event_sum.1), channel_id=1, replica_groups=mesh['sx'=8,'sy'=16,'ev'=8] {'ev'}, dimensions={0} | all-to-all | bytes 196608 | tf_op jit(solution)/shard_map/all_to_all | solution.py:458
  69.7 0.6 copy.15
  (1 shorter events, 0.0 us)
Async XLA Ops:
  2.8 11.6 %collective-permute-start.1 = (f32[34,8,128]{2,1,0:T(8,128)S(1)}, f32[34,8,128]{2,1,0:T(8,128)S(1)}, u32[]{:S(2)}, u32[]{:S(2)}) collective-permute-start(f32[34,8,128]{2,1,0:T(8,128)S(1)} %get-tuple-element.11), channel_id=1, source_target_pairs={{128,256},{384,512},{640,768},{256,128},{512,384},{768,640},{129,2... | collective-permute-start | bytes 417800 | tf_op jit(solution)/shard_map/ppermute | solution.py:393
  4.7 13.1 %collective-permute-start = (f32[34,8,128]{2,1,0:T(8,128)S(1)}, f32[34,8,128]{2,1,0:T(8,128)S(1)}, u32[]{:S(2)}, u32[]{:S(2)}) collective-permute-start(f32[34,8,128]{2,1,0:T(8,128)S(1)} %get-tuple-element.10.own_ref), channel_id=1, source_target_pairs={{0,128},{256,384},{512,640},{768,896},{128,0},{384,256},{640,512},... | collective-permute-start | bytes 417800 | tf_op jit(solution)/shard_map/ppermute | solution.py:392
  17.9 21.1 %collective-permute-start.3 = (f32[464,128]{1,0:T(8,128)S(1)}, f32[464,128]{1,0:T(8,128)S(1)}, u32[]{:S(2)}, u32[]{:S(2)}) collective-permute-start(f32[464,128]{1,0:T(8,128)S(1)} %get-tuple-element.13), channel_id=1, source_target_pairs={{8,0},{16,8},{24,16},{32,24},{40,32},{48,40},{56,48},{64,56},{72,6... | collective-permute-start | bytes 712712 | tf_op jit(solution)/shard_map/ppermute | solution.py:415
  19.2 19.8 %collective-permute-start.2 = (f32[408,128]{1,0:T(8,128)S(1)}, f32[408,128]{1,0:T(8,128)S(1)}, u32[]{:S(2)}, u32[]{:S(2)}) collective-permute-start(f32[408,128]{1,0:T(8,128)S(1)} %get-tuple-element.12), channel_id=1, source_target_pairs={{0,8},{8,16},{16,24},{24,32},{32,40},{40,48},{48,56},{56,64},{64,7... | collective-permute-start | bytes 626696 | tf_op jit(solution)/shard_map/ppermute | solution.py:414
  22.9 15.5 %all-to-all-start = ((f32[16,8,128]{2,1,0:T(8,128)}), f32[16,8,128]{2,1,0:T(8,128)S(1)}, u32[]{:S(2)}, u32[]{:S(2)}) async-start(f32[16,8,128]{2,1,0:T(8,128)} %tiles.1), calls=%async_computation | async-start | bytes 131072 | tf_op jit(solution)/shard_map/all_to_all | solution.py:403

commit v8 on v4

--- a/solution.py
+++ b/solution.py
@@ -52,18 +52,12 @@
 ):
     params = (rho_hbm, lam_hbm, mu_hbm)
     rows_in = [
-        pltpu.make_async_copy(source, target, sems.at[3, i])
+        pltpu.make_async_copy(source, target, sems.at[1, i])
         for i, (source, target) in enumerate(((block_hbm, block_ref), (cell_hbm, cell_ref), (trace_hbm, trace_ref)))
     ]
-    copies = []
-    for side, (out, counts) in enumerate(((low_ref, X_HIGH), (high_ref, X_LOW))):
-        for f, (at, count) in enumerate(zip(starts(counts), counts)):
-            planes = pl.ds(B - count if side else 0, count)
-            source = adj_hbm.at[f, planes] if f < 9 else params[f - 9].at[planes]
-            copies.append(pltpu.make_async_copy(source, out.at[pl.ds(at, count)], sems.at[side, f]))
-    copies.append(pltpu.make_async_copy(adj_hbm, base_ref.at[pl.ds(0, 9)], sems.at[2, 0]))
+    copies = [pltpu.make_async_copy(adj_hbm, base_ref.at[pl.ds(0, 9)], sems.at[0, 0])]
     for i, p in enumerate(params):
-        copies.append(pltpu.make_async_copy(p, base_ref.at[9 + i], sems.at[2, 1 + i]))
+        copies.append(pltpu.make_async_copy(p, base_ref.at[9 + i], sems.at[0, 1 + i]))
     for copy in rows_in + copies:
         copy.start()
     for copy in rows_in:
@@ -82,6 +76,9 @@
     high_ref[sum(X_LOW)] = pack
     for copy in copies:
         copy.wait()
+    for out, counts, side in ((low_ref, X_HIGH, 0), (high_ref, X_LOW, 1)):
+        for f, (at, count) in enumerate(zip(starts(counts), counts)):
+            out[pl.ds(at, count)] = base_ref[f, pl.ds(B - count if side else 0, count)]
 
 
 def tiles_kernel(ny, own_ref, low_ref, high_ref, tiles_ref):
@@ -204,11 +201,11 @@
     def z_down(v):
         return jnp.where(lanes == 0, 0.0, pltpu.roll(v, 1, 1))
 
-    def get(f, e):
-        return ext[pl.ds(pl.multiple_of(f * PLANE + e * YR, YR), YR), :]
+    def get(f, e, rows=YR):
+        return ext[pl.ds(pl.multiple_of(f * PLANE + e * YR, YR), rows), :]
 
     def put(f, e, v):
-        ext[pl.ds(pl.multiple_of(f * PLANE + e * YR, YR), YR), :] = v
+        ext[pl.ds(pl.multiple_of(f * PLANE + e * YR, YR), v.shape[0]), :] = v
 
     for step in range(steps):
 
@@ -233,14 +230,18 @@
             exy = 0.5 * ((y_up(vx) - vx) + (get(1, e + 1) - vy))
             exz = 0.5 * ((z_up(vx) - vx) + (get(2, e + 1) - vz))
             eyz = 0.5 * ((z_up(vy) - vy) + (y_up(vz) - vz))
-            trace = exx + eyy + ezz
-            lam = get(10, e) * trace
-            twice = 2.0 * get(11, e)
-            for f, rate in enumerate((exx, eyy, ezz, exy, exz, eyz)):
+            rates = (exx, eyy, ezz, exy, exz, eyz)
+            if step == steps - 1:
+                rates = [rate[0:8] for rate in rates]
+            rows = rates[0].shape[0]
+            trace = rates[0] + rates[1] + rates[2]
+            lam = get(10, e, rows) * trace
+            twice = 2.0 * get(11, e, rows)
+            for f, rate in enumerate(rates):
                 if f < 3:
-                    put(3 + f, e, get(3 + f, e) + DT * (lam + twice * rate))
+                    put(3 + f, e, get(3 + f, e, rows) + DT * (lam + twice * rate))
                 else:
-                    put(3 + f, e, get(3 + f, e) + DT * twice * rate)
+                    put(3 + f, e, get(3 + f, e, rows) + DT * twice * rate)
                 rate_ref[f, e] = rate[0:8]
 
         def pair(body, first):
@@ -339,7 +340,7 @@
             pltpu.VMEM((1, rows), jnp.int32),
             pltpu.VMEM((1, rows), jnp.int32),
             pltpu.VMEM((9, 1, rows), jnp.float32),
-            pltpu.SemaphoreType.DMA((4, FIELDS)),
+            pltpu.SemaphoreType.DMA((2, 4)),
         ],
         compiler_params=pltpu.CompilerParams(vmem_limit_bytes=3 * MIB),
         name="x_faces",

time: 67.8 us -> 67.3 us (level)
  no operation moved by 1% of the time
where the time goes in v8:
time: 67.3 us; the launch traced here: 66.9 us
  starting transfers between devices  23 us (34%)
  blocking collectives  22.6 us (34%)
  waiting for transfers between devices  12.5 us (19%)
  Pallas kernels  6.71 us (10%)
  between operations  1.38 us (2%)
    ppermute x1, starting transfers between devices, on_device(): high = lax.ppermute(low_face, 'sx', down_x)  13.3 us
    all_to_all x1, blocking collectives, on_device(): lax.all_to_all(kernels.reshape(3 * B, 8, 128), 'ev', split_axis=0, concat...  11.5 us
    all_to_all x1, blocking collectives, on_device(): lax.all_to_all(shared, 'ev', split_axis=0, concat_axis=0, tiled=True)  11.1 us
    all_to_all x1, waiting for transfers between devices, on_device(): tiles = lax.all_to_all(tiles, 'sy', split_axis=0, concat_axis=0, tiled=True)  7.65 us
    ppermute x1, waiting for transfers between devices, on_device(): low = lax.ppermute(high_face, 'sx', up_x)  4.85 us
    pallas_call x1, Pallas kernels, on_device(): pl.pallas_call(functools.partial(steps_kernel, steps), out_shape=[f32(FIE...  4.08 us
    all_to_all x1, starting transfers between devices, on_device(): tiles = lax.all_to_all(tiles, 'sy', split_axis=0, concat_axis=0, tiled=True)  3.5 us
    ppermute x1, starting transfers between devices, on_device(): y_low = lax.ppermute(y_high_face, 'sy', up_y)  3.04 us
  transfers between devices with their start and end apart: 5, of which 2 were waited for; matrix products, arithmetic and copies ran while one was open for 0% of the time, Pallas kernels for 2%

profile of v8, /device:TPU:128, one launch (start us, length us, event | category | flops | bytes accessed | tf_op | source)
XLA Modules:
  0.0 66.9 jit_solution(4578009620150964058)
XLA Ops:
  1.3 1.1 %x_faces.1 = (f32[34,8,128]{2,1,0:T(8,128)S(1)}, f32[30,8,128]{2,1,0:T(8,128)S(1)}, f32[12,8,8,128]{3,2,1,0:T(8,128)S(1)}) custom-call(f32[9,8,8,128]{3,2,1,0:T(8,128)} %bitcast.17, f32[8,8,128]{2,1,0:T(8,128)} %rho_hbm.1, f32[8,8,128]{2,1,0:T(8,128)} %lam_hbm.1, f32[8,8,128]{2,1,0:T(8,128)} %mu_hbm.1, s32[1,1]{1,0:T(1,128)S(6)} %copy.14.count_ref, ...), custom_call_target="tpu_custom_call" | custom-call | tf_op jit(solution)/shard_map/x_faces/pallas_call | solution.py:334
  2.4 13.3 %collective-permute-start.1 = (f32[34,8,128]{2,1,0:T(8,128)S(1)}, f32[34,8,128]{2,1,0:T(8,128)S(1)}, u32[]{:S(2)}, u32[]{:S(2)}) collective-permute-start(f32[34,8,128]{2,1,0:T(8,128)S(1)} %get-tuple-element.11.own_ref), channel_id=1, source_target_pairs={{128,0},{256,128},{384,256},{512,384},{640,512},{768,640},{896,768... | collective-permute-start | bytes 417800 | tf_op jit(solution)/shard_map/ppermute | solution.py:358
  15.7 1.9 %collective-permute-start = (f32[30,8,128]{2,1,0:T(8,128)S(1)}, f32[30,8,128]{2,1,0:T(8,128)S(1)}, u32[]{:S(2)}, u32[]{:S(2)}) collective-permute-start(f32[30,8,128]{2,1,0:T(8,128)S(1)} %get-tuple-element.10), channel_id=1, source_target_pairs={{0,128},{128,256},{256,384},{384,512},{512,640},{640,768},{768,896... | collective-permute-start | bytes 368648 | tf_op jit(solution)/shard_map/ppermute | solution.py:357
  17.6 4.8 %collective-permute-done.low_ref = f32[30,8,128]{2,1,0:T(8,128)S(1)} collective-permute-done((f32[30,8,128]{2,1,0:T(8,128)S(1)}, f32[30,8,128]{2,1,0:T(8,128)S(1)}, u32[]{:S(2)}, u32[]{:S(2)}) %collective-permute-start) | collective-permute-done | bytes 122912 | tf_op jit(solution)/shard_map/ppermute | solution.py:357
  22.4 0.0 collective-permute-done.1.high_ref
  22.4 0.1 y_faces.1
  22.6 1.3 %collective-permute-start.3 = (f32[464,128]{1,0:T(8,128)S(1)}, f32[464,128]{1,0:T(8,128)S(1)}, u32[]{:S(2)}, u32[]{:S(2)}) collective-permute-start(f32[464,128]{1,0:T(8,128)S(1)} %get-tuple-element.13), channel_id=1, source_target_pairs={{8,0},{16,8},{24,16},{32,24},{40,32},{48,40},{56,48},{64,56},{72,6... | collective-permute-start | bytes 712712 | tf_op jit(solution)/shard_map/ppermute | solution.py:380
  23.9 3.0 %collective-permute-start.2 = (f32[408,128]{1,0:T(8,128)S(1)}, f32[408,128]{1,0:T(8,128)S(1)}, u32[]{:S(2)}, u32[]{:S(2)}) collective-permute-start(f32[408,128]{1,0:T(8,128)S(1)} %get-tuple-element.12), channel_id=1, source_target_pairs={{0,8},{8,16},{16,24},{24,32},{32,40},{40,48},{48,56},{56,64},{64,7... | collective-permute-start | bytes 626696 | tf_op jit(solution)/shard_map/ppermute | solution.py:379
  26.9 0.7 %tiles.1 = f32[16,8,128]{2,1,0:T(8,128)} custom-call(f32[34,8,128]{2,1,0:T(8,128)S(1)} %get-tuple-element.11.own_ref, f32[30,8,128]{2,1,0:T(8,128)S(1)} %collective-permute-done.low_ref, f32[34,8,128]{2,1,0:T(8,128)S(1)} %collective-permute-done.1.high_ref), custom_call_target="tpu_custom_call" | custom-call | tf_op jit(solution)/shard_map/tiles/pallas_call | solution.py:360
  27.6 3.5 %all-to-all-start = ((f32[16,8,128]{2,1,0:T(8,128)}), f32[16,8,128]{2,1,0:T(8,128)S(1)}, u32[]{:S(2)}, u32[]{:S(2)}) async-start(f32[16,8,128]{2,1,0:T(8,128)} %tiles.1), calls=%async_computation | async-start | bytes 131072 | tf_op jit(solution)/shard_map/all_to_all | solution.py:368
  31.1 0.1 block.1._
  31.3 7.7 %all-to-all-done.tiles_ref = f32[16,8,128]{2,1,0:T(8,128)S(1)} async-done(((f32[16,8,128]{2,1,0:T(8,128)}), f32[16,8,128]{2,1,0:T(8,128)S(1)}, u32[]{:S(2)}, u32[]{:S(2)}) %all-to-all-start) | async-done | bytes 65568 | tf_op jit(solution)/shard_map/all_to_all | solution.py:368
  38.9 0.6 surface.1.force_ref
  39.5 0.0 collective-permute-done.2.y_low_ref
  39.5 0.0 collective-permute-done.3.y_high_ref
  39.5 4.1 %steps.1 = (f32[3072,128]{1,0:T(8,128)S(1)}, f32[9,8,8,128]{3,2,1,0:T(8,128)}, f32[3,8,8,128]{3,2,1,0:T(8,128)S(1)}) custom-call(f32[3072,128]{1,0:T(8,128)S(1)} %block.1._, bf16[3,9,8,8,128]{4,3,2,1,0:T(8,128)(2,1)} %bitcast.15, f32[408,128]{1,0:T(8,128)S(1)} %collective-permute-done.2.y_low_ref, ...), custom_call_target="tpu_custom_call", output_to_operand_aliasing={{0}: (0, {})} | custom-call | tf_op jit(solution)/shard_map/steps/pallas_call | solution.py:401
  43.6 11.5 %all_to_all.15.parts_ref = f32[24,8,128]{2,1,0:T(8,128)S(1)} all-to-all(f32[24,8,128]{2,1,0:T(8,128)S(1)} %bitcast.14), channel_id=1, replica_groups=mesh['sx'=8,'sy'=16,'ev'=8] {'ev'}, dimensions={0} | all-to-all | bytes 196608 | tf_op jit(solution)/shard_map/all_to_all | solution.py:418
  55.2 11.1 %all_to_all.16 = f32[24,8,128]{2,1,0:T(8,128)S(1)} all-to-all(f32[24,8,128]{2,1,0:T(8,128)S(1)} %event_sum.1), channel_id=1, replica_groups=mesh['sx'=8,'sy'=16,'ev'=8] {'ev'}, dimensions={0} | all-to-all | bytes 196608 | tf_op jit(solution)/shard_map/all_to_all | solution.py:423
  66.3 0.6 copy.15
  (1 shorter events, 0.0 us)
Async XLA Ops:
  2.4 20.1 %collective-permute-start.1 = (f32[34,8,128]{2,1,0:T(8,128)S(1)}, f32[34,8,128]{2,1,0:T(8,128)S(1)}, u32[]{:S(2)}, u32[]{:S(2)}) collective-permute-start(f32[34,8,128]{2,1,0:T(8,128)S(1)} %get-tuple-element.11.own_ref), channel_id=1, source_target_pairs={{128,0},{256,128},{384,256},{512,384},{640,512},{768,640},{896,768... | collective-permute-start | bytes 417800 | tf_op jit(solution)/shard_map/ppermute | solution.py:358
  15.7 6.8 %collective-permute-start = (f32[30,8,128]{2,1,0:T(8,128)S(1)}, f32[30,8,128]{2,1,0:T(8,128)S(1)}, u32[]{:S(2)}, u32[]{:S(2)}) collective-permute-start(f32[30,8,128]{2,1,0:T(8,128)S(1)} %get-tuple-element.10), channel_id=1, source_target_pairs={{0,128},{128,256},{256,384},{384,512},{512,640},{640,768},{768,896... | collective-permute-start | bytes 368648 | tf_op jit(solution)/shard_map/ppermute | solution.py:357
  22.6 16.9 %collective-permute-start.3 = (f32[464,128]{1,0:T(8,128)S(1)}, f32[464,128]{1,0:T(8,128)S(1)}, u32[]{:S(2)}, u32[]{:S(2)}) collective-permute-start(f32[464,128]{1,0:T(8,128)S(1)} %get-tuple-element.13), channel_id=1, source_target_pairs={{8,0},{16,8},{24,16},{32,24},{40,32},{48,40},{56,48},{64,56},{72,6... | collective-permute-start | bytes 712712 | tf_op jit(solution)/shard_map/ppermute | solution.py:380
  23.9 15.6 %collective-permute-start.2 = (f32[408,128]{1,0:T(8,128)S(1)}, f32[408,128]{1,0:T(8,128)S(1)}, u32[]{:S(2)}, u32[]{:S(2)}) collective-permute-start(f32[408,128]{1,0:T(8,128)S(1)} %get-tuple-element.12), channel_id=1, source_target_pairs={{0,8},{8,16},{16,24},{24,32},{32,40},{40,48},{48,56},{56,64},{64,7... | collective-permute-start | bytes 626696 | tf_op jit(solution)/shard_map/ppermute | solution.py:379
  27.6 11.3 %all-to-all-start = ((f32[16,8,128]{2,1,0:T(8,128)}), f32[16,8,128]{2,1,0:T(8,128)S(1)}, u32[]{:S(2)}, u32[]{:S(2)}) async-start(f32[16,8,128]{2,1,0:T(8,128)} %tiles.1), calls=%async_computation | async-start | bytes 131072 | tf_op jit(solution)/shard_map/all_to_all | solution.py:368

commit v9 on v8

--- a/solution.py
+++ b/solution.py
@@ -220,7 +220,7 @@
                 force = jnp.where(lanes == 0, pltpu.roll(surface, 127 - 3 * step - c, 1), 0.0)
                 change = scale * (accel + force)
                 put(c, e, get(c, e) + change)
-                change_ref[c, e] = change[0:8]
+                change_ref[3 * step + c, e] = change[0:8]
 
         def stress(e):
             vx, vy, vz = [get(f, e) for f in range(3)]
@@ -242,7 +242,7 @@
                     put(3 + f, e, get(3 + f, e, rows) + DT * (lam + twice * rate))
                 else:
                     put(3 + f, e, get(3 + f, e, rows) + DT * twice * rate)
-                rate_ref[f, e] = rate[0:8]
+                rate_ref[6 * step + f, e] = rate[0:8]
 
         def pair(body, first):
             def run(i, carry):
@@ -255,23 +255,24 @@
 
         lax.fori_loop(0, (XE - 2 * step) // 2, pair(velocity, 1 + step), 0)
         lax.fori_loop(0, (XE - 2 * step - 2) // 2, pair(stress, 2 + step), 0)
-        if step == steps - 1:
-            copies = [
-                pltpu.make_async_copy(
-                    ext.reshape(FIELDS, XS, YR, 128).at[f, pl.ds(1 + W, B), pl.ds(0, B)], state_ref.at[f], sem.at[f]
-                )
-                for f in range(9)
-            ]
-            for copy in copies:
-                copy.start()
-
-        loads[step].wait()
-
-        def sensitivities(x, carry):
-            e = x + 1 + W
+    copies = [
+        pltpu.make_async_copy(
+            ext.reshape(FIELDS, XS, YR, 128).at[f, pl.ds(1 + W, B), pl.ds(0, B)], state_ref.at[f], sem.at[f]
+        )
+        for f in range(9)
+    ]
+    for copy in copies:
+        copy.start()
+    for load in loads:
+        load.wait()
+
+    def sensitivities(x, carry):
+        e = x + 1 + W
+        totals = None
+        for step in range(steps):
             f = [forward_ref[step, c, x].astype(jnp.float32) for c in range(9)]
-            change = [change_ref[c, e] for c in range(3)]
-            rate = [rate_ref[c, e] for c in range(6)]
+            change = [change_ref[3 * step + c, e] for c in range(3)]
+            rate = [rate_ref[6 * step + c, e] for c in range(6)]
             trace = rate[0] + rate[1] + rate[2]
             terms = (
                 f[0] * change[0] + f[1] * change[1] + f[2] * change[2],
@@ -283,11 +284,12 @@
                     + 2.0 * (f[6] * rate[3] + f[7] * rate[4] + f[8] * rate[5])
                 ),
             )
-            for k, term in enumerate(terms):
-                kernels_ref[k, x] = kernels_ref[k, x] + term if step else term
-            return carry
-
-        lax.fori_loop(0, B, sensitivities, 0, unroll=4)
+            totals = [total + term for total, term in zip(totals, terms)] if step else terms
+        for k in range(3):
+            kernels_ref[k, x] = totals[k]
+        return carry
+
+    lax.fori_loop(0, B, sensitivities, 0, unroll=2)
 
     for copy in copies:
         copy.wait()
@@ -405,8 +407,8 @@
         out_specs=[VMEM, HBM, VMEM],
         input_output_aliases={0: 0},
         scratch_shapes=[
-            pltpu.VMEM((3, XS, 8, 128), jnp.float32),
-            pltpu.VMEM((6, XS, 8, 128), jnp.float32),
+            pltpu.VMEM((3 * steps, XS, 8, 128), jnp.float32),
+            pltpu.VMEM((6 * steps, XS, 8, 128), jnp.float32),
             pltpu.VMEM(forward_state.shape[1:], forward_state.dtype),
             pltpu.SemaphoreType.DMA((9,)),
             pltpu.SemaphoreType.DMA((steps,)),

time: 67.3 us -> 67.2 us (level)
  no operation moved by 1% of the time
where the time goes in v9:
time: 67.2 us; the launch traced here: 66.8 us
  starting transfers between devices  23 us (34%)
  blocking collectives  22.6 us (34%)
  waiting for transfers between devices  12.5 us (19%)
  Pallas kernels  6.61 us (10%)
  between operations  1.38 us (2%)
    ppermute x1, starting transfers between devices, on_device(): high = lax.ppermute(low_face, 'sx', down_x)  13.3 us
    all_to_all x1, blocking collectives, on_device(): lax.all_to_all(kernels.reshape(3 * B, 8, 128), 'ev', split_axis=0, concat...  11.5 us
    all_to_all x1, blocking collectives, on_device(): lax.all_to_all(shared, 'ev', split_axis=0, concat_axis=0, tiled=True)  11.1 us
    all_to_all x1, waiting for transfers between devices, on_device(): tiles = lax.all_to_all(tiles, 'sy', split_axis=0, concat_axis=0, tiled=True)  7.65 us
    ppermute x1, waiting for transfers between devices, on_device(): low = lax.ppermute(high_face, 'sx', up_x)  4.85 us
    pallas_call x1, Pallas kernels, on_device(): pl.pallas_call(functools.partial(steps_kernel, steps), out_shape=[f32(FIE...  3.98 us
    all_to_all x1, starting transfers between devices, on_device(): tiles = lax.all_to_all(tiles, 'sy', split_axis=0, concat_axis=0, tiled=True)  3.5 us
    ppermute x1, starting transfers between devices, on_device(): y_low = lax.ppermute(y_high_face, 'sy', up_y)  3.04 us
  transfers between devices with their start and end apart: 5, of which 2 were waited for; matrix products, arithmetic and copies ran while one was open for 0% of the time, Pallas kernels for 2%

profile of v9, /device:TPU:128, one launch (start us, length us, event | category | flops | bytes accessed | tf_op | source)
XLA Modules:
  0.0 66.8 jit_solution(7915777108061777033)
XLA Ops:
  1.3 1.1 %x_faces.1 = (f32[34,8,128]{2,1,0:T(8,128)S(1)}, f32[30,8,128]{2,1,0:T(8,128)S(1)}, f32[12,8,8,128]{3,2,1,0:T(8,128)S(1)}) custom-call(f32[9,8,8,128]{3,2,1,0:T(8,128)} %bitcast.17, f32[8,8,128]{2,1,0:T(8,128)} %rho_hbm.1, f32[8,8,128]{2,1,0:T(8,128)} %lam_hbm.1, f32[8,8,128]{2,1,0:T(8,128)} %mu_hbm.1, s32[1,1]{1,0:T(1,128)S(6)} %copy.14.count_ref, ...), custom_call_target="tpu_custom_call" | custom-call | tf_op jit(solution)/shard_map/x_faces/pallas_call | solution.py:336
  2.4 13.3 %collective-permute-start.1 = (f32[34,8,128]{2,1,0:T(8,128)S(1)}, f32[34,8,128]{2,1,0:T(8,128)S(1)}, u32[]{:S(2)}, u32[]{:S(2)}) collective-permute-start(f32[34,8,128]{2,1,0:T(8,128)S(1)} %get-tuple-element.11.own_ref), channel_id=1, source_target_pairs={{128,0},{256,128},{384,256},{512,384},{640,512},{768,640},{896,768... | collective-permute-start | bytes 417800 | tf_op jit(solution)/shard_map/ppermute | solution.py:360
  15.7 1.9 %collective-permute-start = (f32[30,8,128]{2,1,0:T(8,128)S(1)}, f32[30,8,128]{2,1,0:T(8,128)S(1)}, u32[]{:S(2)}, u32[]{:S(2)}) collective-permute-start(f32[30,8,128]{2,1,0:T(8,128)S(1)} %get-tuple-element.10), channel_id=1, source_target_pairs={{0,128},{128,256},{256,384},{384,512},{512,640},{640,768},{768,896... | collective-permute-start | bytes 368648 | tf_op jit(solution)/shard_map/ppermute | solution.py:359
  17.6 4.8 %collective-permute-done.low_ref = f32[30,8,128]{2,1,0:T(8,128)S(1)} collective-permute-done((f32[30,8,128]{2,1,0:T(8,128)S(1)}, f32[30,8,128]{2,1,0:T(8,128)S(1)}, u32[]{:S(2)}, u32[]{:S(2)}) %collective-permute-start) | collective-permute-done | bytes 122912 | tf_op jit(solution)/shard_map/ppermute | solution.py:359
  22.4 0.0 collective-permute-done.1.high_ref
  22.4 0.1 y_faces.1
  22.6 1.3 %collective-permute-start.3 = (f32[464,128]{1,0:T(8,128)S(1)}, f32[464,128]{1,0:T(8,128)S(1)}, u32[]{:S(2)}, u32[]{:S(2)}) collective-permute-start(f32[464,128]{1,0:T(8,128)S(1)} %get-tuple-element.13), channel_id=1, source_target_pairs={{8,0},{16,8},{24,16},{32,24},{40,32},{48,40},{56,48},{64,56},{72,6... | collective-permute-start | bytes 712712 | tf_op jit(solution)/shard_map/ppermute | solution.py:382
  23.9 3.0 %collective-permute-start.2 = (f32[408,128]{1,0:T(8,128)S(1)}, f32[408,128]{1,0:T(8,128)S(1)}, u32[]{:S(2)}, u32[]{:S(2)}) collective-permute-start(f32[408,128]{1,0:T(8,128)S(1)} %get-tuple-element.12), channel_id=1, source_target_pairs={{0,8},{8,16},{16,24},{24,32},{32,40},{40,48},{48,56},{56,64},{64,7... | collective-permute-start | bytes 626696 | tf_op jit(solution)/shard_map/ppermute | solution.py:381
  26.9 0.7 %tiles.1 = f32[16,8,128]{2,1,0:T(8,128)} custom-call(f32[34,8,128]{2,1,0:T(8,128)S(1)} %get-tuple-element.11.own_ref, f32[30,8,128]{2,1,0:T(8,128)S(1)} %collective-permute-done.low_ref, f32[34,8,128]{2,1,0:T(8,128)S(1)} %collective-permute-done.1.high_ref), custom_call_target="tpu_custom_call" | custom-call | tf_op jit(solution)/shard_map/tiles/pallas_call | solution.py:362
  27.6 3.5 %all-to-all-start = ((f32[16,8,128]{2,1,0:T(8,128)}), f32[16,8,128]{2,1,0:T(8,128)S(1)}, u32[]{:S(2)}, u32[]{:S(2)}) async-start(f32[16,8,128]{2,1,0:T(8,128)} %tiles.1), calls=%async_computation | async-start | bytes 131072 | tf_op jit(solution)/shard_map/all_to_all | solution.py:370
  31.1 0.1 block.1._
  31.3 7.7 %all-to-all-done.tiles_ref = f32[16,8,128]{2,1,0:T(8,128)S(1)} async-done(((f32[16,8,128]{2,1,0:T(8,128)}), f32[16,8,128]{2,1,0:T(8,128)S(1)}, u32[]{:S(2)}, u32[]{:S(2)}) %all-to-all-start) | async-done | bytes 65568 | tf_op jit(solution)/shard_map/all_to_all | solution.py:370
  38.9 0.6 surface.1.force_ref
  39.5 0.0 collective-permute-done.2.y_low_ref
  39.5 0.0 collective-permute-done.3.y_high_ref
  39.5 4.0 %steps.1 = (f32[3072,128]{1,0:T(8,128)S(1)}, f32[9,8,8,128]{3,2,1,0:T(8,128)}, f32[3,8,8,128]{3,2,1,0:T(8,128)S(1)}) custom-call(f32[3072,128]{1,0:T(8,128)S(1)} %block.1._, bf16[3,9,8,8,128]{4,3,2,1,0:T(8,128)(2,1)} %bitcast.15, f32[408,128]{1,0:T(8,128)S(1)} %collective-permute-done.2.y_low_ref, ...), custom_call_target="tpu_custom_call", output_to_operand_aliasing={{0}: (0, {})} | custom-call | tf_op jit(solution)/shard_map/steps/pallas_call | solution.py:403
  43.5 11.5 %all_to_all.15.parts_ref = f32[24,8,128]{2,1,0:T(8,128)S(1)} all-to-all(f32[24,8,128]{2,1,0:T(8,128)S(1)} %bitcast.14), channel_id=1, replica_groups=mesh['sx'=8,'sy'=16,'ev'=8] {'ev'}, dimensions={0} | all-to-all | bytes 196608 | tf_op jit(solution)/shard_map/all_to_all | solution.py:420
  55.1 11.1 %all_to_all.16 = f32[24,8,128]{2,1,0:T(8,128)S(1)} all-to-all(f32[24,8,128]{2,1,0:T(8,128)S(1)} %event_sum.1), channel_id=1, replica_groups=mesh['sx'=8,'sy'=16,'ev'=8] {'ev'}, dimensions={0} | all-to-all | bytes 196608 | tf_op jit(solution)/shard_map/all_to_all | solution.py:425
  66.2 0.6 copy.15
  (1 shorter events, 0.0 us)
Async XLA Ops:
  2.4 20.1 %collective-permute-start.1 = (f32[34,8,128]{2,1,0:T(8,128)S(1)}, f32[34,8,128]{2,1,0:T(8,128)S(1)}, u32[]{:S(2)}, u32[]{:S(2)}) collective-permute-start(f32[34,8,128]{2,1,0:T(8,128)S(1)} %get-tuple-element.11.own_ref), channel_id=1, source_target_pairs={{128,0},{256,128},{384,256},{512,384},{640,512},{768,640},{896,768... | collective-permute-start | bytes 417800 | tf_op jit(solution)/shard_map/ppermute | solution.py:360
  15.7 6.8 %collective-permute-start = (f32[30,8,128]{2,1,0:T(8,128)S(1)}, f32[30,8,128]{2,1,0:T(8,128)S(1)}, u32[]{:S(2)}, u32[]{:S(2)}) collective-permute-start(f32[30,8,128]{2,1,0:T(8,128)S(1)} %get-tuple-element.10), channel_id=1, source_target_pairs={{0,128},{128,256},{256,384},{384,512},{512,640},{640,768},{768,896... | collective-permute-start | bytes 368648 | tf_op jit(solution)/shard_map/ppermute | solution.py:359
  22.6 16.9 %collective-permute-start.3 = (f32[464,128]{1,0:T(8,128)S(1)}, f32[464,128]{1,0:T(8,128)S(1)}, u32[]{:S(2)}, u32[]{:S(2)}) collective-permute-start(f32[464,128]{1,0:T(8,128)S(1)} %get-tuple-element.13), channel_id=1, source_target_pairs={{8,0},{16,8},{24,16},{32,24},{40,32},{48,40},{56,48},{64,56},{72,6... | collective-permute-start | bytes 712712 | tf_op jit(solution)/shard_map/ppermute | solution.py:382
  23.9 15.6 %collective-permute-start.2 = (f32[408,128]{1,0:T(8,128)S(1)}, f32[408,128]{1,0:T(8,128)S(1)}, u32[]{:S(2)}, u32[]{:S(2)}) collective-permute-start(f32[408,128]{1,0:T(8,128)S(1)} %get-tuple-element.12), channel_id=1, source_target_pairs={{0,8},{8,16},{16,24},{24,32},{32,40},{40,48},{48,56},{56,64},{64,7... | collective-permute-start | bytes 626696 | tf_op jit(solution)/shard_map/ppermute | solution.py:381
  27.6 11.3 %all-to-all-start = ((f32[16,8,128]{2,1,0:T(8,128)}), f32[16,8,128]{2,1,0:T(8,128)S(1)}, u32[]{:S(2)}, u32[]{:S(2)}) async-start(f32[16,8,128]{2,1,0:T(8,128)} %tiles.1), calls=%async_computation | async-start | bytes 131072 | tf_op jit(solution)/shard_map/all_to_all | solution.py:370

commit v10 on v9

--- a/solution.py
+++ b/solution.py
@@ -202,10 +202,10 @@
         return jnp.where(lanes == 0, 0.0, pltpu.roll(v, 1, 1))
 
     def get(f, e, rows=YR):
-        return ext[pl.ds(pl.multiple_of(f * PLANE + e * YR, YR), rows), :]
+        return ext[pl.ds(f * PLANE + e * YR, rows), :]
 
     def put(f, e, v):
-        ext[pl.ds(pl.multiple_of(f * PLANE + e * YR, YR), v.shape[0]), :] = v
+        ext[pl.ds(f * PLANE + e * YR, v.shape[0]), :] = v
 
     for step in range(steps):
 
@@ -215,7 +215,7 @@
             ay = (sxy - get(6, e - 1)) + (y_up(syy) - syy) + (syz - z_down(syz))
             az = (sxz - get(7, e - 1)) + (syz - y_down(syz)) + (z_up(szz) - szz)
             scale = DT * get(9, e)
-            surface = force_ref[pl.ds(pl.multiple_of((e - 1) * YR, YR), YR), :]
+            surface = force_ref[pl.ds((e - 1) * YR, YR), :]
             for c, accel in enumerate((ax, ay, az)):
                 force = jnp.where(lanes == 0, pltpu.roll(surface, 127 - 3 * step - c, 1), 0.0)
                 change = scale * (accel + force)
@@ -244,17 +244,10 @@
                     put(3 + f, e, get(3 + f, e, rows) + DT * twice * rate)
                 rate_ref[6 * step + f, e] = rate[0:8]
 
-        def pair(body, first):
-            def run(i, carry):
-                e = first + 2 * i
-                body(e)
-                body(e + 1)
-                return carry
-
-            return run
-
-        lax.fori_loop(0, (XE - 2 * step) // 2, pair(velocity, 1 + step), 0)
-        lax.fori_loop(0, (XE - 2 * step - 2) // 2, pair(stress, 2 + step), 0)
+        for e in range(1 + step, 1 + XE - step):
+            velocity(e)
+        for e in range(2 + step, XE - step):
+            stress(e)
     copies = [
         pltpu.make_async_copy(
             ext.reshape(FIELDS, XS, YR, 128).at[f, pl.ds(1 + W, B), pl.ds(0, B)], state_ref.at[f], sem.at[f]

time: 67.2 us -> 65.5 us (0.975)
  Pallas kernels: 6.61 us -> 4.94 us
    pallas_call x1, Pallas kernels: 3.98 us -> 2.31 us  [on_device(): pl.pallas_call(functools.partial(steps_kernel, steps), out_shape=[f32(FIE...]
where the time goes in v10:
time: 65.5 us; the launch traced here: 65.1 us
  starting transfers between devices  23 us (35%)
  blocking collectives  22.6 us (35%)
  waiting for transfers between devices  12.5 us (19%)
  Pallas kernels  4.94 us (8%)
  between operations  1.38 us (2%)
    ppermute x1, starting transfers between devices, on_device(): high = lax.ppermute(low_face, 'sx', down_x)  13.3 us
    all_to_all x1, blocking collectives, on_device(): lax.all_to_all(kernels.reshape(3 * B, 8, 128), 'ev', split_axis=0, concat...  11.5 us
    all_to_all x1, blocking collectives, on_device(): lax.all_to_all(shared, 'ev', split_axis=0, concat_axis=0, tiled=True)  11.1 us
    all_to_all x1, waiting for transfers between devices, on_device(): tiles = lax.all_to_all(tiles, 'sy', split_axis=0, concat_axis=0, tiled=True)  7.65 us
    ppermute x1, waiting for transfers between devices, on_device(): low = lax.ppermute(high_face, 'sx', up_x)  4.85 us
    all_to_all x1, starting transfers between devices, on_device(): tiles = lax.all_to_all(tiles, 'sy', split_axis=0, concat_axis=0, tiled=True)  3.5 us
    ppermute x1, starting transfers between devices, on_device(): y_low = lax.ppermute(y_high_face, 'sy', up_y)  3.04 us
    pallas_call x1, Pallas kernels, on_device(): pl.pallas_call(functools.partial(steps_kernel, steps), out_shape=[f32(FIE...  2.31 us
  transfers between devices with their start and end apart: 5, of which 2 were waited for; matrix products, arithmetic and copies ran while one was open for 0% of the time, Pallas kernels for 2%

profile of v10, /device:TPU:128, one launch (start us, length us, event | category | flops | bytes accessed | tf_op | source)
XLA Modules:
  0.0 65.1 jit_solution(15086717063949725192)
XLA Ops:
  1.3 1.1 %x_faces.1 = (f32[34,8,128]{2,1,0:T(8,128)S(1)}, f32[30,8,128]{2,1,0:T(8,128)S(1)}, f32[12,8,8,128]{3,2,1,0:T(8,128)S(1)}) custom-call(f32[9,8,8,128]{3,2,1,0:T(8,128)} %bitcast.17, f32[8,8,128]{2,1,0:T(8,128)} %rho_hbm.1, f32[8,8,128]{2,1,0:T(8,128)} %lam_hbm.1, f32[8,8,128]{2,1,0:T(8,128)} %mu_hbm.1, s32[1,1]{1,0:T(1,128)S(6)} %copy.14.count_ref, ...), custom_call_target="tpu_custom_call" | custom-call | tf_op jit(solution)/shard_map/x_faces/pallas_call | solution.py:329
  2.4 13.3 %collective-permute-start.1 = (f32[34,8,128]{2,1,0:T(8,128)S(1)}, f32[34,8,128]{2,1,0:T(8,128)S(1)}, u32[]{:S(2)}, u32[]{:S(2)}) collective-permute-start(f32[34,8,128]{2,1,0:T(8,128)S(1)} %get-tuple-element.11.own_ref), channel_id=1, source_target_pairs={{128,0},{256,128},{384,256},{512,384},{640,512},{768,640},{896,768... | collective-permute-start | bytes 417800 | tf_op jit(solution)/shard_map/ppermute | solution.py:353
  15.7 1.9 %collective-permute-start = (f32[30,8,128]{2,1,0:T(8,128)S(1)}, f32[30,8,128]{2,1,0:T(8,128)S(1)}, u32[]{:S(2)}, u32[]{:S(2)}) collective-permute-start(f32[30,8,128]{2,1,0:T(8,128)S(1)} %get-tuple-element.10), channel_id=1, source_target_pairs={{0,128},{128,256},{256,384},{384,512},{512,640},{640,768},{768,896... | collective-permute-start | bytes 368648 | tf_op jit(solution)/shard_map/ppermute | solution.py:352
  17.6 4.8 %collective-permute-done.low_ref = f32[30,8,128]{2,1,0:T(8,128)S(1)} collective-permute-done((f32[30,8,128]{2,1,0:T(8,128)S(1)}, f32[30,8,128]{2,1,0:T(8,128)S(1)}, u32[]{:S(2)}, u32[]{:S(2)}) %collective-permute-start) | collective-permute-done | bytes 122912 | tf_op jit(solution)/shard_map/ppermute | solution.py:352
  22.4 0.0 collective-permute-done.1.high_ref
  22.4 0.1 y_faces.1
  22.6 1.3 %collective-permute-start.3 = (f32[464,128]{1,0:T(8,128)S(1)}, f32[464,128]{1,0:T(8,128)S(1)}, u32[]{:S(2)}, u32[]{:S(2)}) collective-permute-start(f32[464,128]{1,0:T(8,128)S(1)} %get-tuple-element.13), channel_id=1, source_target_pairs={{8,0},{16,8},{24,16},{32,24},{40,32},{48,40},{56,48},{64,56},{72,6... | collective-permute-start | bytes 712712 | tf_op jit(solution)/shard_map/ppermute | solution.py:375
  23.9 3.0 %collective-permute-start.2 = (f32[408,128]{1,0:T(8,128)S(1)}, f32[408,128]{1,0:T(8,128)S(1)}, u32[]{:S(2)}, u32[]{:S(2)}) collective-permute-start(f32[408,128]{1,0:T(8,128)S(1)} %get-tuple-element.12), channel_id=1, source_target_pairs={{0,8},{8,16},{16,24},{24,32},{32,40},{40,48},{48,56},{56,64},{64,7... | collective-permute-start | bytes 626696 | tf_op jit(solution)/shard_map/ppermute | solution.py:374
  26.9 0.7 %tiles.1 = f32[16,8,128]{2,1,0:T(8,128)} custom-call(f32[34,8,128]{2,1,0:T(8,128)S(1)} %get-tuple-element.11.own_ref, f32[30,8,128]{2,1,0:T(8,128)S(1)} %collective-permute-done.low_ref, f32[34,8,128]{2,1,0:T(8,128)S(1)} %collective-permute-done.1.high_ref), custom_call_target="tpu_custom_call" | custom-call | tf_op jit(solution)/shard_map/tiles/pallas_call | solution.py:355
  27.6 3.5 %all-to-all-start = ((f32[16,8,128]{2,1,0:T(8,128)}), f32[16,8,128]{2,1,0:T(8,128)S(1)}, u32[]{:S(2)}, u32[]{:S(2)}) async-start(f32[16,8,128]{2,1,0:T(8,128)} %tiles.1), calls=%async_computation | async-start | bytes 131072 | tf_op jit(solution)/shard_map/all_to_all | solution.py:363
  31.1 0.1 block.1._
  31.3 7.7 %all-to-all-done.tiles_ref = f32[16,8,128]{2,1,0:T(8,128)S(1)} async-done(((f32[16,8,128]{2,1,0:T(8,128)}), f32[16,8,128]{2,1,0:T(8,128)S(1)}, u32[]{:S(2)}, u32[]{:S(2)}) %all-to-all-start) | async-done | bytes 65568 | tf_op jit(solution)/shard_map/all_to_all | solution.py:363
  38.9 0.6 surface.1.force_ref
  39.5 0.0 collective-permute-done.2.y_low_ref
  39.5 0.0 collective-permute-done.3.y_high_ref
  39.5 2.3 %steps.1 = (f32[3072,128]{1,0:T(8,128)S(1)}, f32[9,8,8,128]{3,2,1,0:T(8,128)}, f32[3,8,8,128]{3,2,1,0:T(8,128)S(1)}) custom-call(f32[3072,128]{1,0:T(8,128)S(1)} %block.1._, bf16[3,9,8,8,128]{4,3,2,1,0:T(8,128)(2,1)} %bitcast.15, f32[408,128]{1,0:T(8,128)S(1)} %collective-permute-done.2.y_low_ref, ...), custom_call_target="tpu_custom_call", output_to_operand_aliasing={{0}: (0, {})} | custom-call | tf_op jit(solution)/shard_map/steps/pallas_call | solution.py:396
  41.8 11.5 %all_to_all.15.parts_ref = f32[24,8,128]{2,1,0:T(8,128)S(1)} all-to-all(f32[24,8,128]{2,1,0:T(8,128)S(1)} %bitcast.14), channel_id=1, replica_groups=mesh['sx'=8,'sy'=16,'ev'=8] {'ev'}, dimensions={0} | all-to-all | bytes 196608 | tf_op jit(solution)/shard_map/all_to_all | solution.py:413
  53.4 11.1 %all_to_all.16 = f32[24,8,128]{2,1,0:T(8,128)S(1)} all-to-all(f32[24,8,128]{2,1,0:T(8,128)S(1)} %event_sum.1), channel_id=1, replica_groups=mesh['sx'=8,'sy'=16,'ev'=8] {'ev'}, dimensions={0} | all-to-all | bytes 196608 | tf_op jit(solution)/shard_map/all_to_all | solution.py:418
  64.5 0.6 copy.15
  (1 shorter events, 0.0 us)
Async XLA Ops:
  2.4 20.1 %collective-permute-start.1 = (f32[34,8,128]{2,1,0:T(8,128)S(1)}, f32[34,8,128]{2,1,0:T(8,128)S(1)}, u32[]{:S(2)}, u32[]{:S(2)}) collective-permute-start(f32[34,8,128]{2,1,0:T(8,128)S(1)} %get-tuple-element.11.own_ref), channel_id=1, source_target_pairs={{128,0},{256,128},{384,256},{512,384},{640,512},{768,640},{896,768... | collective-permute-start | bytes 417800 | tf_op jit(solution)/shard_map/ppermute | solution.py:353
  15.7 6.8 %collective-permute-start = (f32[30,8,128]{2,1,0:T(8,128)S(1)}, f32[30,8,128]{2,1,0:T(8,128)S(1)}, u32[]{:S(2)}, u32[]{:S(2)}) collective-permute-start(f32[30,8,128]{2,1,0:T(8,128)S(1)} %get-tuple-element.10), channel_id=1, source_target_pairs={{0,128},{128,256},{256,384},{384,512},{512,640},{640,768},{768,896... | collective-permute-start | bytes 368648 | tf_op jit(solution)/shard_map/ppermute | solution.py:352
  22.6 16.9 %collective-permute-start.3 = (f32[464,128]{1,0:T(8,128)S(1)}, f32[464,128]{1,0:T(8,128)S(1)}, u32[]{:S(2)}, u32[]{:S(2)}) collective-permute-start(f32[464,128]{1,0:T(8,128)S(1)} %get-tuple-element.13), channel_id=1, source_target_pairs={{8,0},{16,8},{24,16},{32,24},{40,32},{48,40},{56,48},{64,56},{72,6... | collective-permute-start | bytes 712712 | tf_op jit(solution)/shard_map/ppermute | solution.py:375
  23.9 15.6 %collective-permute-start.2 = (f32[408,128]{1,0:T(8,128)S(1)}, f32[408,128]{1,0:T(8,128)S(1)}, u32[]{:S(2)}, u32[]{:S(2)}) collective-permute-start(f32[408,128]{1,0:T(8,128)S(1)} %get-tuple-element.12), channel_id=1, source_target_pairs={{0,8},{8,16},{16,24},{24,32},{32,40},{40,48},{48,56},{56,64},{64,7... | collective-permute-start | bytes 626696 | tf_op jit(solution)/shard_map/ppermute | solution.py:374
  27.6 11.3 %all-to-all-start = ((f32[16,8,128]{2,1,0:T(8,128)}), f32[16,8,128]{2,1,0:T(8,128)S(1)}, u32[]{:S(2)}, u32[]{:S(2)}) async-start(f32[16,8,128]{2,1,0:T(8,128)} %tiles.1), calls=%async_computation | async-start | bytes 131072 | tf_op jit(solution)/shard_map/all_to_all | solution.py:363
